TPU v7x, 32 devices: a whole 2x2x4 slice. The times are simulated.
32 devices in a mesh: comp: 2 (over y), tile: 4 (over x, core), lev: 4 (over z).
Axes of the slice: x: 2, y: 2, z: 4, core: 2. Of those that a mesh axis runs over, the one named last changes fastest.
Arguments:
- thermal_anomaly: float32 [2, 80, 2048], P('comp', 'lev', 'tile'), may hold values from -6 to 6
- right_face_transport_ratio: float32 [2, 80, 2048], P('comp', 'lev', 'tile'), may hold values from -0.45 to 0.45
- species_ratios: float32 [2, 40, 80, 2048], P('comp', None, 'lev', 'tile'), may hold values from 0.1 to 3
- lateral_spreading_number: float32 [2, 80, 2048], P('comp', 'lev', 'tile'), may hold values from 0.05 to 0.2
- depth_physics_operator: float32 [2, 80, 80], P('comp'), may hold values from -1 to 1, as said below
- exchange_weight_table: float32 [2048, 4], P('tile'), may hold values from 0.05 to 0.5
- sky_point_of_entry: int32 [2048, 4], P('tile'), may hold values from 0 to 2047, as said below
- water_indicator: int32 [2048], P('tile'), may hold values 0 or 1
Outputs:
- thermal_anomaly_ending: float32 [2, 80, 2048], P('comp', 'lev', 'tile')
- species_ratios_ending: float32 [2, 40, 80, 2048], P('comp', None, 'lev', 'tile')
Inputs may be any that keep to these rules, and one draw needn't show every extreme that they name: The ocean cells of each block of 512 (cells b * 512 to (b + 1) * 512 - 1) take their sources near the matching cells of one atmosphere block p(b), p a permutation of the blocks: sky_point_of_entry[j, k] lies cyclically within 128 cells of p(b) * 512 + (j mod 512). `depth_physics_operator`: each matrix has diagonal entries between 0.5 and 1.
All inputs are finite; a program needn't handle non-finite values. No bound on the sum of `water_indicator` on one device may be relied on, other than what follows from the above.
Results may differ from a plain program's by a relative error of at most 0.0003.
Values sent between devices are 32-bit elements; how exact they have to be, the bound alone decides.
No kernel may reach another device: no remote copies, remote signals or barrier semaphores. Data moves between devices by JAX's collectives and lax.ppermute only.
A program may use at most 64 MiB of HBM per device.

v0:
```python
import jax
import jax.numpy as jnp
from jax import lax
from jax.sharding import PartitionSpec as P

NFLUX = 4


def extended(x, sides, width):
    for axis, dim in sides:
        devices, length = (lax.axis_size(axis), x.shape[dim])
        up = [(i, (i + 1) % devices) for i in range(devices)]
        down = [(j, i) for i, j in up]
        last = lax.slice_in_dim(x, length - width, length, axis=dim)
        first = lax.slice_in_dim(x, 0, width, axis=dim)
        before = lax.ppermute(last, axis, up)
        after = lax.ppermute(first, axis, down)
        x = jnp.concatenate([before, x, after], axis=dim)
    return x


def passed_along(value, axis, steps):
    count = lax.axis_size(axis)
    first, last = (max(0, -steps), min(count, count - steps))
    return lax.ppermute(value, axis, [(source, source + steps) for source in range(first, last)])


def advance(padded, lateral_spreading_number):
    middle = padded[..., 1:-1]
    before = padded[..., :-2]
    after = padded[..., 2:]
    speed = middle[:, 1:2]
    speed_left = before[:, 1:2]
    flux_right = jnp.maximum(speed, 0.0) * middle + jnp.minimum(speed, 0.0) * after
    flux_left = jnp.maximum(speed_left, 0.0) * before + jnp.minimum(speed_left, 0.0) * middle
    tendency = -(flux_right - flux_left)
    thermal_energy = middle[:, 0]
    heat_next = thermal_energy + (
        tendency[:, 0]
        + lateral_spreading_number * (before[:, 0] - 2.0 * thermal_energy + after[:, 0])
    )
    tracer_next = middle[:, 2:] + tendency[:, 2:]
    return jnp.concatenate([heat_next[:, None], speed, tracer_next], axis=1)


def body(
    thermal_anomaly,
    right_face_transport_ratio,
    species_ratios,
    lateral_spreading_number,
    depth_physics_operator,
    exchange_weight_table,
    sky_point_of_entry,
    water_indicator,
):
    sections = lax.axis_size("comp")
    is_ocean = lax.axis_index("comp") >= sections // 2
    joined_quantities = jnp.concatenate(
        [thermal_anomaly[:, None], right_face_transport_ratio[:, None], species_ratios], axis=1
    )
    for substep in range(2):
        padded = extended(joined_quantities, (("tile", 3),), 1)
        advanced = advance(padded, lateral_spreading_number)
        if substep == 0:
            joined_quantities = advanced
        else:
            joined_quantities = jnp.where(is_ocean, joined_quantities, advanced)
    column = joined_quantities[0, 0]
    level_count = column.shape[0]
    offset = lax.axis_index("lev") * level_count
    matrix = depth_physics_operator[0]
    my_rows = lax.dynamic_slice_in_dim(matrix, offset, level_count, 0)
    blended_profiles = jnp.dot(
        my_rows,
        lax.all_gather(column, "lev", axis=0, tiled=True),
        precision=lax.Precision.HIGHEST,
        preferred_element_type=jnp.float32,
    )
    surface = jnp.concatenate(
        [blended_profiles[0:1], joined_quantities[0, 2 : 2 + NFLUX - 1, 0]], 0
    )
    whole = lax.all_gather(surface, "tile", axis=1, tiled=True)
    received = passed_along(whole, "comp", sections // 2)
    picked = received[:, sky_point_of_entry]
    remapped = jnp.sum(picked * exchange_weight_table, -1)
    updated = surface + 0.5 * (remapped - surface)
    at_sea = jnp.logical_and(
        jnp.logical_and(is_ocean, lax.axis_index("lev") == 0), water_indicator == 1
    )
    renewed_interface_values = jnp.where(at_sea[None, :], updated, surface)
    thermal_anomaly_ending = blended_profiles.at[0].set(renewed_interface_values[0])[None]
    species_ratios_ending = (
        joined_quantities[:, 2:].at[0, 0 : NFLUX - 1, 0].set(renewed_interface_values[1:])
    )
    return (thermal_anomaly_ending, species_ratios_ending)


def solution(mesh):
    in_specs = (
        P("comp", "lev", "tile"),
        P("comp", "lev", "tile"),
        P("comp", None, "lev", "tile"),
        P("comp", "lev", "tile"),
        P("comp", None, None),
        P("tile", None),
        P("tile", None),
        P("tile"),
    )
    out_specs = (P("comp", "lev", "tile"), P("comp", None, "lev", "tile"))
    return jax.shard_map(body, mesh=mesh, in_specs=in_specs, out_specs=out_specs, check_vma=False)
```

profile of v0, /device:TPU:0, one launch (start us, length us, event | category | flops | bytes accessed | tf_op | source)
XLA Modules:
  0.0 121.7 jit_solution(12595853146820664689)
XLA Ops:
  0.7 3.1 %copy.245 = f32[1,40,20,512]{3,0,2,1:T(1,128)S(1)} copy(f32[1,40,20,512]{3,1,2,0:T(8,128)} %param.14) | data formatting | bytes 3276800 | tf_op args[2]
  3.8 2.4 %fusion.8 = f32[1,42,20,512]{3,0,2,1:T(1,128)S(1)} fusion(f32[1,1,20,512]{3,0,2,1:T(1,128)S(1)} %bitcast.89, f32[1,40,20,512]{3,0,2,1:T(1,128)S(1)} %copy.245, f32[1,1,20,512]{3,0,2,1:T(1,128)S(1)} %bitcast.100), kind=kLoop, calls=%fused_computation.17 | loop fusion | flops 860160 | bytes 3440640 | tf_op jit(solution)/shard_map/concatenate | solution.py:58
  6.2 2.1 %fusion.40 = (f32[1,42,20,1]{3,0,2,1:T(1,128)}, f32[1,42,20,1]{3,0,2,1:T(1,128)}) fusion(f32[1,42,20,512]{3,0,2,1:T(1,128)S(1)} %fusion.8), kind=kLoop, calls=%fused_computation.80 | loop fusion | bytes 13440 | tf_op jit(solution)/shard_map/slice | solution.py:15
  8.3 2.4 %collective-permute-start = (f32[1,42,20,1]{3,0,2,1:T(1,128)}, f32[1,42,20,1]{3,0,2,1:T(1,128)S(1)}, u32[]{:S(2)}, u32[]{:S(2)}) collective-permute-start(f32[1,42,20,1]{3,0,2,1:T(1,128)} %get-tuple-element.56), channel_id=1, source_target_pairs={{4,0},{8,4},{12,8},{0,12},{5,1},{9,5},{13,9},{1,13},{6,2},{10,6},{... | collective-permute-start | bytes 10088 | tf_op jit(solution)/shard_map/ppermute | solution.py:17
  10.8 0.6 copy_bitcast_fusion
  11.8 9.5 %collective-permute-done = f32[1,42,20,1]{3,0,2,1:T(1,128)S(1)} collective-permute-done((f32[1,42,20,1]{3,0,2,1:T(1,128)}, f32[1,42,20,1]{3,0,2,1:T(1,128)S(1)}, u32[]{:S(2)}, u32[]{:S(2)}) %collective-permute-start) | collective-permute-done | bytes 3392 | tf_op jit(solution)/shard_map/ppermute | solution.py:17
  21.3 0.9 collective-permute-done.1
  22.3 12.0 %fusion.5 = (f32[1,42,20,513]{3,0,2,1:T(1,128)S(1)}, f32[1,42,20,513]{3,0,2,1:T(1,128)S(1)}) fusion(f32[1,1,20,512]{3,0,2,1:T(1,128)S(1)} %bitcast.90, f32[1,42,20,1]{3,0,2,1:T(1,128)S(1)} %collective-permute-done, f32[1,40,20,512]{3,0,2,1:T(1,128)S(1)} %copy.245, f32[1,1,20,512]{3,0,2,1:T(1,128)S(1)} %bitcast.101, ...), kind=kLoop, calls=%fused_computation.10 | loop fusion | flops 2585520 | bytes 5174400 | tf_op jit(solution)/shard_map/concatenate | solution.py:18
  34.4 4.9 %fusion.17 = f32[1,42,20,512]{3,0,2,1:T(1,128)S(1)} fusion(f32[1,42,20,513]{3,0,2,1:T(1,128)S(1)} %get-tuple-element.55, f32[1,42,20,513]{3,0,2,1:T(1,128)S(1)} %get-tuple-element.54, f32[20,512]{1,0:T(8,128)S(1)} %get-tuple-element.63, f32[20,512]{1,0:T(8,128)S(1)} %get-tuple-element.62, f32[20,512]{1,0:T(8,128)S(1)} %copy-done.5, ...), kind=kLoop, calls=%fused_computation.30 | loop fusion | flops 4300800 | bytes 7045120 | tf_op jit(solution)/shard_map/neg | solution.py:36
  39.3 2.2 %slice_add_fusion.1 = f32[1,40,20,512]{3,0,2,1:T(1,128)S(1)} fusion(f32[1,42,20,512]{3,0,2,1:T(1,128)S(1)} %fusion.17, f32[1,40,20,512]{3,1,2,0:T(8,128)S(1)} %copy-done.2), kind=kLoop, calls=%fused_computation.33 | loop fusion | flops 409600 | bytes 4915200 | tf_op jit(solution)/shard_map/add | solution.py:42
  41.8 2.4 %fusion.9 = f32[1,42,20,512]{3,0,2,1:T(1,128)S(1)} fusion(f32[1,1,20,512]{3,0,2,1:T(1,128)S(1)} %bitcast.92, f32[1,40,20,512]{3,0,2,1:T(1,128)S(1)} %slice_add_fusion.1, f32[1,1,20,512]{3,0,2,1:T(1,128)S(1)} %bitcast.97), kind=kLoop, calls=%fused_computation.18 | loop fusion | flops 860160 | bytes 3440640 | tf_op jit(solution)/shard_map/concatenate | solution.py:43
  44.2 2.1 %fusion.39 = (f32[1,42,20,1]{3,0,2,1:T(1,128)}, f32[1,42,20,1]{3,0,2,1:T(1,128)}) fusion(f32[1,42,20,512]{3,0,2,1:T(1,128)S(1)} %fusion.9), kind=kLoop, calls=%fused_computation.79 | loop fusion | bytes 13440 | tf_op jit(solution)/shard_map/slice | solution.py:15
  46.2 1.2 collective-permute-start.2
  47.4 10.3 %collective-permute-done.2 = f32[1,42,20,1]{3,0,2,1:T(1,128)} collective-permute-done((f32[1,42,20,1]{3,0,2,1:T(1,128)}, f32[1,42,20,1]{3,0,2,1:T(1,128)}, u32[]{:S(2)}, u32[]{:S(2)}) %collective-permute-start.2) | collective-permute-done | bytes 3392 | tf_op jit(solution)/shard_map/ppermute | solution.py:17
  57.7 1.0 collective-permute-done.3
  58.7 13.0 %fusion.7 = (f32[1,42,20,513]{3,0,2,1:T(1,128)S(1)}, f32[1,42,20,513]{3,0,2,1:T(1,128)S(1)}) fusion(f32[1,1,20,512]{3,0,2,1:T(1,128)S(1)} %bitcast.93, f32[1,42,20,1]{3,0,2,1:T(1,128)} %collective-permute-done.2, f32[1,40,20,512]{3,0,2,1:T(1,128)S(1)} %slice_add_fusion.1, f32[1,1,20,512]{3,0,2,1:T(1,128)S(1)} %bitcast.98, ...), kind=kLoop, calls=%fused_computation.12 | loop fusion | flops 2585520 | bytes 5174400 | tf_op jit(solution)/shard_map/concatenate | solution.py:18
  71.9 4.9 %fusion.18 = f32[1,42,20,512]{3,0,2,1:T(1,128)S(1)} fusion(f32[1,42,20,513]{3,0,2,1:T(1,128)S(1)} %get-tuple-element.51, f32[1,42,20,513]{3,0,2,1:T(1,128)S(1)} %get-tuple-element.50, f32[20,512]{1,0:T(8,128)S(1)} %get-tuple-element.59, f32[20,512]{1,0:T(8,128)S(1)} %get-tuple-element.58, f32[20,512]{1,0:T(8,128)S(1)} %copy-done.6, ...), kind=kLoop, calls=%fused_computation.31 | loop fusion | flops 4300800 | bytes 7045120 | tf_op jit(solution)/shard_map/neg | solution.py:36
  76.8 0.2 add_bitcast_fusion
  77.0 3.3 %slice_add_fusion = f32[1,40,20,512]{3,0,2,1:T(1,128)S(1)} fusion(f32[1,40,20,512]{3,0,2,1:T(1,128)S(1)} %slice_add_fusion.1, f32[1,42,20,512]{3,0,2,1:T(1,128)S(1)} %fusion.18), kind=kLoop, calls=%fused_computation.32 | loop fusion | flops 409600 | bytes 4915200 | tf_op jit(solution)/shard_map/add | solution.py:42
  80.3 2.4 %fusion.10 = f32[1,42,20,512]{3,0,2,1:T(1,128)S(1)} fusion(f32[1,1,20,512]{3,0,2,1:T(1,128)S(1)} %bitcast.95, f32[1,40,20,512]{3,0,2,1:T(1,128)S(1)} %slice_add_fusion, f32[1,1,20,512]{3,0,2,1:T(1,128)S(1)} %add_bitcast_fusion), kind=kLoop, calls=%fused_computation.19 | loop fusion | flops 860160 | bytes 3440640 | tf_op jit(solution)/shard_map/concatenate | solution.py:43
  82.7 1.0 copy_select_fusion
  83.8 1.2 %copy-done.1 = f32[1,42,20,512]{3,1,0,2:T(8,128)} copy-done((f32[1,42,20,512]{3,1,0,2:T(8,128)}, f32[1,42,20,512]{3,1,0,2:T(8,128)S(1)}, u32[]{:S(2)}) %copy-start.1) | copy-done | bytes 1720344
  85.0 13.7 %all-gather = f32[1,1,80,512]{3,1,0,2:T(1,128)S(1)} all-gather(f32[1,1,20,512]{3,1,0,2:T(1,128)S(1)} %slice.171), channel_id=2, replica_groups=mesh['comp'=2,'tile'=4,'lev'=4] {'lev'}, dimensions={2}, use_global_device_ids=true | all-gather | bytes 204800 | tf_op jit(solution)/shard_map/all_gather | solution.py:75
  98.8 0.2 fusion.19
  99.0 5.2 %all_gather.7 = f32[4,2048]{1,0:T(4,128)S(1)} all-gather(f32[4,512]{1,0:T(4,128)S(1)} %pad_maximum_fusion.7), channel_id=1, replica_groups=mesh['comp'=2,'tile'=4,'lev'=4] {'tile'}, dimensions={1}, use_global_device_ids=true | all-gather | bytes 40960 | tf_op jit(solution)/shard_map/all_gather | solution.py:82
  104.2 3.4 %collective-permute-start.4 = (f32[4,2048]{1,0:T(4,128)S(1)}, f32[4,2048]{1,0:T(4,128)S(1)}, u32[]{:S(2)}, u32[]{:S(2)}) collective-permute-start(f32[4,2048]{1,0:T(4,128)S(1)} %all_gather.7), channel_id=1, source_target_pairs={{0,16},{1,17},{2,18},{3,19},{4,20},{5,21},{6,22},{7,23},{8,24},{9,... | collective-permute-start | bytes 98312 | tf_op jit(solution)/shard_map/ppermute | solution.py:25
  107.8 3.0 %slice.175 = f32[1,40,20,512]{3,1,0,2:T(8,128)} slice(f32[1,42,20,512]{3,1,0,2:T(8,128)} %copy-done.1), slice={[0:1], [2:42], [0:20], [0:512]} | slice | bytes 3276800 | tf_op jit(solution)/shard_map/slice | solution.py:93
  110.8 0.4 copy.252
  111.2 5.5 %gather_fusion = f32[2048,4]{1,0:T(8,128)S(1)} fusion(f32[4,2048]{0,1:T(8,128)S(1)} %copy.252, s32[2048]{0:T(1024)S(1)} %broadcast_clamp_fusion), kind=kCustom, calls=%fused_computation | custom fusion | bytes 73728 | tf_op jit(solution)/shard_map/gather | solution.py:84
  116.7 2.8 %multiply_reduce_fusion = f32[512,4]{1,0:T(8,128)S(1)} fusion(f32[512,4,4]{2,1,0:T(4,128)S(1)} %bitcast.88, f32[512,4]{1,0:T(8,128)S(1)} %copy.253), kind=kLoop, calls=%fused_computation.34 | loop fusion | flops 14336 | bytes 49152 | tf_op jit(solution)/shard_map/reduce_sum | solution.py:85
  119.7 0.7 copy.256
  120.4 1.4 %scatter.9 = f32[1,40,20,512]{3,1,0,2:T(8,128)} dynamic-update-slice(f32[1,40,20,512]{3,1,0,2:T(8,128)} %slice.175, f32[1,3,1,512]{3,1,0,2:T(4,128)S(1)} %slice_bitcast_fusion.6, s32[]{:T(128)} %constant.77.clone.1, s32[]{:T(128)} %constant.77.clone.1, s32[]{:T(128)} %constant.77.clone.1, s32[]{:T(128)} %constant.77.clone.1) | dynamic-update-slice | bytes 12292 | tf_op jit(solution)/shard_map/scatter | solution.py:93
  (51 shorter events, 1.1 us)
Async XLA Ops:
  0.6 98.1 %copy-start = (f32[1,80,80]{2,1,0:T(8,128)S(1)}, f32[1,80,80]{2,1,0:T(8,128)}, u32[]{:S(2)}) copy-start(f32[1,80,80]{2,1,0:T(8,128)} %param.16) | copy-start | bytes 76804
  0.6 3.2 %copy-start.3 = (f32[1,20,512]{2,0,1:T(1,128)S(1)}, f32[1,20,512]{2,0,1:T(1,128)}, u32[]{:S(2)}) copy-start(f32[1,20,512]{2,0,1:T(1,128)} %param.13) | copy-start | bytes 122884
  0.7 3.2 %copy-start.4 = (f32[1,20,512]{2,0,1:T(1,128)S(1)}, f32[1,20,512]{2,0,1:T(1,128)}, u32[]{:S(2)}) copy-start(f32[1,20,512]{2,0,1:T(1,128)} %param.12) | copy-start | bytes 122884
  6.2 5.2 %copy-start.12 = (s32[512,4]{0,1:T(4,128)S(1)}, s32[512,4]{0,1:T(4,128)}, u32[]{:S(2)}) copy-start(s32[512,4]{0,1:T(4,128)} %param.18) | copy-start | bytes 24580
  8.3 13.0 %collective-permute-start = (f32[1,42,20,1]{3,0,2,1:T(1,128)}, f32[1,42,20,1]{3,0,2,1:T(1,128)S(1)}, u32[]{:S(2)}, u32[]{:S(2)}) collective-permute-start(f32[1,42,20,1]{3,0,2,1:T(1,128)} %get-tuple-element.56), channel_id=1, source_target_pairs={{4,0},{8,4},{12,8},{0,12},{5,1},{9,5},{13,9},{1,13},{6,2},{10,6},{... | collective-permute-start | bytes 10088 | tf_op jit(solution)/shard_map/ppermute | solution.py:17
  10.7 11.5 %collective-permute-start.1 = (f32[1,42,20,1]{3,0,2,1:T(1,128)}, f32[1,42,20,1]{3,0,2,1:T(1,128)S(1)}, u32[]{:S(2)}, u32[]{:S(2)}) collective-permute-start(f32[1,42,20,1]{3,0,2,1:T(1,128)} %get-tuple-element.57), channel_id=1, source_target_pairs={{0,4},{4,8},{8,12},{12,0},{1,5},{5,9},{9,13},{13,1},{2,6},{6,10},{... | collective-permute-start | bytes 10088 | tf_op jit(solution)/shard_map/ppermute | solution.py:16
  11.8 22.6 %copy-start.5 = (f32[20,512]{1,0:T(8,128)S(1)}, f32[20,512]{1,0:T(8,128)}, u32[]{:S(2)}) copy-start(f32[20,512]{1,0:T(8,128)} %get-tuple-element.64) | copy-start | bytes 122884
  11.8 22.6 %copy-start.7 = (f32[20,512]{1,0:T(8,128)S(1)}, f32[20,512]{1,0:T(8,128)}, u32[]{:S(2)}) copy-start(f32[20,512]{1,0:T(8,128)} %get-tuple-element.65) | copy-start | bytes 122884
  34.4 4.9 %copy-start.2 = (f32[1,40,20,512]{3,1,2,0:T(8,128)S(1)}, f32[1,40,20,512]{3,1,2,0:T(8,128)}, u32[]{:S(2)}) copy-start(f32[1,40,20,512]{3,1,2,0:T(8,128)} %param.14) | copy-start | bytes 4915204
  39.3 2.3 %copy-start.9 = (f32[1,20,512]{2,0,1:T(1,128)S(1)}, f32[1,20,512]{2,0,1:T(1,128)}, u32[]{:S(2)}) copy-start(f32[1,20,512]{2,0,1:T(1,128)} %param.15) | copy-start | bytes 122884
  46.2 11.5 %collective-permute-start.2 = (f32[1,42,20,1]{3,0,2,1:T(1,128)}, f32[1,42,20,1]{3,0,2,1:T(1,128)}, u32[]{:S(2)}, u32[]{:S(2)}) collective-permute-start(f32[1,42,20,1]{3,0,2,1:T(1,128)} %get-tuple-element.52), channel_id=1, source_target_pairs={{4,0},{8,4},{12,8},{0,12},{5,1},{9,5},{13,9},{1,13},{6,2},{10,6},{... | collective-permute-start | bytes 10088 | tf_op jit(solution)/shard_map/ppermute | solution.py:17
  47.4 11.3 %collective-permute-start.3 = (f32[1,42,20,1]{3,0,2,1:T(1,128)}, f32[1,42,20,1]{3,0,2,1:T(1,128)}, u32[]{:S(2)}, u32[]{:S(2)}) collective-permute-start(f32[1,42,20,1]{3,0,2,1:T(1,128)} %get-tuple-element.53), channel_id=1, source_target_pairs={{0,4},{4,8},{8,12},{12,0},{1,5},{5,9},{9,13},{13,1},{2,6},{6,10},{... | collective-permute-start | bytes 10088 | tf_op jit(solution)/shard_map/ppermute | solution.py:16
  47.4 24.4 %copy-start.6 = (f32[20,512]{1,0:T(8,128)S(1)}, f32[20,512]{1,0:T(8,128)}, u32[]{:S(2)}) copy-start(f32[20,512]{1,0:T(8,128)} %get-tuple-element.64) | copy-start | bytes 122884
  47.4 24.4 %copy-start.8 = (f32[20,512]{1,0:T(8,128)S(1)}, f32[20,512]{1,0:T(8,128)}, u32[]{:S(2)}) copy-start(f32[20,512]{1,0:T(8,128)} %get-tuple-element.65) | copy-start | bytes 122884
  71.8 4.9 %copy-start.10 = (f32[1,20,512]{2,0,1:T(1,128)S(1)}, f32[1,20,512]{2,0,1:T(1,128)}, u32[]{:S(2)}) copy-start(f32[1,20,512]{2,0,1:T(1,128)} %param.15) | copy-start | bytes 122884
  82.7 24.9 %copy-start.13 = (s32[512]{0:T(512)S(1)}, s32[512]{0:T(512)}, u32[]{:S(2)}) copy-start(s32[512]{0:T(512)} %param.19) | copy-start | bytes 6148
  82.7 24.9 %copy-start.11 = (f32[512,4]{0,1:T(4,128)S(1)}, f32[512,4]{0,1:T(4,128)}, u32[]{:S(2)}) copy-start(f32[512,4]{0,1:T(4,128)} %param.17) | copy-start | bytes 24580
  83.7 1.3 %copy-start.1 = (f32[1,42,20,512]{3,1,0,2:T(8,128)}, f32[1,42,20,512]{3,1,0,2:T(8,128)S(1)}, u32[]{:S(2)}) copy-start(f32[1,42,20,512]{3,1,0,2:T(8,128)S(1)} %copy_select_fusion) | copy-start | bytes 5160964
  104.2 6.6 %collective-permute-start.4 = (f32[4,2048]{1,0:T(4,128)S(1)}, f32[4,2048]{1,0:T(4,128)S(1)}, u32[]{:S(2)}, u32[]{:S(2)}) collective-permute-start(f32[4,2048]{1,0:T(4,128)S(1)} %all_gather.7), channel_id=1, source_target_pairs={{0,16},{1,17},{2,18},{3,19},{4,20},{5,21},{6,22},{7,23},{8,24},{9,... | collective-permute-start | bytes 98312 | tf_op jit(solution)/shard_map/ppermute | solution.py:25
where the time goes:
time: 122 us
  other arithmetic  52 us (43%)
  waiting for transfers between devices  21.8 us (18%)
  local copies, waits for them, and re-layouts  20.8 us (17%)
  blocking collectives  18.9 us (15%)
  starting transfers between devices  6.99 us (6%)
    concatenate x2, other arithmetic, extended(): x = jnp.concatenate([before, x, after], axis=dim)  25.1 us
    ppermute x2, waiting for transfers between devices, extended(): after = lax.ppermute(first, axis, down)  19.8 us
    all_gather x1, blocking collectives, body(): lax.all_gather(column, 'lev', axis=0, tiled=True)  13.7 us
    neg x2, other arithmetic, advance(): tendency = -(flux_right - flux_left)  9.84 us
    unnamed x32, local copies, waits for them, and re-layouts  5.92 us
    add x2, other arithmetic, advance(): tracer_next = middle[:, 2:] + tendency[:, 2:]  5.57 us
    gather x1, local copies, waits for them, and re-layouts, body(): picked = received[:, sky_point_of_entry]  5.48 us
    all_gather x1, blocking collectives, body(): whole = lax.all_gather(surface, 'tile', axis=1, tiled=True)  5.19 us
  transfers between devices with their start and end apart: 5, of which 4 were waited for; matrix products, arithmetic and copies ran while one was open for 3% of the time, Pallas kernels for 0%

commit v1 on v0

v1 whole, which is shorter than its diff:
```python
import functools

import jax
import jax.numpy as jnp
from jax import lax
from jax.experimental import pallas as pl
from jax.experimental.pallas import tpu as pltpu
from jax.sharding import PartitionSpec as P

NFLUX = 4
LANES = 128
SUB = 8
REACH = 128

VMEM = pl.BlockSpec(memory_space=pltpu.VMEM)
SMEM = pl.BlockSpec(memory_space=pltpu.SMEM)
ANY = pl.BlockSpec(memory_space=pl.ANY)


def padded_rows(n):
    return -(-n // SUB) * SUB


def peer(i, s, n):
    return i ^ s if n & (n - 1) == 0 else (i + s) % n


def slot_of(me, other, n):
    return me ^ other if n & (n - 1) == 0 else lax.rem(me - other + n, n)


def source_of(me, s, n):
    return me ^ s if n & (n - 1) == 0 else lax.rem(me - s + n, n)


def lane_iota(shape):
    return lax.broadcasted_iota(jnp.int32, shape, len(shape) - 1)


def wide(ref, levels, tiles):
    return jnp.concatenate([ref[pl.ds(t, levels, stride=tiles), :] for t in range(tiles)], axis=1)


def from_left(x, k, halo, place):
    moved = pltpu.roll(x, k, 1)
    edge = pltpu.roll(halo, lax.rem(k - place - 2 + 4 * LANES, LANES), 1)
    head = jnp.where(lane_iota(edge.shape) < k, edge, moved[:, :LANES])
    return jnp.concatenate([head, moved[:, LANES:]], axis=1)


def from_right(x, k, halo, place):
    width = x.shape[1]
    moved = pltpu.roll(x, width - k, 1)
    edge = pltpu.roll(halo, lax.rem(LANES - k - place + 4 * LANES, LANES), 1)
    tail = jnp.where(lane_iota(edge.shape) >= LANES - k, edge, moved[:, width - LANES :])
    return jnp.concatenate([moved[:, : width - LANES], tail], axis=1)


def pack_kernel(levels, tiles, tracers, t_ref, u_ref, n_ref, q_ref, a_ref, b_ref, left, right, sems):
    width = tiles * LANES
    copies = [
        pltpu.make_async_copy(q_ref.at[:, :, pl.ds(0, LANES)], left, sems.at[0]),
        pltpu.make_async_copy(q_ref.at[:, :, pl.ds(width - LANES, LANES)], right, sems.at[1]),
    ]
    for copy in copies:
        copy.start()
    even = lax.rem(lax.axis_index("tile"), 2) == 0
    lane = lane_iota((levels, LANES))

    def small(row, shifts, low):
        t, u, n = [r[pl.ds(row, levels, stride=tiles), :] for r in (t_ref, u_ref, n_ref)]
        u = pltpu.roll(u, shifts[0], 1)
        n = pltpu.roll(n, shifts[1], 1)
        if low:
            return jnp.where(lane < 2, t, jnp.where(lane < 4, u, n))
        return jnp.where(lane >= LANES - 2, t, jnp.where(lane >= LANES - 4, u, n))

    small_left = small(0, (2, 4), True)
    small_right = small(tiles - 1, (LANES - 2, LANES - 4), False)
    a_ref[pl.ds(tracers, levels), :] = jnp.where(even, small_right, small_left)
    b_ref[pl.ds(tracers, levels), :] = jnp.where(even, small_left, small_right)
    for copy in copies:
        copy.wait()
    pair = lane_iota((tracers, LANES)) // 2
    packed_left = left[0]
    packed_right = pltpu.roll(right[0], 2, 1)
    for level in range(1, levels):
        here = pair == level
        packed_left = jnp.where(here, pltpu.roll(left[level], 2 * level, 1), packed_left)
        packed_right = jnp.where(here, pltpu.roll(right[level], 2 * level + 2, 1), packed_right)
    a_ref[pl.ds(0, tracers), :] = jnp.where(even, packed_right, packed_left)
    b_ref[pl.ds(0, tracers), :] = jnp.where(even, packed_left, packed_right)


def heat_kernel(levels, tiles, tracers, sections, t_ref, u_ref, n_ref, a_ref, b_ref, heat_ref, coef_ref):
    even = lax.rem(lax.axis_index("tile"), 2) == 0
    ocean = lax.axis_index("comp") >= sections // 2
    t, u, n = [wide(r, levels, tiles) for r in (t_ref, u_ref, n_ref)]
    got_a = a_ref[pl.ds(tracers, levels), :]
    got_b = b_ref[pl.ds(tracers, levels), :]
    low = jnp.where(even, got_b, got_a)
    high = jnp.where(even, got_a, got_b)
    ul1, ul2 = [from_left(u, k, low, LANES - 4) for k in (1, 2)]
    ur1 = from_right(u, 1, high, 2)
    plus = lambda v: jnp.maximum(v, 0.0)
    minus = lambda v: jnp.minimum(v, 0.0)
    a0, b0, c0 = 1.0 - plus(u) + minus(ul1), plus(ul1), -minus(u)
    am, bm, cm = 1.0 - plus(ul1) + minus(ul2), plus(ul2), -minus(ul1)
    ap, bp, cp = 1.0 - plus(ur1) + minus(u), plus(u), -minus(ur1)

    def composed(a0, b0, c0, am, bm, cm, ap, bp, cp):
        return (
            jnp.where(ocean, a0, a0 * a0 + b0 * cm + c0 * bp),
            jnp.where(ocean, b0, b0 * (a0 + am)),
            jnp.where(ocean, c0, c0 * (a0 + ap)),
            jnp.where(ocean, 0.0, b0 * bm),
            jnp.where(ocean, 0.0, c0 * cp),
        )

    for k, value in enumerate(composed(a0, b0, c0, am, bm, cm, ap, bp, cp)):
        coef_ref[k] = value
    nl = from_left(n, 1, low, LANES - 6)
    nr = from_right(n, 1, high, 4)
    e0, e1, e2, e3, e4 = composed(
        a0 - 2.0 * n, b0 + n, c0 + n, am - 2.0 * nl, bm + nl, cm + nl, ap - 2.0 * nr, bp + nr, cp + nr
    )
    tl1, tl2 = [from_left(t, k, low, LANES - 2) for k in (1, 2)]
    tr1, tr2 = [from_right(t, k, high, 0) for k in (1, 2)]
    heat = e0 * t + e1 * tl1 + e2 * tr1 + e3 * tl2 + e4 * tr2
    for tile in range(tiles):
        heat_ref[pl.ds(tile, levels, stride=tiles), :] = heat[:, tile * LANES : (tile + 1) * LANES]


def tracer_kernel(block, tracers, q_ref, coef_ref, a_ref, b_ref, out_ref, top_ref):
    even = lax.rem(lax.axis_index("tile"), 2) == 0
    got_a = a_ref[pl.ds(0, tracers), :]
    got_b = b_ref[pl.ds(0, tracers), :]
    low = jnp.where(even, got_b, got_a)
    high = jnp.where(even, got_a, got_b)
    for i in range(block):
        level = pl.program_id(0) * block + i
        q = q_ref[i]
        place = 2 * level
        e0, e1, e2, e3, e4 = [coef_ref[k, pl.ds(level, 1), :] for k in range(5)]
        new = (
            e0 * q
            + e1 * from_left(q, 1, low, place)
            + e2 * from_right(q, 1, high, place)
            + e3 * from_left(q, 2, low, place)
            + e4 * from_right(q, 2, high, place)
        )
        out_ref[i] = new
        if i == 0:

            @pl.when(pl.program_id(0) == 0)
            def _():
                top_ref[...] = new[:SUB]


def surface_kernel(levels, tiles, count, m_ref, own_ref, *refs):
    got, (top_ref, mixed_ref, send_ref, whole) = refs[: count - 1], refs[count - 1 :]
    for s, ref in enumerate((own_ref,) + tuple(got)):
        whole[pl.ds(s * levels, levels), :] = wide(ref, levels, tiles)
    mixed = jnp.dot(
        m_ref[...], whole[...], precision=lax.Precision.HIGHEST, preferred_element_type=jnp.float32
    )
    mixed_ref[...] = mixed
    fields = jnp.where(
        lax.broadcasted_iota(jnp.int32, (SUB, tiles * LANES), 0) == 0,
        jnp.broadcast_to(mixed[0:1], (SUB, tiles * LANES)),
        pltpu.roll(top_ref[...], 1, 0),
    )
    for tile in range(tiles):
        send_ref[pl.ds(tile * SUB, SUB), :] = fields[:, tile * LANES : (tile + 1) * LANES]


def final_kernel(
    levels, tiles, count, sections, first_ref, mixed_ref, top_ref, index_ref, weight_ref, water_ref, *refs
):
    got, (q_ref, heat_ref, out_ref, whole, patch, sem) = refs[:count], refs[count:]
    del q_ref
    width = tiles * LANES
    cells = count * width
    here = lax.axis_index("tile")
    sea = jnp.logical_and(
        lax.axis_index("comp") >= sections // 2, lax.axis_index("lev") == 0
    )
    rows = tiles * SUB
    for s in range(count):
        whole[pl.ds(pl.multiple_of(source_of(here, s, count) * rows, rows), rows), :] = got[s][...]
    first = first_ref[0]
    top = top_ref[...]
    mixed = mixed_ref[...]
    first_row = lax.broadcasted_iota(jnp.int32, (SUB, LANES), 0) == 0
    lane = lane_iota((SUB, LANES))
    for tile in range(tiles):
        cut = slice(tile * LANES, (tile + 1) * LANES)
        windows = []
        for q in range(3):
            block = lax.rem(first + tile + q - 1 + count * tiles, count * tiles)
            windows.append(whole[pl.ds(pl.multiple_of(block * SUB, SUB), SUB), :])
        total = jnp.zeros((SUB, LANES), jnp.float32)
        start = first * LANES + tile * LANES - REACH
        for k in range(index_ref.shape[0]):
            index = jnp.broadcast_to(index_ref[k : k + 1, cut], (SUB, LANES))
            weight = jnp.broadcast_to(weight_ref[k : k + 1, cut], (SUB, LANES))
            at = index - start - lane
            at = jnp.where(at < 0, at + cells, at)
            at = jnp.where(at >= cells, at - cells, at) + lane
            inner = jnp.bitwise_and(at, LANES - 1)
            outer = jnp.right_shift(at, 7)
            picks = [jnp.take_along_axis(w, inner, axis=1) for w in windows]
            picked = jnp.where(outer == 0, picks[0], jnp.where(outer == 1, picks[1], picks[2]))
            total = total + picked * weight
        own_heat = jnp.broadcast_to(mixed[0:1, cut], (SUB, LANES))
        surface = jnp.where(first_row, own_heat, pltpu.roll(top[:, cut], 1, 0))
        wet = jnp.logical_and(sea, jnp.broadcast_to(water_ref[0:1, cut], (SUB, LANES)) == 1)
        wet = jnp.logical_and(wet, lax.broadcasted_iota(jnp.int32, (SUB, LANES), 0) < NFLUX)
        renewed = jnp.where(wet, surface + 0.5 * (total - surface), surface)
        heat_ref[pl.ds(tile, levels, stride=tiles), :] = mixed[:, cut]
        heat_ref[pl.ds(tile, 1), :] = renewed[0:1]
        patch[:, cut] = jnp.where(
            lax.broadcasted_iota(jnp.int32, (SUB, LANES), 0) < NFLUX - 1,
            pltpu.roll(renewed, SUB - 1, 0),
            top[:, cut],
        )
    copy = pltpu.make_async_copy(patch, out_ref.at[0, pl.ds(0, SUB), :], sem)
    copy.start()
    copy.wait()


def body(
    sizes,
    thermal_anomaly,
    right_face_transport_ratio,
    species_ratios,
    lateral_spreading_number,
    depth_physics_operator,
    exchange_weight_table,
    sky_point_of_entry,
    water_indicator,
):
    sections, tile_count, lev_count = sizes
    _, levels, width = thermal_anomaly.shape
    tracers = species_ratios.shape[1]
    tiles = width // LANES
    rows = levels * tiles
    f32 = jnp.float32
    shape = jax.ShapeDtypeStruct
    flat = lambda x: x.reshape(rows, LANES)
    t, u, n = flat(thermal_anomaly), flat(right_face_transport_ratio), flat(lateral_spreading_number)
    q = jnp.transpose(species_ratios, (0, 2, 1, 3)).reshape(levels, tracers, width)
    lev = lax.axis_index("lev")

    pack_rows = tracers + padded_rows(levels)
    send_a, send_b = pl.pallas_call(
        functools.partial(pack_kernel, levels, tiles, tracers),
        out_shape=[shape((pack_rows, LANES), f32)] * 2,
        in_specs=[VMEM, VMEM, VMEM, ANY],
        out_specs=[VMEM, VMEM],
        scratch_shapes=[pltpu.VMEM((levels, tracers, LANES), f32)] * 2 + [pltpu.SemaphoreType.DMA((2,))],
        name="pack",
    )(t, u, n, q)
    swap_a = [(i, i ^ 1) for i in range(tile_count)]
    swap_b = [(i, (i + 1) % tile_count if i % 2 else (i - 1) % tile_count) for i in range(tile_count)]
    got_a = lax.ppermute(send_a, "tile", swap_a)
    got_b = lax.ppermute(send_b, "tile", swap_b)

    heat, coef = pl.pallas_call(
        functools.partial(heat_kernel, levels, tiles, tracers, sections),
        out_shape=[shape((rows, LANES), f32), shape((5, levels, width), f32)],
        in_specs=[VMEM] * 5,
        out_specs=[VMEM, VMEM],
        name="heat",
    )(t, u, n, got_a, got_b)

    others = [
        lax.ppermute(heat, "lev", [(i, peer(i, s, lev_count)) for i in range(lev_count)])
        for s in range(1, lev_count)
    ]

    block = 5 if levels % 5 == 0 else 1
    whole = lambda *dims: pl.BlockSpec(dims, lambda i: (0,) * len(dims))
    moved, top = pl.pallas_call(
        functools.partial(tracer_kernel, block, tracers),
        out_shape=[shape((levels, tracers, width), f32), shape((SUB, width), f32)],
        grid=(levels // block,),
        in_specs=[
            pl.BlockSpec((block, tracers, width), lambda i: (i, 0, 0)),
            whole(5, levels, width),
            whole(pack_rows, LANES),
            whole(pack_rows, LANES),
        ],
        out_specs=[pl.BlockSpec((block, tracers, width), lambda i: (i, 0, 0)), whole(SUB, width)],
        cost_estimate=pl.CostEstimate(
            flops=9 * levels * tracers * width, bytes_accessed=8 * levels * tracers * width, transcendentals=0
        ),
        name="tracers",
    )(q, coef, got_a, got_b)

    mine = lax.dynamic_slice_in_dim(depth_physics_operator[0], lev * levels, levels, 0)
    columns = [
        lax.dynamic_slice_in_dim(mine, source_of(lev, s, lev_count) * levels, levels, 1)
        for s in range(lev_count)
    ]
    matrix = jnp.concatenate(columns, axis=1)
    mixed, surface = pl.pallas_call(
        functools.partial(surface_kernel, levels, tiles, lev_count),
        out_shape=[shape((levels, width), f32), shape((tiles * SUB, LANES), f32)],
        in_specs=[VMEM] * (lev_count + 2),
        out_specs=[VMEM, VMEM],
        scratch_shapes=[pltpu.VMEM((levels * lev_count, width), f32)],
        name="surface",
    )(matrix, heat, *others, top)

    half = sections // 2
    place = lambda c, i, l: (c * tile_count + i) * lev_count + l
    got = [
        lax.ppermute(
            surface,
            ("comp", "tile", "lev"),
            [
                (place(c, i, l), place((c + half) % sections, peer(i, s, tile_count), l))
                for c in range(sections)
                for i in range(tile_count)
                for l in range(lev_count)
            ],
        )
        for s in range(tile_count)
    ]

    index = sky_point_of_entry.T
    cells = tile_count * width
    first = ((index[0, 0:1] + REACH) % cells) // width * tiles
    heat_out, q_out = pl.pallas_call(
        functools.partial(final_kernel, levels, tiles, tile_count, sections),
        out_shape=[shape((rows, LANES), f32), shape((levels, tracers, width), f32)],
        in_specs=[SMEM] + [VMEM] * (5 + tile_count) + [ANY],
        out_specs=[VMEM, ANY],
        scratch_shapes=[
            pltpu.VMEM((tile_count * tiles * SUB, LANES), f32),
            pltpu.VMEM((SUB, width), f32),
            pltpu.SemaphoreType.DMA,
        ],
        input_output_aliases={6 + tile_count: 1},
        name="remap",
    )(
        first, mixed, top, index, exchange_weight_table.T, water_indicator.reshape(1, width), *got, moved
    )
    thermal_anomaly_ending = heat_out.reshape(1, levels, width)
    species_ratios_ending = jnp.transpose(q_out.reshape(1, levels, tracers, width), (0, 2, 1, 3))
    return thermal_anomaly_ending, species_ratios_ending


def solution(mesh):
    in_specs = (
        P("comp", "lev", "tile"),
        P("comp", "lev", "tile"),
        P("comp", None, "lev", "tile"),
        P("comp", "lev", "tile"),
        P("comp", None, None),
        P("tile", None),
        P("tile", None),
        P("tile"),
    )
    out_specs = (P("comp", "lev", "tile"), P("comp", None, "lev", "tile"))
    sizes = (mesh.shape["comp"], mesh.shape["tile"], mesh.shape["lev"])
    return jax.shard_map(
        functools.partial(body, sizes), mesh=mesh, in_specs=in_specs, out_specs=out_specs, check_vma=False
    )
```

time: 122 us -> 34.7 us (0.28)
  other arithmetic: 52 us -> 0.68 us
  blocking collectives: 18.9 us -> 0 us
  waiting for transfers between devices: 21.8 us -> 3.47 us
  local copies, waits for them, and re-layouts: 20.8 us -> 3.09 us
  Pallas kernels: 0 us -> 13.7 us
  starting transfers between devices: 6.99 us -> 11.9 us
    concatenate x7 -> x1, other arithmetic: 32.5 us -> 0.68 us  [body(): matrix = jnp.concatenate(columns, axis=1)]
    all_gather x2 -> x0, blocking collectives: 18.9 us -> none  [the longest x1 13.7 us: body(): lax.all_gather(column, 'lev', axis=0, tiled=True)]
    ppermute x5 -> x9, waiting for transfers between devices: 21.8 us -> 3.47 us  [the longest x1 1.81 us: body(): got_b = lax.ppermute(send_b, 'tile', swap_b)]
    pallas_call x0 -> x5, Pallas kernels: none -> 13.7 us  [the longest x1 5.07 us: body(): pl.pallas_call(functools.partial(tracer_kernel, block, tracers), out_shap...]
    neg x2 -> x0, other arithmetic: 9.84 us -> none  [advance(): tendency = -(flux_right - flux_left)]
    slice x7 -> x1, local copies, waits for them, and re-layouts: 7.2 us -> 1.19 us  [body(): first = (index[0, 0:1] + REACH) % cells // width * tiles]
    add x3 -> x0, other arithmetic: 5.74 us -> none  [the longest x2 5.57 us: advance(): tracer_next = middle[:, 2:] + tendency[:, 2:]]
    gather x1 -> x0, local copies, waits for them, and re-layouts: 5.48 us -> none  [body(): picked = received[:, sky_point_of_entry]]
  transfers between devices with their start and end apart: 5 -> 9, of which waited for: 4 -> 3; matrix products, arithmetic and copies ran while one was open for 3% -> 6% of each run, Pallas kernels for 0% -> 15%
where the time goes in v1:
time: 34.7 us; the launch traced here: 34.2 us
  Pallas kernels  13.7 us (39%)
  starting transfers between devices  11.9 us (34%)
  waiting for transfers between devices  3.47 us (10%)
  local copies, waits for them, and re-layouts  3.09 us (9%)
  between operations  1.42 us (4%)
  other arithmetic  0.68 us (2%)
    pallas_call x1, Pallas kernels, body(): pl.pallas_call(functools.partial(tracer_kernel, block, tracers), out_shap...  5.07 us
    ppermute x4, starting transfers between devices, body(): lax.ppermute(surface, ('comp', 'tile', 'lev'), [(place(c, i, l), place((c...  4.39 us
    ppermute x3, starting transfers between devices, body(): lax.ppermute(heat, 'lev', [(i, peer(i, s, lev_count)) for i in range(lev_...  4.39 us
    pallas_call x1, Pallas kernels, body(): pl.pallas_call(functools.partial(pack_kernel, levels, tiles, tracers), ou...  2.89 us
    ppermute x1, starting transfers between devices, body(): got_b = lax.ppermute(send_b, 'tile', swap_b)  2.59 us
    pallas_call x1, Pallas kernels, body(): pl.pallas_call(functools.partial(final_kernel, levels, tiles, tile_count,...  2.3 us
    unnamed x20, local copies, waits for them, and re-layouts  1.82 us
    ppermute x1, waiting for transfers between devices, body(): got_b = lax.ppermute(send_b, 'tile', swap_b)  1.81 us
  transfers between devices with their start and end apart: 9, of which 3 were waited for; matrix products, arithmetic and copies ran while one was open for 6% of the time, Pallas kernels for 15%

profile of v1, /device:TPU:0, one launch (start us, length us, event | category | flops | bytes accessed | tf_op | source)
XLA Modules:
  0.0 34.2 jit_solution(6704631681608938186)
XLA Ops:
  0.6 2.9 %pack.1 = (f32[64,128]{1,0:T(8,128)}, f32[64,128]{1,0:T(8,128)}) custom-call(f32[80,128]{1,0:T(8,128)} %bitcast.25, f32[80,128]{1,0:T(8,128)} %bitcast.27, f32[80,128]{1,0:T(8,128)} %bitcast.29, f32[20,40,512]{2,1,0:T(8,128)} %bitcast.22), custom_call_target="tpu_custom_call" | custom-call | tf_op jit(solution)/shard_map/pack/pallas_call | solution.py:256
  3.5 0.6 %collective-permute-start = (f32[64,128]{1,0:T(8,128)}, f32[64,128]{1,0:T(8,128)S(1)}, u32[]{:S(2)}, u32[]{:S(2)}) collective-permute-start(f32[64,128]{1,0:T(8,128)} %get-tuple-element.12), channel_id=1, source_target_pairs={{0,4},{4,0},{8,12},{12,8},{1,5},{5,1},{9,13},{13,9},{2,6},{6,2},{1... | collective-permute-start | bytes 98312 | tf_op jit(solution)/shard_map/ppermute | solution.py:266
  4.1 2.6 %collective-permute-start.1 = (f32[64,128]{1,0:T(8,128)}, f32[64,128]{1,0:T(8,128)S(1)}, u32[]{:S(2)}, u32[]{:S(2)}) collective-permute-start(f32[64,128]{1,0:T(8,128)} %get-tuple-element.13), channel_id=1, source_target_pairs={{0,12},{4,8},{8,4},{12,0},{1,13},{5,9},{9,5},{13,1},{2,14},{6,10},... | collective-permute-start | bytes 98312 | tf_op jit(solution)/shard_map/ppermute | solution.py:267
  6.7 0.1 dynamic-slice_bitcast_fusion.3
  6.8 0.0 collective-permute-done.a_ref
  6.8 1.8 %collective-permute-done.1.b_ref = f32[64,128]{1,0:T(8,128)S(1)} collective-permute-done((f32[64,128]{1,0:T(8,128)}, f32[64,128]{1,0:T(8,128)S(1)}, u32[]{:S(2)}, u32[]{:S(2)}) %collective-permute-start.1) | collective-permute-done | bytes 32800 | tf_op jit(solution)/shard_map/ppermute | solution.py:267
  8.6 0.0 copy-done
  8.6 0.6 %copy-done.1 = f32[64,128]{1,0:T(8,128)} copy-done((f32[64,128]{1,0:T(8,128)}, f32[64,128]{1,0:T(8,128)S(1)}, u32[]{:S(2)}) %copy-start.1) | copy-done | bytes 32792
  9.2 1.7 %heat.1 = (f32[80,128]{1,0:T(8,128)}, f32[5,20,512]{2,1,0:T(8,128)}) custom-call(f32[80,128]{1,0:T(8,128)} %bitcast.26, f32[80,128]{1,0:T(8,128)} %bitcast.28, f32[80,128]{1,0:T(8,128)} %bitcast.30, f32[64,128]{1,0:T(8,128)} %copy-done, f32[64,128]{1,0:T(8,128)} %copy-done.1), custom_call_target="tpu_custom_call" | custom-call | tf_op jit(solution)/shard_map/heat/pallas_call | solution.py:269
  10.9 3.7 %collective-permute-start.4 = (f32[80,128]{1,0:T(8,128)}, f32[80,128]{1,0:T(8,128)S(1)}, u32[]{:S(2)}, u32[]{:S(2)}) collective-permute-start(f32[80,128]{1,0:T(8,128)} %get-tuple-element.14.own_ref), channel_id=1, source_target_pairs={{0,3},{1,2},{2,1},{3,0},{4,7},{5,6},{6,5},{7,4},{8,11},{9,10},{10,... | collective-permute-start | bytes 122888 | tf_op jit(solution)/shard_map/ppermute | solution.py:278
  14.6 0.0 collective-permute-start.3
  14.6 0.7 %collective-permute-start.2 = (f32[80,128]{1,0:T(8,128)}, f32[80,128]{1,0:T(8,128)S(1)}, u32[]{:S(2)}, u32[]{:S(2)}) collective-permute-start(f32[80,128]{1,0:T(8,128)} %get-tuple-element.14.own_ref), channel_id=1, source_target_pairs={{0,1},{1,0},{2,3},{3,2},{4,5},{5,4},{6,7},{7,6},{8,9},{9,8},{10,11... | collective-permute-start | bytes 122888 | tf_op jit(solution)/shard_map/ppermute | solution.py:278
  15.3 0.7 %pad_maximum_fusion.m_ref = f32[20,80]{1,0:T(8,128)} fusion(f32[20,20]{1,0:T(8,128)S(1)} %get-tuple-element.28, f32[20,20]{1,0:T(8,128)S(1)} %get-tuple-element.29, f32[20,20]{1,0:T(8,128)S(1)} %get-tuple-element.27, f32[20,20]{1,0:T(8,128)S(1)} %get-tuple-element.26), kind=kLoop, calls=%fused_computation | loop fusion | flops 4800 | bytes 12800 | tf_op jit(solution)/shard_map/concatenate | solution.py:306
  16.0 5.1 %tracers.1 = (f32[20,40,512]{2,1,0:T(8,128)}, f32[8,512]{1,0:T(8,128)}) custom-call(f32[20,40,512]{2,1,0:T(8,128)} %bitcast.23, f32[5,20,512]{2,1,0:T(8,128)} %get-tuple-element.15.coef_ref, f32[64,128]{1,0:T(8,128)} %copy-done, f32[64,128]{1,0:T(8,128)} %copy-done.1), custom_call_target="tpu_custom_call" | custom-call | flops 3686400 | bytes 3276800 | tf_op jit(solution)/shard_map/tracers/pallas_call | solution.py:284
  21.0 0.0 collective-permute-done.4.refs_2_
  21.0 0.0 collective-permute-done.3.refs_1_
  21.1 0.0 collective-permute-done.2.refs_0_
  21.1 0.6 %copy-done.3 = f32[80,128]{1,0:T(8,128)} copy-done((f32[80,128]{1,0:T(8,128)}, f32[80,128]{1,0:T(8,128)S(1)}, u32[]{:S(2)}) %copy-start.3) | copy-done | bytes 40984
  21.7 0.0 copy-done.4
  21.7 0.0 copy-done.5
  21.7 1.7 %surface.1 = (f32[20,512]{1,0:T(8,128)}, f32[32,128]{1,0:T(8,128)}) custom-call(f32[20,80]{1,0:T(8,128)} %pad_maximum_fusion.m_ref, f32[80,128]{1,0:T(8,128)} %get-tuple-element.14.own_ref, f32[80,128]{1,0:T(8,128)} %copy-done.5, f32[80,128]{1,0:T(8,128)} %copy-done.4, f32[80,128]{1,0:T(8,128)} %copy-done.3, f32[8,512]{1,0:T(8,128)} %get-tuple-element.16.refs_3_.top_ref), custom_call_target="tpu_custom_call" | custom-call | tf_op jit(solution)/shard_map/surface/pallas_call | solution.py:307
  23.4 1.8 %collective-permute-start.8 = (f32[32,128]{1,0:T(8,128)}, f32[32,128]{1,0:T(8,128)S(1)}, u32[]{:S(2)}, u32[]{:S(2)}) collective-permute-start(f32[32,128]{1,0:T(8,128)} %get-tuple-element.18), channel_id=1, source_target_pairs={{0,28},{1,29},{2,30},{3,31},{4,24},{5,25},{6,26},{7,27},{8,20},{9,... | collective-permute-start | bytes 49160 | tf_op jit(solution)/shard_map/ppermute | solution.py:319
  25.2 0.7 %collective-permute-start.7 = (f32[32,128]{1,0:T(8,128)}, f32[32,128]{1,0:T(8,128)S(1)}, u32[]{:S(2)}, u32[]{:S(2)}) collective-permute-start(f32[32,128]{1,0:T(8,128)} %get-tuple-element.18), channel_id=1, source_target_pairs={{0,24},{1,25},{2,26},{3,27},{4,28},{5,29},{6,30},{7,31},{8,16},{9,... | collective-permute-start | bytes 49160 | tf_op jit(solution)/shard_map/ppermute | solution.py:319
  25.9 1.4 %collective-permute-start.6 = (f32[32,128]{1,0:T(8,128)}, f32[32,128]{1,0:T(8,128)S(1)}, u32[]{:S(2)}, u32[]{:S(2)}) collective-permute-start(f32[32,128]{1,0:T(8,128)} %get-tuple-element.18), channel_id=1, source_target_pairs={{0,20},{1,21},{2,22},{3,23},{4,16},{5,17},{6,18},{7,19},{8,28},{9,... | collective-permute-start | bytes 49160 | tf_op jit(solution)/shard_map/ppermute | solution.py:319
  27.4 0.4 %collective-permute-start.5 = (f32[32,128]{1,0:T(8,128)}, f32[32,128]{1,0:T(8,128)S(1)}, u32[]{:S(2)}, u32[]{:S(2)}) collective-permute-start(f32[32,128]{1,0:T(8,128)} %get-tuple-element.18), channel_id=1, source_target_pairs={{0,16},{1,17},{2,18},{3,19},{4,20},{5,21},{6,22},{7,23},{8,24},{9,... | collective-permute-start | bytes 49160 | tf_op jit(solution)/shard_map/ppermute | solution.py:319
  27.8 1.2 %slice.4 = s32[1,1]{1,0:T(1,128)} slice(s32[4,512]{1,0:T(4,128)} %bitcast.31), slice={[0:1], [0:1]} | slice | bytes 8 | tf_op jit(solution)/shard_map/slice | solution.py:334
  29.7 0.0 collective-permute-done.8.refs_3_
  29.7 0.4 %collective-permute-done.7.refs_2_ = f32[32,128]{1,0:T(8,128)S(1)} collective-permute-done((f32[32,128]{1,0:T(8,128)}, f32[32,128]{1,0:T(8,128)S(1)}, u32[]{:S(2)}, u32[]{:S(2)}) %collective-permute-start.7) | collective-permute-done | bytes 16416 | tf_op jit(solution)/shard_map/ppermute | solution.py:319
  30.1 0.0 collective-permute-done.6.refs_1_
  30.1 1.2 %collective-permute-done.5.refs_0_ = f32[32,128]{1,0:T(8,128)S(1)} collective-permute-done((f32[32,128]{1,0:T(8,128)}, f32[32,128]{1,0:T(8,128)S(1)}, u32[]{:S(2)}, u32[]{:S(2)}) %collective-permute-start.5) | collective-permute-done | bytes 16416 | tf_op jit(solution)/shard_map/ppermute | solution.py:319
  31.3 0.6 %copy-done.9 = f32[32,128]{1,0:T(8,128)} copy-done((f32[32,128]{1,0:T(8,128)}, f32[32,128]{1,0:T(8,128)S(1)}, u32[]{:S(2)}) %copy-start.9) | copy-done | bytes 16408
  31.9 2.3 %remap.1 = (f32[80,128]{1,0:T(8,128)}, f32[20,40,512]{2,1,0:T(8,128)}) custom-call(s32[1]{0:T(128)S(6)} %mul.16.first_ref, f32[20,512]{1,0:T(8,128)} %get-tuple-element.17.mixed_ref, f32[8,512]{1,0:T(8,128)} %get-tuple-element.16.refs_3_.top_ref, s32[4,512]{1,0:T(4,128)} %bitcast.32, f32[4,512]{1,0:T(4,128)} %bitcast.33, ...), custom_call_target="tpu_custom_call", output_to_operand_aliasing={{1}: (10, {})} | custom-call | tf_op jit(solution)/shard_map/remap/pallas_call | solution.py:335
  (14 shorter events, 0.0 us)
Async XLA Ops:
  0.6 6.1 %copy-start.2 = (f32[1,80,80]{2,1,0:T(8,128)S(1)}, f32[1,80,80]{2,1,0:T(8,128)}, u32[]{:S(2)}) copy-start(f32[1,80,80]{2,1,0:T(8,128)} %param.12) | copy-start | bytes 76804
  3.5 3.2 %collective-permute-start = (f32[64,128]{1,0:T(8,128)}, f32[64,128]{1,0:T(8,128)S(1)}, u32[]{:S(2)}, u32[]{:S(2)}) collective-permute-start(f32[64,128]{1,0:T(8,128)} %get-tuple-element.12), channel_id=1, source_target_pairs={{0,4},{4,0},{8,12},{12,8},{1,5},{5,1},{9,13},{13,9},{2,6},{6,2},{1... | collective-permute-start | bytes 98312 | tf_op jit(solution)/shard_map/ppermute | solution.py:266
  4.1 4.5 %collective-permute-start.1 = (f32[64,128]{1,0:T(8,128)}, f32[64,128]{1,0:T(8,128)S(1)}, u32[]{:S(2)}, u32[]{:S(2)}) collective-permute-start(f32[64,128]{1,0:T(8,128)} %get-tuple-element.13), channel_id=1, source_target_pairs={{0,12},{4,8},{8,4},{12,0},{1,13},{5,9},{9,5},{13,1},{2,14},{6,10},... | collective-permute-start | bytes 98312 | tf_op jit(solution)/shard_map/ppermute | solution.py:267
  6.8 1.8 %copy-start = (f32[64,128]{1,0:T(8,128)}, f32[64,128]{1,0:T(8,128)S(1)}, u32[]{:S(2)}) copy-start(f32[64,128]{1,0:T(8,128)S(1)} %collective-permute-done.a_ref) | copy-start | bytes 98308
  8.6 0.6 %copy-start.1 = (f32[64,128]{1,0:T(8,128)}, f32[64,128]{1,0:T(8,128)S(1)}, u32[]{:S(2)}) copy-start(f32[64,128]{1,0:T(8,128)S(1)} %collective-permute-done.1.b_ref) | copy-start | bytes 98308
  10.9 10.1 %collective-permute-start.4 = (f32[80,128]{1,0:T(8,128)}, f32[80,128]{1,0:T(8,128)S(1)}, u32[]{:S(2)}, u32[]{:S(2)}) collective-permute-start(f32[80,128]{1,0:T(8,128)} %get-tuple-element.14.own_ref), channel_id=1, source_target_pairs={{0,3},{1,2},{2,1},{3,0},{4,7},{5,6},{6,5},{7,4},{8,11},{9,10},{10,... | collective-permute-start | bytes 122888 | tf_op jit(solution)/shard_map/ppermute | solution.py:278
  14.6 6.4 %collective-permute-start.3 = (f32[80,128]{1,0:T(8,128)}, f32[80,128]{1,0:T(8,128)S(1)}, u32[]{:S(2)}, u32[]{:S(2)}) collective-permute-start(f32[80,128]{1,0:T(8,128)} %get-tuple-element.14.own_ref), channel_id=1, source_target_pairs={{0,2},{1,3},{2,0},{3,1},{4,6},{5,7},{6,4},{7,5},{8,10},{9,11},{10,... | collective-permute-start | bytes 122888 | tf_op jit(solution)/shard_map/ppermute | solution.py:278
  14.6 6.5 %collective-permute-start.2 = (f32[80,128]{1,0:T(8,128)}, f32[80,128]{1,0:T(8,128)S(1)}, u32[]{:S(2)}, u32[]{:S(2)}) collective-permute-start(f32[80,128]{1,0:T(8,128)} %get-tuple-element.14.own_ref), channel_id=1, source_target_pairs={{0,1},{1,0},{2,3},{3,2},{4,5},{5,4},{6,7},{7,6},{8,9},{9,8},{10,11... | collective-permute-start | bytes 122888 | tf_op jit(solution)/shard_map/ppermute | solution.py:278
  21.0 0.6 %copy-start.3 = (f32[80,128]{1,0:T(8,128)}, f32[80,128]{1,0:T(8,128)S(1)}, u32[]{:S(2)}) copy-start(f32[80,128]{1,0:T(8,128)S(1)} %collective-permute-done.4.refs_2_) | copy-start | bytes 122884
  21.1 0.6 %copy-start.4 = (f32[80,128]{1,0:T(8,128)}, f32[80,128]{1,0:T(8,128)S(1)}, u32[]{:S(2)}) copy-start(f32[80,128]{1,0:T(8,128)S(1)} %collective-permute-done.3.refs_1_) | copy-start | bytes 122884
  21.1 0.6 %copy-start.5 = (f32[80,128]{1,0:T(8,128)}, f32[80,128]{1,0:T(8,128)S(1)}, u32[]{:S(2)}) copy-start(f32[80,128]{1,0:T(8,128)S(1)} %collective-permute-done.2.refs_0_) | copy-start | bytes 122884
  23.4 6.3 %collective-permute-start.8 = (f32[32,128]{1,0:T(8,128)}, f32[32,128]{1,0:T(8,128)S(1)}, u32[]{:S(2)}, u32[]{:S(2)}) collective-permute-start(f32[32,128]{1,0:T(8,128)} %get-tuple-element.18), channel_id=1, source_target_pairs={{0,28},{1,29},{2,30},{3,31},{4,24},{5,25},{6,26},{7,27},{8,20},{9,... | collective-permute-start | bytes 49160 | tf_op jit(solution)/shard_map/ppermute | solution.py:319
  25.2 4.9 %collective-permute-start.7 = (f32[32,128]{1,0:T(8,128)}, f32[32,128]{1,0:T(8,128)S(1)}, u32[]{:S(2)}, u32[]{:S(2)}) collective-permute-start(f32[32,128]{1,0:T(8,128)} %get-tuple-element.18), channel_id=1, source_target_pairs={{0,24},{1,25},{2,26},{3,27},{4,28},{5,29},{6,30},{7,31},{8,16},{9,... | collective-permute-start | bytes 49160 | tf_op jit(solution)/shard_map/ppermute | solution.py:319
  25.9 4.2 %collective-permute-start.6 = (f32[32,128]{1,0:T(8,128)}, f32[32,128]{1,0:T(8,128)S(1)}, u32[]{:S(2)}, u32[]{:S(2)}) collective-permute-start(f32[32,128]{1,0:T(8,128)} %get-tuple-element.18), channel_id=1, source_target_pairs={{0,20},{1,21},{2,22},{3,23},{4,16},{5,17},{6,18},{7,19},{8,28},{9,... | collective-permute-start | bytes 49160 | tf_op jit(solution)/shard_map/ppermute | solution.py:319
  27.4 3.9 %collective-permute-start.5 = (f32[32,128]{1,0:T(8,128)}, f32[32,128]{1,0:T(8,128)S(1)}, u32[]{:S(2)}, u32[]{:S(2)}) collective-permute-start(f32[32,128]{1,0:T(8,128)} %get-tuple-element.18), channel_id=1, source_target_pairs={{0,16},{1,17},{2,18},{3,19},{4,20},{5,21},{6,22},{7,23},{8,24},{9,... | collective-permute-start | bytes 49160 | tf_op jit(solution)/shard_map/ppermute | solution.py:319
  29.7 1.7 %copy-start.6 = (f32[32,128]{1,0:T(8,128)}, f32[32,128]{1,0:T(8,128)S(1)}, u32[]{:S(2)}) copy-start(f32[32,128]{1,0:T(8,128)S(1)} %collective-permute-done.8.refs_3_) | copy-start | bytes 49156
  30.1 1.2 %copy-start.7 = (f32[32,128]{1,0:T(8,128)}, f32[32,128]{1,0:T(8,128)S(1)}, u32[]{:S(2)}) copy-start(f32[32,128]{1,0:T(8,128)S(1)} %collective-permute-done.7.refs_2_) | copy-start | bytes 49156
  30.1 1.2 %copy-start.8 = (f32[32,128]{1,0:T(8,128)}, f32[32,128]{1,0:T(8,128)S(1)}, u32[]{:S(2)}) copy-start(f32[32,128]{1,0:T(8,128)S(1)} %collective-permute-done.6.refs_1_) | copy-start | bytes 49156
  31.3 0.6 %copy-start.9 = (f32[32,128]{1,0:T(8,128)}, f32[32,128]{1,0:T(8,128)S(1)}, u32[]{:S(2)}) copy-start(f32[32,128]{1,0:T(8,128)S(1)} %collective-permute-done.5.refs_0_) | copy-start | bytes 49156

commit v2 on v1

--- a/solution.py
+++ b/solution.py
@@ -15,6 +15,7 @@
 VMEM = pl.BlockSpec(memory_space=pltpu.VMEM)
 SMEM = pl.BlockSpec(memory_space=pltpu.SMEM)
 ANY = pl.BlockSpec(memory_space=pl.ANY)
+PARAMS = pltpu.CompilerParams(vmem_limit_bytes=8 * 2**20)
 
 
 def padded_rows(n):
@@ -259,6 +260,7 @@
         in_specs=[VMEM, VMEM, VMEM, ANY],
         out_specs=[VMEM, VMEM],
         scratch_shapes=[pltpu.VMEM((levels, tracers, LANES), f32)] * 2 + [pltpu.SemaphoreType.DMA((2,))],
+        compiler_params=PARAMS,
         name="pack",
     )(t, u, n, q)
     swap_a = [(i, i ^ 1) for i in range(tile_count)]
@@ -271,6 +273,7 @@
         out_shape=[shape((rows, LANES), f32), shape((5, levels, width), f32)],
         in_specs=[VMEM] * 5,
         out_specs=[VMEM, VMEM],
+        compiler_params=PARAMS,
         name="heat",
     )(t, u, n, got_a, got_b)
 
@@ -295,6 +298,7 @@
         cost_estimate=pl.CostEstimate(
             flops=9 * levels * tracers * width, bytes_accessed=8 * levels * tracers * width, transcendentals=0
         ),
+        compiler_params=PARAMS,
         name="tracers",
     )(q, coef, got_a, got_b)
 
@@ -310,6 +314,7 @@
         in_specs=[VMEM] * (lev_count + 2),
         out_specs=[VMEM, VMEM],
         scratch_shapes=[pltpu.VMEM((levels * lev_count, width), f32)],
+        compiler_params=PARAMS,
         name="surface",
     )(matrix, heat, *others, top)
 
@@ -343,6 +348,7 @@
             pltpu.SemaphoreType.DMA,
         ],
         input_output_aliases={6 + tile_count: 1},
+        compiler_params=PARAMS,
         name="remap",
     )(
         first, mixed, top, index, exchange_weight_table.T, water_indicator.reshape(1, width), *got, moved

time: 34.7 us -> 28.4 us (0.82)
  Pallas kernels: 13.7 us -> 5.94 us
  local copies, waits for them, and re-layouts: 3.09 us -> 4.39 us
  waiting for transfers between devices: 3.47 us -> 4.2 us
  other arithmetic: 0.68 us -> 0.08 us
    pallas_call x1, Pallas kernels: 2.89 us -> 0.49 us  [body(): pl.pallas_call(functools.partial(pack_kernel, levels, tiles, tracers), ou...]
    unnamed x20 -> x24, local copies, waits for them, and re-layouts: 1.82 us -> 3.8 us
    pallas_call x1, Pallas kernels: 5.07 us -> 3.58 us  [body(): pl.pallas_call(functools.partial(tracer_kernel, block, tracers), out_shap...]
    pallas_call x1, Pallas kernels: 1.71 us -> 0.22 us  [body(): pl.pallas_call(functools.partial(surface_kernel, levels, tiles, lev_count...]
    pallas_call x1, Pallas kernels: 1.68 us -> 0.23 us  [body(): pl.pallas_call(functools.partial(heat_kernel, levels, tiles, tracers, sec...]
    pallas_call x1, Pallas kernels: 2.3 us -> 1.43 us  [body(): pl.pallas_call(functools.partial(final_kernel, levels, tiles, tile_count,...]
    slice x1, local copies, waits for them, and re-layouts: 1.19 us -> 0.51 us  [body(): first = (index[0, 0:1] + REACH) % cells // width * tiles]
    concatenate x1, other arithmetic: 0.68 us -> 0.08 us  [body(): matrix = jnp.concatenate(columns, axis=1)]
  transfers between devices with their start and end apart: 9 -> 9, of which waited for: 3 -> 4; matrix products, arithmetic and copies ran while one was open for 6% -> 2% of each run, Pallas kernels for 15% -> 13%
where the time goes in v2:
time: 28.4 us; the launch traced here: 28 us
  starting transfers between devices  12 us (42%)
  Pallas kernels  5.94 us (21%)
  local copies, waits for them, and re-layouts  4.39 us (15%)
  waiting for transfers between devices  4.2 us (15%)
  between operations  1.41 us (5%)
    ppermute x3, starting transfers between devices, body(): lax.ppermute(heat, 'lev', [(i, peer(i, s, lev_count)) for i in range(lev_...  4.45 us
    ppermute x4, starting transfers between devices, body(): lax.ppermute(surface, ('comp', 'tile', 'lev'), [(place(c, i, l), place((c...  4.4 us
    unnamed x24, local copies, waits for them, and re-layouts  3.8 us
    pallas_call x1, Pallas kernels, body(): pl.pallas_call(functools.partial(tracer_kernel, block, tracers), out_shap...  3.58 us
    ppermute x1, starting transfers between devices, body(): got_b = lax.ppermute(send_b, 'tile', swap_b)  2.59 us
    ppermute x4, waiting for transfers between devices, body(): lax.ppermute(surface, ('comp', 'tile', 'lev'), [(place(c, i, l), place((c...  2.02 us
    ppermute x1, waiting for transfers between devices, body(): got_b = lax.ppermute(send_b, 'tile', swap_b)  1.59 us
    pallas_call x1, Pallas kernels, body(): pl.pallas_call(functools.partial(final_kernel, levels, tiles, tile_count,...  1.43 us
  transfers between devices with their start and end apart: 9, of which 4 were waited for; matrix products, arithmetic and copies ran while one was open for 2% of the time, Pallas kernels for 13%

profile of v2, /device:TPU:0, one launch (start us, length us, event | category | flops | bytes accessed | tf_op | source)
XLA Modules:
  0.0 28.0 jit_solution(9336901651805054506)
XLA Ops:
  0.6 1.4 %copy-done = f32[1,40,20,512]{3,1,2,0:T(8,128)S(1)} copy-done((f32[1,40,20,512]{3,1,2,0:T(8,128)S(1)}, f32[1,40,20,512]{3,1,2,0:T(8,128)}, u32[]{:S(2)}) %copy-start) | copy-done | bytes 1638424
  2.1 0.8 %copy-done.2 = f32[1,20,512]{2,0,1:T(1,128)S(1)} copy-done((f32[1,20,512]{2,0,1:T(1,128)S(1)}, f32[1,20,512]{2,0,1:T(1,128)}, u32[]{:S(2)}) %copy-start.2) | copy-done | bytes 40984
  2.8 0.8 %copy-done.4 = f32[1,20,512]{2,0,1:T(1,128)S(1)} copy-done((f32[1,20,512]{2,0,1:T(1,128)S(1)}, f32[1,20,512]{2,0,1:T(1,128)}, u32[]{:S(2)}) %copy-start.4) | copy-done | bytes 40984
  3.6 0.8 %copy-done.6 = f32[1,20,512]{2,0,1:T(1,128)S(1)} copy-done((f32[1,20,512]{2,0,1:T(1,128)S(1)}, f32[1,20,512]{2,0,1:T(1,128)}, u32[]{:S(2)}) %copy-start.6) | copy-done | bytes 40984
  4.4 0.5 %pack.1 = (f32[64,128]{1,0:T(8,128)S(1)}, f32[64,128]{1,0:T(8,128)S(1)}) custom-call(f32[80,128]{1,0:T(8,128)S(1)} %bitcast.24, f32[80,128]{1,0:T(8,128)S(1)} %bitcast.26, f32[80,128]{1,0:T(8,128)S(1)} %bitcast.28, f32[20,40,512]{2,1,0:T(8,128)S(1)} %bitcast.22), custom_call_target="tpu_custom_call" | custom-call | tf_op jit(solution)/shard_map/pack/pallas_call | solution.py:257
  4.9 0.0 copy-start.8
  4.9 0.0 copy-start.9
  4.9 0.0 copy-start.10
  5.0 0.6 %collective-permute-start = (f32[64,128]{1,0:T(8,128)S(1)}, f32[64,128]{1,0:T(8,128)S(1)}, u32[]{:S(2)}, u32[]{:S(2)}) collective-permute-start(f32[64,128]{1,0:T(8,128)S(1)} %get-tuple-element.12), channel_id=1, source_target_pairs={{0,4},{4,0},{8,12},{12,8},{1,5},{5,1},{9,13},{13,9},{2,6},{6,2},{1... | collective-permute-start | bytes 98312 | tf_op jit(solution)/shard_map/ppermute | solution.py:268
  5.5 2.6 %collective-permute-start.1 = (f32[64,128]{1,0:T(8,128)S(1)}, f32[64,128]{1,0:T(8,128)S(1)}, u32[]{:S(2)}, u32[]{:S(2)}) collective-permute-start(f32[64,128]{1,0:T(8,128)S(1)} %get-tuple-element.13), channel_id=1, source_target_pairs={{0,12},{4,8},{8,4},{12,0},{1,13},{5,9},{9,5},{13,1},{2,14},{6,10},... | collective-permute-start | bytes 98312 | tf_op jit(solution)/shard_map/ppermute | solution.py:269
  8.1 0.1 dynamic-slice_bitcast_fusion.3
  8.2 0.0 collective-permute-done.a_ref
  8.2 1.6 %collective-permute-done.1.b_ref = f32[64,128]{1,0:T(8,128)S(1)} collective-permute-done((f32[64,128]{1,0:T(8,128)S(1)}, f32[64,128]{1,0:T(8,128)S(1)}, u32[]{:S(2)}, u32[]{:S(2)}) %collective-permute-start.1) | collective-permute-done | bytes 32800 | tf_op jit(solution)/shard_map/ppermute | solution.py:269
  9.8 0.2 heat.1
  10.0 3.8 %collective-permute-start.4 = (f32[80,128]{1,0:T(8,128)S(1)}, f32[80,128]{1,0:T(8,128)S(1)}, u32[]{:S(2)}, u32[]{:S(2)}) collective-permute-start(f32[80,128]{1,0:T(8,128)S(1)} %get-tuple-element.14.own_ref), channel_id=1, source_target_pairs={{0,3},{1,2},{2,1},{3,0},{4,7},{5,6},{6,5},{7,4},{8,11},{9,10},{10,... | collective-permute-start | bytes 122888 | tf_op jit(solution)/shard_map/ppermute | solution.py:281
  13.8 0.0 collective-permute-start.3
  13.8 0.7 %collective-permute-start.2 = (f32[80,128]{1,0:T(8,128)S(1)}, f32[80,128]{1,0:T(8,128)S(1)}, u32[]{:S(2)}, u32[]{:S(2)}) collective-permute-start(f32[80,128]{1,0:T(8,128)S(1)} %get-tuple-element.14.own_ref), channel_id=1, source_target_pairs={{0,1},{1,0},{2,3},{3,2},{4,5},{5,4},{6,7},{7,6},{8,9},{9,8},{10,11... | collective-permute-start | bytes 122888 | tf_op jit(solution)/shard_map/ppermute | solution.py:281
  14.5 0.1 pad_maximum_fusion.m_ref
  14.6 3.6 %tracers.1 = (f32[20,40,512]{2,1,0:T(8,128)}, f32[8,512]{1,0:T(8,128)S(1)}) custom-call(f32[20,40,512]{2,1,0:T(8,128)S(1)} %bitcast.23, f32[5,20,512]{2,1,0:T(8,128)S(1)} %get-tuple-element.15.coef_ref, f32[64,128]{1,0:T(8,128)S(1)} %collective-permute-done.a_ref, f32[64,128]{1,0:T(8,128)S(1)} %collective-permute-done.1.b_ref), custom_call_target="tpu_custom_call" | custom-call | flops 3686400 | bytes 3276800 | tf_op jit(solution)/shard_map/tracers/pallas_call | solution.py:287
  18.1 0.0 collective-permute-done.4.refs_2_
  18.1 0.6 %collective-permute-done.3.refs_1_ = f32[80,128]{1,0:T(8,128)S(1)} collective-permute-done((f32[80,128]{1,0:T(8,128)S(1)}, f32[80,128]{1,0:T(8,128)S(1)}, u32[]{:S(2)}, u32[]{:S(2)}) %collective-permute-start.3) | collective-permute-done | bytes 40992 | tf_op jit(solution)/shard_map/ppermute | solution.py:281
  18.7 0.0 collective-permute-done.2.refs_0_
  18.7 0.2 surface.1
  18.9 1.4 %collective-permute-start.8 = (f32[32,128]{1,0:T(8,128)S(1)}, f32[32,128]{1,0:T(8,128)S(1)}, u32[]{:S(2)}, u32[]{:S(2)}) collective-permute-start(f32[32,128]{1,0:T(8,128)S(1)} %get-tuple-element.18), channel_id=1, source_target_pairs={{0,28},{1,29},{2,30},{3,31},{4,24},{5,25},{6,26},{7,27},{8,20},{9,... | collective-permute-start | bytes 49160 | tf_op jit(solution)/shard_map/ppermute | solution.py:324
  20.4 1.1 %collective-permute-start.7 = (f32[32,128]{1,0:T(8,128)S(1)}, f32[32,128]{1,0:T(8,128)S(1)}, u32[]{:S(2)}, u32[]{:S(2)}) collective-permute-start(f32[32,128]{1,0:T(8,128)S(1)} %get-tuple-element.18), channel_id=1, source_target_pairs={{0,24},{1,25},{2,26},{3,27},{4,28},{5,29},{6,30},{7,31},{8,16},{9,... | collective-permute-start | bytes 49160 | tf_op jit(solution)/shard_map/ppermute | solution.py:324
  21.5 1.4 %collective-permute-start.6 = (f32[32,128]{1,0:T(8,128)S(1)}, f32[32,128]{1,0:T(8,128)S(1)}, u32[]{:S(2)}, u32[]{:S(2)}) collective-permute-start(f32[32,128]{1,0:T(8,128)S(1)} %get-tuple-element.18), channel_id=1, source_target_pairs={{0,20},{1,21},{2,22},{3,23},{4,16},{5,17},{6,18},{7,19},{8,28},{9,... | collective-permute-start | bytes 49160 | tf_op jit(solution)/shard_map/ppermute | solution.py:324
  22.8 0.5 %collective-permute-start.5 = (f32[32,128]{1,0:T(8,128)S(1)}, f32[32,128]{1,0:T(8,128)S(1)}, u32[]{:S(2)}, u32[]{:S(2)}) collective-permute-start(f32[32,128]{1,0:T(8,128)S(1)} %get-tuple-element.18), channel_id=1, source_target_pairs={{0,16},{1,17},{2,18},{3,19},{4,20},{5,21},{6,22},{7,23},{8,24},{9,... | collective-permute-start | bytes 49160 | tf_op jit(solution)/shard_map/ppermute | solution.py:324
  23.3 0.5 %slice.4 = s32[1,1]{1,0:T(1,128)} slice(s32[4,512]{1,0:T(4,128)S(1)} %bitcast.30), slice={[0:1], [0:1]} | slice | bytes 8 | tf_op jit(solution)/shard_map/slice | solution.py:339
  24.6 0.4 %collective-permute-done.7.refs_2_ = f32[32,128]{1,0:T(8,128)S(1)} collective-permute-done((f32[32,128]{1,0:T(8,128)S(1)}, f32[32,128]{1,0:T(8,128)S(1)}, u32[]{:S(2)}, u32[]{:S(2)}) %collective-permute-start.7) | collective-permute-done | bytes 16416 | tf_op jit(solution)/shard_map/ppermute | solution.py:324
  25.0 0.0 collective-permute-done.6.refs_1_
  25.0 1.6 %collective-permute-done.5.refs_0_ = f32[32,128]{1,0:T(8,128)S(1)} collective-permute-done((f32[32,128]{1,0:T(8,128)S(1)}, f32[32,128]{1,0:T(8,128)S(1)}, u32[]{:S(2)}, u32[]{:S(2)}) %collective-permute-start.5) | collective-permute-done | bytes 16416 | tf_op jit(solution)/shard_map/ppermute | solution.py:324
  26.6 1.4 %remap.1 = (f32[80,128]{1,0:T(8,128)}, f32[20,40,512]{2,1,0:T(8,128)}) custom-call(s32[1]{0:T(128)S(6)} %mul.16.first_ref, f32[20,512]{1,0:T(8,128)S(1)} %get-tuple-element.17.mixed_ref, f32[8,512]{1,0:T(8,128)S(1)} %get-tuple-element.16.refs_3_.top_ref, s32[4,512]{1,0:T(4,128)S(1)} %bitcast.31, ...), custom_call_target="tpu_custom_call", output_to_operand_aliasing={{1}: (10, {})} | custom-call | tf_op jit(solution)/shard_map/remap/pallas_call | solution.py:340
  (18 shorter events, 0.0 us)
Async XLA Ops:
  0.6 1.4 %copy-start = (f32[1,40,20,512]{3,1,2,0:T(8,128)S(1)}, f32[1,40,20,512]{3,1,2,0:T(8,128)}, u32[]{:S(2)}) copy-start(f32[1,40,20,512]{3,1,2,0:T(8,128)} %param.10) | copy-start | bytes 4915204
  2.1 0.8 %copy-start.2 = (f32[1,20,512]{2,0,1:T(1,128)S(1)}, f32[1,20,512]{2,0,1:T(1,128)}, u32[]{:S(2)}) copy-start(f32[1,20,512]{2,0,1:T(1,128)} %param.8) | copy-start | bytes 122884
  2.8 0.8 %copy-start.4 = (f32[1,20,512]{2,0,1:T(1,128)S(1)}, f32[1,20,512]{2,0,1:T(1,128)}, u32[]{:S(2)}) copy-start(f32[1,20,512]{2,0,1:T(1,128)} %param.9) | copy-start | bytes 122884
  3.6 0.8 %copy-start.6 = (f32[1,20,512]{2,0,1:T(1,128)S(1)}, f32[1,20,512]{2,0,1:T(1,128)}, u32[]{:S(2)}) copy-start(f32[1,20,512]{2,0,1:T(1,128)} %param.11) | copy-start | bytes 122884
  4.4 3.7 %copy-start.11 = (f32[1,80,80]{2,1,0:T(8,128)S(1)}, f32[1,80,80]{2,1,0:T(8,128)}, u32[]{:S(2)}) copy-start(f32[1,80,80]{2,1,0:T(8,128)} %param.12) | copy-start | bytes 76804
  4.4 5.4 %copy-start.3 = (f32[1,20,512]{2,0,1:T(1,128)S(1)}, f32[1,20,512]{2,0,1:T(1,128)}, u32[]{:S(2)}) copy-start(f32[1,20,512]{2,0,1:T(1,128)} %param.8) | copy-start | bytes 122884
  4.4 5.4 %copy-start.5 = (f32[1,20,512]{2,0,1:T(1,128)S(1)}, f32[1,20,512]{2,0,1:T(1,128)}, u32[]{:S(2)}) copy-start(f32[1,20,512]{2,0,1:T(1,128)} %param.9) | copy-start | bytes 122884
  4.4 5.4 %copy-start.7 = (f32[1,20,512]{2,0,1:T(1,128)S(1)}, f32[1,20,512]{2,0,1:T(1,128)}, u32[]{:S(2)}) copy-start(f32[1,20,512]{2,0,1:T(1,128)} %param.11) | copy-start | bytes 122884
  4.4 10.2 %copy-start.1 = (f32[1,40,20,512]{3,1,2,0:T(8,128)S(1)}, f32[1,40,20,512]{3,1,2,0:T(8,128)}, u32[]{:S(2)}) copy-start(f32[1,40,20,512]{3,1,2,0:T(8,128)} %param.10) | copy-start | bytes 4915204
  4.9 18.4 %copy-start.8 = (s32[512,4]{0,1:T(4,128)S(1)}, s32[512,4]{0,1:T(4,128)}, u32[]{:S(2)}) copy-start(s32[512,4]{0,1:T(4,128)} %param.14) | copy-start | bytes 24580
  4.9 21.7 %copy-start.9 = (f32[512,4]{0,1:T(4,128)S(1)}, f32[512,4]{0,1:T(4,128)}, u32[]{:S(2)}) copy-start(f32[512,4]{0,1:T(4,128)} %param.13) | copy-start | bytes 24580
  4.9 21.6 %copy-start.10 = (s32[512]{0:T(512)S(1)}, s32[512]{0:T(512)}, u32[]{:S(2)}) copy-start(s32[512]{0:T(512)} %param.15) | copy-start | bytes 6148
  5.0 3.2 %collective-permute-start = (f32[64,128]{1,0:T(8,128)S(1)}, f32[64,128]{1,0:T(8,128)S(1)}, u32[]{:S(2)}, u32[]{:S(2)}) collective-permute-start(f32[64,128]{1,0:T(8,128)S(1)} %get-tuple-element.12), channel_id=1, source_target_pairs={{0,4},{4,0},{8,12},{12,8},{1,5},{5,1},{9,13},{13,9},{2,6},{6,2},{1... | collective-permute-start | bytes 98312 | tf_op jit(solution)/shard_map/ppermute | solution.py:268
  5.5 4.3 %collective-permute-start.1 = (f32[64,128]{1,0:T(8,128)S(1)}, f32[64,128]{1,0:T(8,128)S(1)}, u32[]{:S(2)}, u32[]{:S(2)}) collective-permute-start(f32[64,128]{1,0:T(8,128)S(1)} %get-tuple-element.13), channel_id=1, source_target_pairs={{0,12},{4,8},{8,4},{12,0},{1,13},{5,9},{9,5},{13,1},{2,14},{6,10},... | collective-permute-start | bytes 98312 | tf_op jit(solution)/shard_map/ppermute | solution.py:269
  10.0 8.1 %collective-permute-start.4 = (f32[80,128]{1,0:T(8,128)S(1)}, f32[80,128]{1,0:T(8,128)S(1)}, u32[]{:S(2)}, u32[]{:S(2)}) collective-permute-start(f32[80,128]{1,0:T(8,128)S(1)} %get-tuple-element.14.own_ref), channel_id=1, source_target_pairs={{0,3},{1,2},{2,1},{3,0},{4,7},{5,6},{6,5},{7,4},{8,11},{9,10},{10,... | collective-permute-start | bytes 122888 | tf_op jit(solution)/shard_map/ppermute | solution.py:281
  13.8 4.9 %collective-permute-start.3 = (f32[80,128]{1,0:T(8,128)S(1)}, f32[80,128]{1,0:T(8,128)S(1)}, u32[]{:S(2)}, u32[]{:S(2)}) collective-permute-start(f32[80,128]{1,0:T(8,128)S(1)} %get-tuple-element.14.own_ref), channel_id=1, source_target_pairs={{0,2},{1,3},{2,0},{3,1},{4,6},{5,7},{6,4},{7,5},{8,10},{9,11},{10,... | collective-permute-start | bytes 122888 | tf_op jit(solution)/shard_map/ppermute | solution.py:281
  13.8 4.9 %collective-permute-start.2 = (f32[80,128]{1,0:T(8,128)S(1)}, f32[80,128]{1,0:T(8,128)S(1)}, u32[]{:S(2)}, u32[]{:S(2)}) collective-permute-start(f32[80,128]{1,0:T(8,128)S(1)} %get-tuple-element.14.own_ref), channel_id=1, source_target_pairs={{0,1},{1,0},{2,3},{3,2},{4,5},{5,4},{6,7},{7,6},{8,9},{9,8},{10,11... | collective-permute-start | bytes 122888 | tf_op jit(solution)/shard_map/ppermute | solution.py:281
  18.9 5.6 %collective-permute-start.8 = (f32[32,128]{1,0:T(8,128)S(1)}, f32[32,128]{1,0:T(8,128)S(1)}, u32[]{:S(2)}, u32[]{:S(2)}) collective-permute-start(f32[32,128]{1,0:T(8,128)S(1)} %get-tuple-element.18), channel_id=1, source_target_pairs={{0,28},{1,29},{2,30},{3,31},{4,24},{5,25},{6,26},{7,27},{8,20},{9,... | collective-permute-start | bytes 49160 | tf_op jit(solution)/shard_map/ppermute | solution.py:324
  20.4 4.6 %collective-permute-start.7 = (f32[32,128]{1,0:T(8,128)S(1)}, f32[32,128]{1,0:T(8,128)S(1)}, u32[]{:S(2)}, u32[]{:S(2)}) collective-permute-start(f32[32,128]{1,0:T(8,128)S(1)} %get-tuple-element.18), channel_id=1, source_target_pairs={{0,24},{1,25},{2,26},{3,27},{4,28},{5,29},{6,30},{7,31},{8,16},{9,... | collective-permute-start | bytes 49160 | tf_op jit(solution)/shard_map/ppermute | solution.py:324
  21.5 3.5 %collective-permute-start.6 = (f32[32,128]{1,0:T(8,128)S(1)}, f32[32,128]{1,0:T(8,128)S(1)}, u32[]{:S(2)}, u32[]{:S(2)}) collective-permute-start(f32[32,128]{1,0:T(8,128)S(1)} %get-tuple-element.18), channel_id=1, source_target_pairs={{0,20},{1,21},{2,22},{3,23},{4,16},{5,17},{6,18},{7,19},{8,28},{9,... | collective-permute-start | bytes 49160 | tf_op jit(solution)/shard_map/ppermute | solution.py:324
  22.8 3.7 %collective-permute-start.5 = (f32[32,128]{1,0:T(8,128)S(1)}, f32[32,128]{1,0:T(8,128)S(1)}, u32[]{:S(2)}, u32[]{:S(2)}) collective-permute-start(f32[32,128]{1,0:T(8,128)S(1)} %get-tuple-element.18), channel_id=1, source_target_pairs={{0,16},{1,17},{2,18},{3,19},{4,20},{5,21},{6,22},{7,23},{8,24},{9,... | collective-permute-start | bytes 49160 | tf_op jit(solution)/shard_map/ppermute | solution.py:324

commit v3 on v2

--- a/solution.py
+++ b/solution.py
@@ -14,7 +14,7 @@
 
 VMEM = pl.BlockSpec(memory_space=pltpu.VMEM)
 SMEM = pl.BlockSpec(memory_space=pltpu.SMEM)
-ANY = pl.BlockSpec(memory_space=pl.ANY)
+HBM = pl.BlockSpec(memory_space=pltpu.HBM)
 PARAMS = pltpu.CompilerParams(vmem_limit_bytes=8 * 2**20)
 
 
@@ -44,7 +44,7 @@
 
 def from_left(x, k, halo, place):
     moved = pltpu.roll(x, k, 1)
-    edge = pltpu.roll(halo, lax.rem(k - place - 2 + 4 * LANES, LANES), 1)
+    edge = pltpu.roll(halo, (k - place - 2) % LANES, 1)
     head = jnp.where(lane_iota(edge.shape) < k, edge, moved[:, :LANES])
     return jnp.concatenate([head, moved[:, LANES:]], axis=1)
 
@@ -52,19 +52,33 @@
 def from_right(x, k, halo, place):
     width = x.shape[1]
     moved = pltpu.roll(x, width - k, 1)
-    edge = pltpu.roll(halo, lax.rem(LANES - k - place + 4 * LANES, LANES), 1)
+    edge = pltpu.roll(halo, (-k - place) % LANES, 1)
     tail = jnp.where(lane_iota(edge.shape) >= LANES - k, edge, moved[:, width - LANES :])
     return jnp.concatenate([moved[:, : width - LANES], tail], axis=1)
 
 
-def pack_kernel(levels, tiles, tracers, t_ref, u_ref, n_ref, q_ref, a_ref, b_ref, left, right, sems):
+def pack_kernel(
+    levels, tiles, tracers, group, t_hbm, u_hbm, n_hbm, q_hbm, a_ref, b_ref, t_ref, u_ref, n_ref, left, right, sems
+):
     width = tiles * LANES
-    copies = [
-        pltpu.make_async_copy(q_ref.at[:, :, pl.ds(0, LANES)], left, sems.at[0]),
-        pltpu.make_async_copy(q_ref.at[:, :, pl.ds(width - LANES, LANES)], right, sems.at[1]),
-    ]
-    for copy in copies:
+    flats = [
+        pltpu.make_async_copy(source, target, sems.at[0, i])
+        for i, (source, target) in enumerate(((t_hbm, t_ref), (u_hbm, u_ref), (n_hbm, n_ref)))
+    ]
+    chunks = []
+    for g in range(levels // group):
+        cut = pl.ds(g * group, group)
+        chunks.append(
+            [
+                pltpu.make_async_copy(q_hbm.at[cut, :, pl.ds(0, LANES)], left.at[cut], sems.at[1, g]),
+                pltpu.make_async_copy(q_hbm.at[cut, :, pl.ds(width - LANES, LANES)], right.at[cut], sems.at[2, g]),
+            ]
+        )
+    for copy in flats:
         copy.start()
+    for chunk in chunks:
+        for copy in chunk:
+            copy.start()
     even = lax.rem(lax.axis_index("tile"), 2) == 0
     lane = lane_iota((levels, LANES))
 
@@ -76,19 +90,21 @@
             return jnp.where(lane < 2, t, jnp.where(lane < 4, u, n))
         return jnp.where(lane >= LANES - 2, t, jnp.where(lane >= LANES - 4, u, n))
 
+    for copy in flats:
+        copy.wait()
     small_left = small(0, (2, 4), True)
     small_right = small(tiles - 1, (LANES - 2, LANES - 4), False)
     a_ref[pl.ds(tracers, levels), :] = jnp.where(even, small_right, small_left)
     b_ref[pl.ds(tracers, levels), :] = jnp.where(even, small_left, small_right)
-    for copy in copies:
-        copy.wait()
     pair = lane_iota((tracers, LANES)) // 2
-    packed_left = left[0]
-    packed_right = pltpu.roll(right[0], 2, 1)
-    for level in range(1, levels):
-        here = pair == level
-        packed_left = jnp.where(here, pltpu.roll(left[level], 2 * level, 1), packed_left)
-        packed_right = jnp.where(here, pltpu.roll(right[level], 2 * level + 2, 1), packed_right)
+    packed_left = packed_right = jnp.zeros((tracers, LANES), jnp.float32)
+    for g, chunk in enumerate(chunks):
+        for copy in chunk:
+            copy.wait()
+        for level in range(g * group, (g + 1) * group):
+            here = pair == level
+            packed_left = jnp.where(here, pltpu.roll(left[level], 2 * level, 1), packed_left)
+            packed_right = jnp.where(here, pltpu.roll(right[level], (2 * level + 2) % LANES, 1), packed_right)
     a_ref[pl.ds(0, tracers), :] = jnp.where(even, packed_right, packed_left)
     b_ref[pl.ds(0, tracers), :] = jnp.where(even, packed_left, packed_right)
 
@@ -132,17 +148,17 @@
         heat_ref[pl.ds(tile, levels, stride=tiles), :] = heat[:, tile * LANES : (tile + 1) * LANES]
 
 
-def tracer_kernel(block, tracers, q_ref, coef_ref, a_ref, b_ref, out_ref, top_ref):
+def tracer_kernel(levels, group, tracers, q_ref, coef_ref, a_ref, b_ref, out_hbm, top_ref, new_ref, sems):
     even = lax.rem(lax.axis_index("tile"), 2) == 0
     got_a = a_ref[pl.ds(0, tracers), :]
     got_b = b_ref[pl.ds(0, tracers), :]
     low = jnp.where(even, got_b, got_a)
     high = jnp.where(even, got_a, got_b)
-    for i in range(block):
-        level = pl.program_id(0) * block + i
-        q = q_ref[i]
+    copies = []
+    for level in range(levels):
+        q = q_ref[level]
         place = 2 * level
-        e0, e1, e2, e3, e4 = [coef_ref[k, pl.ds(level, 1), :] for k in range(5)]
+        e0, e1, e2, e3, e4 = [coef_ref[k, level : level + 1, :] for k in range(5)]
         new = (
             e0 * q
             + e1 * from_left(q, 1, low, place)
@@ -150,12 +166,15 @@
             + e3 * from_left(q, 2, low, place)
             + e4 * from_right(q, 2, high, place)
         )
-        out_ref[i] = new
-        if i == 0:
-
-            @pl.when(pl.program_id(0) == 0)
-            def _():
-                top_ref[...] = new[:SUB]
+        new_ref[level] = new
+        if level == 0:
+            top_ref[...] = new[:SUB]
+        if level % group == group - 1:
+            cut = pl.ds(level - group + 1, group)
+            copies.append(pltpu.make_async_copy(new_ref.at[cut], out_hbm.at[cut], sems.at[level // group]))
+            copies[-1].start()
+    for copy in copies:
+        copy.wait()
 
 
 def surface_kernel(levels, tiles, count, m_ref, own_ref, *refs):
@@ -178,7 +197,7 @@
 def final_kernel(
     levels, tiles, count, sections, first_ref, mixed_ref, top_ref, index_ref, weight_ref, water_ref, *refs
 ):
-    got, (q_ref, heat_ref, out_ref, whole, patch, sem) = refs[:count], refs[count:]
+    got, (q_ref, heat_hbm, out_ref, whole, patch, heat_ref, sems) = refs[:count], refs[count:]
     del q_ref
     width = tiles * LANES
     cells = count * width
@@ -225,9 +244,14 @@
             pltpu.roll(renewed, SUB - 1, 0),
             top[:, cut],
         )
-    copy = pltpu.make_async_copy(patch, out_ref.at[0, pl.ds(0, SUB), :], sem)
-    copy.start()
-    copy.wait()
+    copies = [
+        pltpu.make_async_copy(patch, out_ref.at[0, pl.ds(0, SUB), :], sems.at[0]),
+        pltpu.make_async_copy(heat_ref, heat_hbm, sems.at[1]),
+    ]
+    for copy in copies:
+        copy.start()
+    for copy in copies:
+        copy.wait()
 
 
 def body(
@@ -254,15 +278,17 @@
     lev = lax.axis_index("lev")
 
     pack_rows = tracers + padded_rows(levels)
-    send_a, send_b = pl.pallas_call(
-        functools.partial(pack_kernel, levels, tiles, tracers),
-        out_shape=[shape((pack_rows, LANES), f32)] * 2,
-        in_specs=[VMEM, VMEM, VMEM, ANY],
-        out_specs=[VMEM, VMEM],
-        scratch_shapes=[pltpu.VMEM((levels, tracers, LANES), f32)] * 2 + [pltpu.SemaphoreType.DMA((2,))],
+    group = 5 if levels % 5 == 0 else 1
+    send_a, send_b, t_near, u_near, n_near = pl.pallas_call(
+        functools.partial(pack_kernel, levels, tiles, tracers, group),
+        out_shape=[shape((pack_rows, LANES), f32)] * 2 + [shape((rows, LANES), f32)] * 3,
+        in_specs=[HBM] * 4,
+        out_specs=[VMEM] * 5,
+        scratch_shapes=[pltpu.VMEM((levels, tracers, LANES), f32)] * 2
+        + [pltpu.SemaphoreType.DMA((3, max(3, levels // group)))],
         compiler_params=PARAMS,
         name="pack",
-    )(t, u, n, q)
+    )(*(pltpu.with_memory_space_constraint(x, pltpu.HBM) for x in (t, u, n, q)))
     swap_a = [(i, i ^ 1) for i in range(tile_count)]
     swap_b = [(i, (i + 1) % tile_count if i % 2 else (i - 1) % tile_count) for i in range(tile_count)]
     got_a = lax.ppermute(send_a, "tile", swap_a)
@@ -275,26 +301,22 @@
         out_specs=[VMEM, VMEM],
         compiler_params=PARAMS,
         name="heat",
-    )(t, u, n, got_a, got_b)
+    )(t_near, u_near, n_near, got_a, got_b)
 
     others = [
         lax.ppermute(heat, "lev", [(i, peer(i, s, lev_count)) for i in range(lev_count)])
         for s in range(1, lev_count)
     ]
 
-    block = 5 if levels % 5 == 0 else 1
-    whole = lambda *dims: pl.BlockSpec(dims, lambda i: (0,) * len(dims))
     moved, top = pl.pallas_call(
-        functools.partial(tracer_kernel, block, tracers),
+        functools.partial(tracer_kernel, levels, group, tracers),
         out_shape=[shape((levels, tracers, width), f32), shape((SUB, width), f32)],
-        grid=(levels // block,),
-        in_specs=[
-            pl.BlockSpec((block, tracers, width), lambda i: (i, 0, 0)),
-            whole(5, levels, width),
-            whole(pack_rows, LANES),
-            whole(pack_rows, LANES),
+        in_specs=[VMEM] * 4,
+        out_specs=[HBM, VMEM],
+        scratch_shapes=[
+            pltpu.VMEM((levels, tracers, width), f32),
+            pltpu.SemaphoreType.DMA((levels // group,)),
         ],
-        out_specs=[pl.BlockSpec((block, tracers, width), lambda i: (i, 0, 0)), whole(SUB, width)],
         cost_estimate=pl.CostEstimate(
             flops=9 * levels * tracers * width, bytes_accessed=8 * levels * tracers * width, transcendentals=0
         ),
@@ -340,12 +362,13 @@
     heat_out, q_out = pl.pallas_call(
         functools.partial(final_kernel, levels, tiles, tile_count, sections),
         out_shape=[shape((rows, LANES), f32), shape((levels, tracers, width), f32)],
-        in_specs=[SMEM] + [VMEM] * (5 + tile_count) + [ANY],
-        out_specs=[VMEM, ANY],
+        in_specs=[SMEM] + [VMEM] * (5 + tile_count) + [HBM],
+        out_specs=[HBM, HBM],
         scratch_shapes=[
             pltpu.VMEM((tile_count * tiles * SUB, LANES), f32),
             pltpu.VMEM((SUB, width), f32),
-            pltpu.SemaphoreType.DMA,
+            pltpu.VMEM((rows, LANES), f32),
+            pltpu.SemaphoreType.DMA((2,)),
         ],
         input_output_aliases={6 + tile_count: 1},
         compiler_params=PARAMS,

time: 28.4 us -> 25 us (0.88)
  local copies, waits for them, and re-layouts: 4.39 us -> 0.62 us
  waiting for transfers between devices: 4.2 us -> 4.73 us
    unnamed x24 -> x10, local copies, waits for them, and re-layouts: 3.8 us -> 0.03 us
    pallas_call x2, Pallas kernels: 4.06 us -> 4.75 us  [the longest x1 3.03 us: body(): pl.pallas_call(functools.partial(tracer_kernel, levels, group, tracers),...]
    pallas_call x1, Pallas kernels: 1.43 us -> 0.84 us  [body(): pl.pallas_call(functools.partial(final_kernel, levels, tiles, tile_count,...]
    ppermute x3, waiting for transfers between devices: 0.59 us -> 1.12 us  [body(): lax.ppermute(heat, 'lev', [(i, peer(i, s, lev_count)) for i in range(lev_...]
  transfers between devices with their start and end apart: 9 -> 9, of which waited for: 4 -> 4; matrix products, arithmetic and copies ran while one was open for 2% -> 3% of each run, Pallas kernels for 13% -> 12%
where the time goes in v3:
time: 25 us; the launch traced here: 24.9 us
  starting transfers between devices  12 us (48%)
  Pallas kernels  6.04 us (24%)
  waiting for transfers between devices  4.73 us (19%)
  between operations  1.41 us (6%)
  local copies, waits for them, and re-layouts  0.62 us (2%)
    ppermute x3, starting transfers between devices, body(): lax.ppermute(heat, 'lev', [(i, peer(i, s, lev_count)) for i in range(lev_...  4.45 us
    ppermute x4, starting transfers between devices, body(): lax.ppermute(surface, ('comp', 'tile', 'lev'), [(place(c, i, l), place((c...  4.4 us
    pallas_call x1, Pallas kernels, body(): pl.pallas_call(functools.partial(tracer_kernel, levels, group, tracers),...  3.03 us
    ppermute x1, starting transfers between devices, body(): got_b = lax.ppermute(send_b, 'tile', swap_b)  2.59 us
    ppermute x4, waiting for transfers between devices, body(): lax.ppermute(surface, ('comp', 'tile', 'lev'), [(place(c, i, l), place((c...  2.02 us
    pallas_call x1, Pallas kernels, body(): pl.pallas_call(functools.partial(pack_kernel, levels, tiles, tracers, gro...  1.72 us
    ppermute x1, waiting for transfers between devices, body(): got_b = lax.ppermute(send_b, 'tile', swap_b)  1.59 us
    ppermute x3, waiting for transfers between devices, body(): lax.ppermute(heat, 'lev', [(i, peer(i, s, lev_count)) for i in range(lev_...  1.12 us
  transfers between devices with their start and end apart: 9, of which 4 were waited for; matrix products, arithmetic and copies ran while one was open for 3% of the time, Pallas kernels for 12%

profile of v3, /device:TPU:0, one launch (start us, length us, event | category | flops | bytes accessed | tf_op | source)
XLA Modules:
  0.0 24.9 jit_solution(5562813910758433878)
XLA Ops:
  0.6 0.0 copy-start
  0.6 0.0 copy-start.4
  0.7 1.7 %pack.1 = (f32[64,128]{1,0:T(8,128)S(1)}, f32[64,128]{1,0:T(8,128)S(1)}, f32[80,128]{1,0:T(8,128)S(1)}, f32[80,128]{1,0:T(8,128)S(1)}, f32[80,128]{1,0:T(8,128)S(1)}) custom-call(f32[80,128]{1,0:T(8,128)} %bitcast.29, f32[80,128]{1,0:T(8,128)} %bitcast.30, f32[80,128]{1,0:T(8,128)} %bitcast.31, f32[20,40,512]{2,1,0:T(8,128)} %bitcast.22), custom_call_target="tpu_custom_call" | custom-call | tf_op jit(solution)/shard_map/pack/pallas_call | solution.py:282
  2.4 0.0 copy-start.1
  2.4 0.0 copy-start.2
  2.4 0.0 copy-start.3
  2.4 0.6 %collective-permute-start = (f32[64,128]{1,0:T(8,128)S(1)}, f32[64,128]{1,0:T(8,128)S(1)}, u32[]{:S(2)}, u32[]{:S(2)}) collective-permute-start(f32[64,128]{1,0:T(8,128)S(1)} %get-tuple-element.18), channel_id=1, source_target_pairs={{0,4},{4,0},{8,12},{12,8},{1,5},{5,1},{9,13},{13,9},{2,6},{6,2},{1... | collective-permute-start | bytes 98312 | tf_op jit(solution)/shard_map/ppermute | solution.py:294
  3.0 2.6 %collective-permute-start.1 = (f32[64,128]{1,0:T(8,128)S(1)}, f32[64,128]{1,0:T(8,128)S(1)}, u32[]{:S(2)}, u32[]{:S(2)}) collective-permute-start(f32[64,128]{1,0:T(8,128)S(1)} %get-tuple-element.19), channel_id=1, source_target_pairs={{0,12},{4,8},{8,4},{12,0},{1,13},{5,9},{9,5},{13,1},{2,14},{6,10},... | collective-permute-start | bytes 98312 | tf_op jit(solution)/shard_map/ppermute | solution.py:295
  5.6 0.0 copy-done.4
  5.6 0.1 dynamic-slice_bitcast_fusion.3
  5.7 0.0 collective-permute-done.a_ref
  5.7 1.6 %collective-permute-done.1.b_ref = f32[64,128]{1,0:T(8,128)S(1)} collective-permute-done((f32[64,128]{1,0:T(8,128)S(1)}, f32[64,128]{1,0:T(8,128)S(1)}, u32[]{:S(2)}, u32[]{:S(2)}) %collective-permute-start.1) | collective-permute-done | bytes 32800 | tf_op jit(solution)/shard_map/ppermute | solution.py:295
  7.2 0.2 heat.1
  7.5 3.8 %collective-permute-start.4 = (f32[80,128]{1,0:T(8,128)S(1)}, f32[80,128]{1,0:T(8,128)S(1)}, u32[]{:S(2)}, u32[]{:S(2)}) collective-permute-start(f32[80,128]{1,0:T(8,128)S(1)} %get-tuple-element.20.own_ref), channel_id=1, source_target_pairs={{0,3},{1,2},{2,1},{3,0},{4,7},{5,6},{6,5},{7,4},{8,11},{9,10},{10,... | collective-permute-start | bytes 122888 | tf_op jit(solution)/shard_map/ppermute | solution.py:307
  11.3 0.0 collective-permute-start.3
  11.3 0.7 %collective-permute-start.2 = (f32[80,128]{1,0:T(8,128)S(1)}, f32[80,128]{1,0:T(8,128)S(1)}, u32[]{:S(2)}, u32[]{:S(2)}) collective-permute-start(f32[80,128]{1,0:T(8,128)S(1)} %get-tuple-element.20.own_ref), channel_id=1, source_target_pairs={{0,1},{1,0},{2,3},{3,2},{4,5},{5,4},{6,7},{7,6},{8,9},{9,8},{10,11... | collective-permute-start | bytes 122888 | tf_op jit(solution)/shard_map/ppermute | solution.py:307
  11.9 0.1 pad_maximum_fusion.m_ref
  12.0 3.0 %tracers.1 = (f32[20,40,512]{2,1,0:T(8,128)}, f32[8,512]{1,0:T(8,128)S(1)}) custom-call(f32[20,40,512]{2,1,0:T(8,128)S(1)} %bitcast.23, f32[5,20,512]{2,1,0:T(8,128)S(1)} %get-tuple-element.21.coef_ref, f32[64,128]{1,0:T(8,128)S(1)} %collective-permute-done.a_ref, f32[64,128]{1,0:T(8,128)S(1)} %collective-permute-done.1.b_ref), custom_call_target="tpu_custom_call" | custom-call | flops 3686400 | bytes 3276800 | tf_op jit(solution)/shard_map/tracers/pallas_call | solution.py:311
  15.1 0.0 collective-permute-done.4.refs_2_
  15.1 1.1 %collective-permute-done.3.refs_1_ = f32[80,128]{1,0:T(8,128)S(1)} collective-permute-done((f32[80,128]{1,0:T(8,128)S(1)}, f32[80,128]{1,0:T(8,128)S(1)}, u32[]{:S(2)}, u32[]{:S(2)}) %collective-permute-start.3) | collective-permute-done | bytes 40992 | tf_op jit(solution)/shard_map/ppermute | solution.py:307
  16.2 0.0 collective-permute-done.2.refs_0_
  16.2 0.2 surface.1
  16.4 1.4 %collective-permute-start.8 = (f32[32,128]{1,0:T(8,128)S(1)}, f32[32,128]{1,0:T(8,128)S(1)}, u32[]{:S(2)}, u32[]{:S(2)}) collective-permute-start(f32[32,128]{1,0:T(8,128)S(1)} %get-tuple-element.24), channel_id=1, source_target_pairs={{0,28},{1,29},{2,30},{3,31},{4,24},{5,25},{6,26},{7,27},{8,20},{9,... | collective-permute-start | bytes 49160 | tf_op jit(solution)/shard_map/ppermute | solution.py:346
  17.8 1.1 %collective-permute-start.7 = (f32[32,128]{1,0:T(8,128)S(1)}, f32[32,128]{1,0:T(8,128)S(1)}, u32[]{:S(2)}, u32[]{:S(2)}) collective-permute-start(f32[32,128]{1,0:T(8,128)S(1)} %get-tuple-element.24), channel_id=1, source_target_pairs={{0,24},{1,25},{2,26},{3,27},{4,28},{5,29},{6,30},{7,31},{8,16},{9,... | collective-permute-start | bytes 49160 | tf_op jit(solution)/shard_map/ppermute | solution.py:346
  18.9 1.4 %collective-permute-start.6 = (f32[32,128]{1,0:T(8,128)S(1)}, f32[32,128]{1,0:T(8,128)S(1)}, u32[]{:S(2)}, u32[]{:S(2)}) collective-permute-start(f32[32,128]{1,0:T(8,128)S(1)} %get-tuple-element.24), channel_id=1, source_target_pairs={{0,20},{1,21},{2,22},{3,23},{4,16},{5,17},{6,18},{7,19},{8,28},{9,... | collective-permute-start | bytes 49160 | tf_op jit(solution)/shard_map/ppermute | solution.py:346
  20.3 0.5 %collective-permute-start.5 = (f32[32,128]{1,0:T(8,128)S(1)}, f32[32,128]{1,0:T(8,128)S(1)}, u32[]{:S(2)}, u32[]{:S(2)}) collective-permute-start(f32[32,128]{1,0:T(8,128)S(1)} %get-tuple-element.24), channel_id=1, source_target_pairs={{0,16},{1,17},{2,18},{3,19},{4,20},{5,21},{6,22},{7,23},{8,24},{9,... | collective-permute-start | bytes 49160 | tf_op jit(solution)/shard_map/ppermute | solution.py:346
  20.8 0.5 %slice.4 = s32[1,1]{1,0:T(1,128)} slice(s32[4,512]{1,0:T(4,128)S(1)} %bitcast.24), slice={[0:1], [0:1]} | slice | bytes 8 | tf_op jit(solution)/shard_map/slice | solution.py:361
  22.0 0.0 collective-permute-done.8.refs_3_
  22.0 0.4 %collective-permute-done.7.refs_2_ = f32[32,128]{1,0:T(8,128)S(1)} collective-permute-done((f32[32,128]{1,0:T(8,128)S(1)}, f32[32,128]{1,0:T(8,128)S(1)}, u32[]{:S(2)}, u32[]{:S(2)}) %collective-permute-start.7) | collective-permute-done | bytes 16416 | tf_op jit(solution)/shard_map/ppermute | solution.py:346
  22.4 0.0 collective-permute-done.6.refs_1_
  22.5 1.6 %collective-permute-done.5.refs_0_ = f32[32,128]{1,0:T(8,128)S(1)} collective-permute-done((f32[32,128]{1,0:T(8,128)S(1)}, f32[32,128]{1,0:T(8,128)S(1)}, u32[]{:S(2)}, u32[]{:S(2)}) %collective-permute-start.5) | collective-permute-done | bytes 16416 | tf_op jit(solution)/shard_map/ppermute | solution.py:346
  24.0 0.8 %remap.1 = (f32[80,128]{1,0:T(8,128)}, f32[20,40,512]{2,1,0:T(8,128)}) custom-call(s32[1]{0:T(128)S(6)} %mul.16.first_ref, f32[20,512]{1,0:T(8,128)S(1)} %get-tuple-element.23.mixed_ref, f32[8,512]{1,0:T(8,128)S(1)} %get-tuple-element.22.refs_3_.top_ref, s32[4,512]{1,0:T(4,128)S(1)} %bitcast.25, ...), custom_call_target="tpu_custom_call", output_to_operand_aliasing={{1}: (10, {})} | custom-call | tf_op jit(solution)/shard_map/remap/pallas_call | solution.py:362
  (4 shorter events, 0.0 us)
Async XLA Ops:
  0.6 11.4 %copy-start = (f32[1,40,20,512]{3,1,2,0:T(8,128)S(1)}, f32[1,40,20,512]{3,1,2,0:T(8,128)}, u32[]{:S(2)}) copy-start(f32[1,40,20,512]{3,1,2,0:T(8,128)} %param.10) | copy-start | bytes 4915204
  0.6 4.9 %copy-start.4 = (f32[1,80,80]{2,1,0:T(8,128)S(1)}, f32[1,80,80]{2,1,0:T(8,128)}, u32[]{:S(2)}) copy-start(f32[1,80,80]{2,1,0:T(8,128)} %param.12) | copy-start | bytes 76804
  2.4 18.4 %copy-start.1 = (s32[512,4]{0,1:T(4,128)S(1)}, s32[512,4]{0,1:T(4,128)}, u32[]{:S(2)}) copy-start(s32[512,4]{0,1:T(4,128)} %param.14) | copy-start | bytes 24580
  2.4 21.6 %copy-start.2 = (f32[512,4]{0,1:T(4,128)S(1)}, f32[512,4]{0,1:T(4,128)}, u32[]{:S(2)}) copy-start(f32[512,4]{0,1:T(4,128)} %param.13) | copy-start | bytes 24580
  2.4 21.6 %copy-start.3 = (s32[512]{0:T(512)S(1)}, s32[512]{0:T(512)}, u32[]{:S(2)}) copy-start(s32[512]{0:T(512)} %param.15) | copy-start | bytes 6148
  2.4 3.2 %collective-permute-start = (f32[64,128]{1,0:T(8,128)S(1)}, f32[64,128]{1,0:T(8,128)S(1)}, u32[]{:S(2)}, u32[]{:S(2)}) collective-permute-start(f32[64,128]{1,0:T(8,128)S(1)} %get-tuple-element.18), channel_id=1, source_target_pairs={{0,4},{4,0},{8,12},{12,8},{1,5},{5,1},{9,13},{13,9},{2,6},{6,2},{1... | collective-permute-start | bytes 98312 | tf_op jit(solution)/shard_map/ppermute | solution.py:294
  3.0 4.3 %collective-permute-start.1 = (f32[64,128]{1,0:T(8,128)S(1)}, f32[64,128]{1,0:T(8,128)S(1)}, u32[]{:S(2)}, u32[]{:S(2)}) collective-permute-start(f32[64,128]{1,0:T(8,128)S(1)} %get-tuple-element.19), channel_id=1, source_target_pairs={{0,12},{4,8},{8,4},{12,0},{1,13},{5,9},{9,5},{13,1},{2,14},{6,10},... | collective-permute-start | bytes 98312 | tf_op jit(solution)/shard_map/ppermute | solution.py:295
  7.5 7.6 %collective-permute-start.4 = (f32[80,128]{1,0:T(8,128)S(1)}, f32[80,128]{1,0:T(8,128)S(1)}, u32[]{:S(2)}, u32[]{:S(2)}) collective-permute-start(f32[80,128]{1,0:T(8,128)S(1)} %get-tuple-element.20.own_ref), channel_id=1, source_target_pairs={{0,3},{1,2},{2,1},{3,0},{4,7},{5,6},{6,5},{7,4},{8,11},{9,10},{10,... | collective-permute-start | bytes 122888 | tf_op jit(solution)/shard_map/ppermute | solution.py:307
  11.3 4.9 %collective-permute-start.3 = (f32[80,128]{1,0:T(8,128)S(1)}, f32[80,128]{1,0:T(8,128)S(1)}, u32[]{:S(2)}, u32[]{:S(2)}) collective-permute-start(f32[80,128]{1,0:T(8,128)S(1)} %get-tuple-element.20.own_ref), channel_id=1, source_target_pairs={{0,2},{1,3},{2,0},{3,1},{4,6},{5,7},{6,4},{7,5},{8,10},{9,11},{10,... | collective-permute-start | bytes 122888 | tf_op jit(solution)/shard_map/ppermute | solution.py:307
  11.3 4.9 %collective-permute-start.2 = (f32[80,128]{1,0:T(8,128)S(1)}, f32[80,128]{1,0:T(8,128)S(1)}, u32[]{:S(2)}, u32[]{:S(2)}) collective-permute-start(f32[80,128]{1,0:T(8,128)S(1)} %get-tuple-element.20.own_ref), channel_id=1, source_target_pairs={{0,1},{1,0},{2,3},{3,2},{4,5},{5,4},{6,7},{7,6},{8,9},{9,8},{10,11... | collective-permute-start | bytes 122888 | tf_op jit(solution)/shard_map/ppermute | solution.py:307
  16.4 5.6 %collective-permute-start.8 = (f32[32,128]{1,0:T(8,128)S(1)}, f32[32,128]{1,0:T(8,128)S(1)}, u32[]{:S(2)}, u32[]{:S(2)}) collective-permute-start(f32[32,128]{1,0:T(8,128)S(1)} %get-tuple-element.24), channel_id=1, source_target_pairs={{0,28},{1,29},{2,30},{3,31},{4,24},{5,25},{6,26},{7,27},{8,20},{9,... | collective-permute-start | bytes 49160 | tf_op jit(solution)/shard_map/ppermute | solution.py:346
  17.8 4.6 %collective-permute-start.7 = (f32[32,128]{1,0:T(8,128)S(1)}, f32[32,128]{1,0:T(8,128)S(1)}, u32[]{:S(2)}, u32[]{:S(2)}) collective-permute-start(f32[32,128]{1,0:T(8,128)S(1)} %get-tuple-element.24), channel_id=1, source_target_pairs={{0,24},{1,25},{2,26},{3,27},{4,28},{5,29},{6,30},{7,31},{8,16},{9,... | collective-permute-start | bytes 49160 | tf_op jit(solution)/shard_map/ppermute | solution.py:346
  18.9 3.5 %collective-permute-start.6 = (f32[32,128]{1,0:T(8,128)S(1)}, f32[32,128]{1,0:T(8,128)S(1)}, u32[]{:S(2)}, u32[]{:S(2)}) collective-permute-start(f32[32,128]{1,0:T(8,128)S(1)} %get-tuple-element.24), channel_id=1, source_target_pairs={{0,20},{1,21},{2,22},{3,23},{4,16},{5,17},{6,18},{7,19},{8,28},{9,... | collective-permute-start | bytes 49160 | tf_op jit(solution)/shard_map/ppermute | solution.py:346
  20.3 3.7 %collective-permute-start.5 = (f32[32,128]{1,0:T(8,128)S(1)}, f32[32,128]{1,0:T(8,128)S(1)}, u32[]{:S(2)}, u32[]{:S(2)}) collective-permute-start(f32[32,128]{1,0:T(8,128)S(1)} %get-tuple-element.24), channel_id=1, source_target_pairs={{0,16},{1,17},{2,18},{3,19},{4,20},{5,21},{6,22},{7,23},{8,24},{9,... | collective-permute-start | bytes 49160 | tf_op jit(solution)/shard_map/ppermute | solution.py:346

commit v4 on v3

--- a/solution.py
+++ b/solution.py
@@ -7,27 +7,20 @@
 from jax.experimental.pallas import tpu as pltpu
 from jax.sharding import PartitionSpec as P
 
+
 NFLUX = 4
 LANES = 128
 SUB = 8
 REACH = 128
+T_AT, U_AT, N_AT = LANES - 6, LANES - 4, LANES - 2
 
 VMEM = pl.BlockSpec(memory_space=pltpu.VMEM)
-SMEM = pl.BlockSpec(memory_space=pltpu.SMEM)
 HBM = pl.BlockSpec(memory_space=pltpu.HBM)
 PARAMS = pltpu.CompilerParams(vmem_limit_bytes=8 * 2**20)
 
 
-def padded_rows(n):
-    return -(-n // SUB) * SUB
-
-
 def peer(i, s, n):
     return i ^ s if n & (n - 1) == 0 else (i + s) % n
-
-
-def slot_of(me, other, n):
-    return me ^ other if n & (n - 1) == 0 else lax.rem(me - other + n, n)
 
 
 def source_of(me, s, n):
@@ -82,22 +75,19 @@
     even = lax.rem(lax.axis_index("tile"), 2) == 0
     lane = lane_iota((levels, LANES))
 
-    def small(row, shifts, low):
-        t, u, n = [r[pl.ds(row, levels, stride=tiles), :] for r in (t_ref, u_ref, n_ref)]
-        u = pltpu.roll(u, shifts[0], 1)
-        n = pltpu.roll(n, shifts[1], 1)
-        if low:
-            return jnp.where(lane < 2, t, jnp.where(lane < 4, u, n))
-        return jnp.where(lane >= LANES - 2, t, jnp.where(lane >= LANES - 4, u, n))
+    def small(row, edge):
+        t, u, n = [
+            pltpu.roll(r[pl.ds(row, levels, stride=tiles), :], (at - edge) % LANES, 1)
+            for r, at in ((t_ref, T_AT), (u_ref, U_AT), (n_ref, N_AT))
+        ]
+        return jnp.where(lane < U_AT, t, jnp.where(lane < N_AT, u, n))
 
     for copy in flats:
         copy.wait()
-    small_left = small(0, (2, 4), True)
-    small_right = small(tiles - 1, (LANES - 2, LANES - 4), False)
-    a_ref[pl.ds(tracers, levels), :] = jnp.where(even, small_right, small_left)
-    b_ref[pl.ds(tracers, levels), :] = jnp.where(even, small_left, small_right)
+    fill = jnp.zeros((tracers - levels, LANES), jnp.float32)
+    packed_left = jnp.concatenate([small(0, 0), fill], axis=0)
+    packed_right = jnp.concatenate([small(tiles - 1, LANES - 2), fill], axis=0)
     pair = lane_iota((tracers, LANES)) // 2
-    packed_left = packed_right = jnp.zeros((tracers, LANES), jnp.float32)
     for g, chunk in enumerate(chunks):
         for copy in chunk:
             copy.wait()
@@ -105,20 +95,20 @@
             here = pair == level
             packed_left = jnp.where(here, pltpu.roll(left[level], 2 * level, 1), packed_left)
             packed_right = jnp.where(here, pltpu.roll(right[level], (2 * level + 2) % LANES, 1), packed_right)
-    a_ref[pl.ds(0, tracers), :] = jnp.where(even, packed_right, packed_left)
-    b_ref[pl.ds(0, tracers), :] = jnp.where(even, packed_left, packed_right)
-
-
-def heat_kernel(levels, tiles, tracers, sections, t_ref, u_ref, n_ref, a_ref, b_ref, heat_ref, coef_ref):
+    a_ref[...] = jnp.where(even, packed_right, packed_left)
+    b_ref[...] = jnp.where(even, packed_left, packed_right)
+
+
+def heat_kernel(levels, tiles, sections, t_ref, u_ref, n_ref, a_ref, b_ref, heat_ref, coef_ref):
     even = lax.rem(lax.axis_index("tile"), 2) == 0
     ocean = lax.axis_index("comp") >= sections // 2
     t, u, n = [wide(r, levels, tiles) for r in (t_ref, u_ref, n_ref)]
-    got_a = a_ref[pl.ds(tracers, levels), :]
-    got_b = b_ref[pl.ds(tracers, levels), :]
+    got_a = a_ref[pl.ds(0, levels), :]
+    got_b = b_ref[pl.ds(0, levels), :]
     low = jnp.where(even, got_b, got_a)
     high = jnp.where(even, got_a, got_b)
-    ul1, ul2 = [from_left(u, k, low, LANES - 4) for k in (1, 2)]
-    ur1 = from_right(u, 1, high, 2)
+    ul1, ul2 = [from_left(u, k, low, U_AT) for k in (1, 2)]
+    ur1 = from_right(u, 1, high, U_AT)
     plus = lambda v: jnp.maximum(v, 0.0)
     minus = lambda v: jnp.minimum(v, 0.0)
     a0, b0, c0 = 1.0 - plus(u) + minus(ul1), plus(ul1), -minus(u)
@@ -136,24 +126,37 @@
 
     for k, value in enumerate(composed(a0, b0, c0, am, bm, cm, ap, bp, cp)):
         coef_ref[k] = value
-    nl = from_left(n, 1, low, LANES - 6)
-    nr = from_right(n, 1, high, 4)
+    nl = from_left(n, 1, low, N_AT)
+    nr = from_right(n, 1, high, N_AT)
     e0, e1, e2, e3, e4 = composed(
         a0 - 2.0 * n, b0 + n, c0 + n, am - 2.0 * nl, bm + nl, cm + nl, ap - 2.0 * nr, bp + nr, cp + nr
     )
-    tl1, tl2 = [from_left(t, k, low, LANES - 2) for k in (1, 2)]
-    tr1, tr2 = [from_right(t, k, high, 0) for k in (1, 2)]
+    tl1, tl2 = [from_left(t, k, low, T_AT) for k in (1, 2)]
+    tr1, tr2 = [from_right(t, k, high, T_AT) for k in (1, 2)]
     heat = e0 * t + e1 * tl1 + e2 * tr1 + e3 * tl2 + e4 * tr2
     for tile in range(tiles):
         heat_ref[pl.ds(tile, levels, stride=tiles), :] = heat[:, tile * LANES : (tile + 1) * LANES]
 
 
-def tracer_kernel(levels, group, tracers, q_ref, coef_ref, a_ref, b_ref, out_hbm, top_ref, new_ref, sems):
+def plan(tiles, count, index_ref, first_ref, inner_ref, outer_ref):
+    width = tiles * LANES
+    cells = count * width
+    index = index_ref[...]
+    lane = lane_iota(index.shape)
+    corner = jnp.max(jnp.where(lane_iota((1, LANES)) == 0, index[0:1, :LANES], 0))
+    block = lax.rem(corner + REACH, cells) // width
+    first_ref[...] = jnp.full(first_ref.shape, block * tiles, jnp.int32)
+    at = index - (block * width - REACH) - lane
+    at = jnp.where(at < 0, at + cells, at)
+    at = jnp.where(at >= cells, at - cells, at) + jnp.bitwise_and(lane, LANES - 1)
+    inner_ref[...] = jnp.bitwise_and(at, LANES - 1)
+    outer_ref[...] = jnp.right_shift(at, 7)
+
+
+def advance(levels, group, q_ref, coef_ref, a_ref, b_ref, out_hbm, new_ref, sems, top_ref):
     even = lax.rem(lax.axis_index("tile"), 2) == 0
-    got_a = a_ref[pl.ds(0, tracers), :]
-    got_b = b_ref[pl.ds(0, tracers), :]
-    low = jnp.where(even, got_b, got_a)
-    high = jnp.where(even, got_a, got_b)
+    low = jnp.where(even, b_ref[...], a_ref[...])
+    high = jnp.where(even, a_ref[...], b_ref[...])
     copies = []
     for level in range(levels):
         q = q_ref[level]
@@ -177,6 +180,15 @@
         copy.wait()
 
 
+def tracer_kernel(
+    levels, group, tiles, count,
+    q_ref, coef_ref, a_ref, b_ref, index_ref,
+    out_hbm, top_ref, first_ref, inner_ref, outer_ref, new_ref, sems,
+):
+    plan(tiles, count, index_ref, first_ref, inner_ref, outer_ref)
+    advance(levels, group, q_ref, coef_ref, a_ref, b_ref, out_hbm, new_ref, sems, top_ref)
+
+
 def surface_kernel(levels, tiles, count, m_ref, own_ref, *refs):
     got, (top_ref, mixed_ref, send_ref, whole) = refs[: count - 1], refs[count - 1 :]
     for s, ref in enumerate((own_ref,) + tuple(got)):
@@ -191,24 +203,23 @@
         pltpu.roll(top_ref[...], 1, 0),
     )
     for tile in range(tiles):
-        send_ref[pl.ds(tile * SUB, SUB), :] = fields[:, tile * LANES : (tile + 1) * LANES]
+        send_ref[pl.ds(tile * NFLUX, NFLUX), :] = fields[:NFLUX, tile * LANES : (tile + 1) * LANES]
 
 
 def final_kernel(
-    levels, tiles, count, sections, first_ref, mixed_ref, top_ref, index_ref, weight_ref, water_ref, *refs
+    levels, tiles, count, sections, first_ref, inner_ref, outer_ref, mixed_ref, top_ref, weight_ref, water_ref, *refs
 ):
     got, (q_ref, heat_hbm, out_ref, whole, patch, heat_ref, sems) = refs[:count], refs[count:]
     del q_ref
-    width = tiles * LANES
-    cells = count * width
     here = lax.axis_index("tile")
     sea = jnp.logical_and(
         lax.axis_index("comp") >= sections // 2, lax.axis_index("lev") == 0
     )
-    rows = tiles * SUB
     for s in range(count):
-        whole[pl.ds(pl.multiple_of(source_of(here, s, count) * rows, rows), rows), :] = got[s][...]
-    first = first_ref[0]
+        base = (here ^ s) * tiles * SUB
+        for tile in range(tiles):
+            whole[pl.ds(pl.multiple_of(base + tile * SUB, SUB), NFLUX), :] = got[s][pl.ds(tile * NFLUX, NFLUX), :]
+    first = jnp.max(first_ref[...])
     top = top_ref[...]
     mixed = mixed_ref[...]
     first_row = lax.broadcasted_iota(jnp.int32, (SUB, LANES), 0) == 0
@@ -220,15 +231,10 @@
             block = lax.rem(first + tile + q - 1 + count * tiles, count * tiles)
             windows.append(whole[pl.ds(pl.multiple_of(block * SUB, SUB), SUB), :])
         total = jnp.zeros((SUB, LANES), jnp.float32)
-        start = first * LANES + tile * LANES - REACH
-        for k in range(index_ref.shape[0]):
-            index = jnp.broadcast_to(index_ref[k : k + 1, cut], (SUB, LANES))
+        for k in range(weight_ref.shape[0]):
             weight = jnp.broadcast_to(weight_ref[k : k + 1, cut], (SUB, LANES))
-            at = index - start - lane
-            at = jnp.where(at < 0, at + cells, at)
-            at = jnp.where(at >= cells, at - cells, at) + lane
-            inner = jnp.bitwise_and(at, LANES - 1)
-            outer = jnp.right_shift(at, 7)
+            inner = jnp.broadcast_to(inner_ref[k : k + 1, cut], (SUB, LANES))
+            outer = jnp.broadcast_to(outer_ref[k : k + 1, cut], (SUB, LANES))
             picks = [jnp.take_along_axis(w, inner, axis=1) for w in windows]
             picked = jnp.where(outer == 0, picks[0], jnp.where(outer == 1, picks[1], picks[2]))
             total = total + picked * weight
@@ -254,7 +260,7 @@
         copy.wait()
 
 
-def body(
+def interval(
     sizes,
     thermal_anomaly,
     right_face_transport_ratio,
@@ -277,7 +283,7 @@
     q = jnp.transpose(species_ratios, (0, 2, 1, 3)).reshape(levels, tracers, width)
     lev = lax.axis_index("lev")
 
-    pack_rows = tracers + padded_rows(levels)
+    pack_rows = tracers
     group = 5 if levels % 5 == 0 else 1
     send_a, send_b, t_near, u_near, n_near = pl.pallas_call(
         functools.partial(pack_kernel, levels, tiles, tracers, group),
@@ -295,7 +301,7 @@
     got_b = lax.ppermute(send_b, "tile", swap_b)
 
     heat, coef = pl.pallas_call(
-        functools.partial(heat_kernel, levels, tiles, tracers, sections),
+        functools.partial(heat_kernel, levels, tiles, sections),
         out_shape=[shape((rows, LANES), f32), shape((5, levels, width), f32)],
         in_specs=[VMEM] * 5,
         out_specs=[VMEM, VMEM],
@@ -308,21 +314,27 @@
         for s in range(1, lev_count)
     ]
 
-    moved, top = pl.pallas_call(
-        functools.partial(tracer_kernel, levels, group, tracers),
-        out_shape=[shape((levels, tracers, width), f32), shape((SUB, width), f32)],
-        in_specs=[VMEM] * 4,
-        out_specs=[HBM, VMEM],
-        scratch_shapes=[
-            pltpu.VMEM((levels, tracers, width), f32),
-            pltpu.SemaphoreType.DMA((levels // group,)),
+    index = sky_point_of_entry.T
+    estimate = pl.CostEstimate(
+        flops=9 * levels * tracers * width, bytes_accessed=8 * levels * tracers * width, transcendentals=0
+    )
+    buffers = [pltpu.VMEM((levels, tracers, width), f32), pltpu.SemaphoreType.DMA((levels,))]
+    moved, top, first, inner, outer = pl.pallas_call(
+        functools.partial(tracer_kernel, levels, group, tiles, tile_count),
+        out_shape=[
+            shape((levels, tracers, width), f32),
+            shape((SUB, width), f32),
+            shape((1, LANES), jnp.int32),
+            shape(index.shape, jnp.int32),
+            shape(index.shape, jnp.int32),
         ],
-        cost_estimate=pl.CostEstimate(
-            flops=9 * levels * tracers * width, bytes_accessed=8 * levels * tracers * width, transcendentals=0
-        ),
+        in_specs=[VMEM] * 5,
+        out_specs=[HBM] + [VMEM] * 4,
+        scratch_shapes=buffers,
+        cost_estimate=estimate,
         compiler_params=PARAMS,
         name="tracers",
-    )(q, coef, got_a, got_b)
+    )(q, coef, got_a, got_b, index)
 
     mine = lax.dynamic_slice_in_dim(depth_physics_operator[0], lev * levels, levels, 0)
     columns = [
@@ -332,7 +344,7 @@
     matrix = jnp.concatenate(columns, axis=1)
     mixed, surface = pl.pallas_call(
         functools.partial(surface_kernel, levels, tiles, lev_count),
-        out_shape=[shape((levels, width), f32), shape((tiles * SUB, LANES), f32)],
+        out_shape=[shape((levels, width), f32), shape((tiles * NFLUX, LANES), f32)],
         in_specs=[VMEM] * (lev_count + 2),
         out_specs=[VMEM, VMEM],
         scratch_shapes=[pltpu.VMEM((levels * lev_count, width), f32)],
@@ -342,27 +354,26 @@
 
     half = sections // 2
     place = lambda c, i, l: (c * tile_count + i) * lev_count + l
-    got = [
-        lax.ppermute(
-            surface,
-            ("comp", "tile", "lev"),
-            [
-                (place(c, i, l), place((c + half) % sections, peer(i, s, tile_count), l))
-                for c in range(sections)
-                for i in range(tile_count)
-                for l in range(lev_count)
-            ],
-        )
-        for s in range(tile_count)
-    ]
-
-    index = sky_point_of_entry.T
-    cells = tile_count * width
-    first = ((index[0, 0:1] + REACH) % cells) // width * tiles
+
+    def across(s):
+        pairs = [
+            (place(c, i, l), place((c + half) % sections, i ^ s, l))
+            for c in range(sections)
+            for i in range(tile_count)
+            for l in range(lev_count)
+        ]
+        return lax.ppermute(surface, ("comp", "tile", "lev"), pairs)
+
+    got = [None] * tile_count
+    for s in range(1, tile_count, 2):
+        got[s] = across(s)
+    for s in range(1, tile_count, 2):
+        got[s ^ 1] = lax.ppermute(got[s], "tile", swap_a)
+
     heat_out, q_out = pl.pallas_call(
         functools.partial(final_kernel, levels, tiles, tile_count, sections),
         out_shape=[shape((rows, LANES), f32), shape((levels, tracers, width), f32)],
-        in_specs=[SMEM] + [VMEM] * (5 + tile_count) + [HBM],
+        in_specs=[VMEM] * (7 + tile_count) + [HBM],
         out_specs=[HBM, HBM],
         scratch_shapes=[
             pltpu.VMEM((tile_count * tiles * SUB, LANES), f32),
@@ -370,11 +381,11 @@
             pltpu.VMEM((rows, LANES), f32),
             pltpu.SemaphoreType.DMA((2,)),
         ],
-        input_output_aliases={6 + tile_count: 1},
+        input_output_aliases={7 + tile_count: 1},
         compiler_params=PARAMS,
         name="remap",
     )(
-        first, mixed, top, index, exchange_weight_table.T, water_indicator.reshape(1, width), *got, moved
+        first, inner, outer, mixed, top, exchange_weight_table.T, water_indicator.reshape(1, width), *got, moved
     )
     thermal_anomaly_ending = heat_out.reshape(1, levels, width)
     species_ratios_ending = jnp.transpose(q_out.reshape(1, levels, tracers, width), (0, 2, 1, 3))
@@ -395,5 +406,5 @@
     out_specs = (P("comp", "lev", "tile"), P("comp", None, "lev", "tile"))
     sizes = (mesh.shape["comp"], mesh.shape["tile"], mesh.shape["lev"])
     return jax.shard_map(
-        functools.partial(body, sizes), mesh=mesh, in_specs=in_specs, out_specs=out_specs, check_vma=False
-    )
+        functools.partial(interval, sizes), mesh=mesh, in_specs=in_specs, out_specs=out_specs, check_vma=False
+    )

time: 25 us -> 23.9 us (0.956)
  between operations: 1.41 us -> 0.72 us
  local copies, waits for them, and re-layouts: 0.62 us -> 0.11 us
  starting transfers between devices: 12 us -> 11.6 us
  Pallas kernels: 6.04 us -> 6.42 us
    slice x1 -> x0, local copies, waits for them, and re-layouts: 0.51 us -> none  [body(): first = (index[0, 0:1] + REACH) % cells // width * tiles]
    ppermute x9, starting transfers between devices: 12 us -> 11.6 us  [the longest x3 4.51 us: interval(): lax.ppermute(heat, 'lev', [(i, peer(i, s, lev_count)) for i in range(lev_...]
    pallas_call x5, Pallas kernels: 6.04 us -> 6.42 us  [the longest x1 3.24 us: interval(): pl.pallas_call(functools.partial(tracer_kernel, levels, group, tiles, til...]
  transfers between devices with their start and end apart: 9 -> 9, of which waited for: 4 -> 5; matrix products, arithmetic and copies ran while one was open for 3% -> 1% of each run, Pallas kernels for 12% -> 14%
where the time goes in v4:
time: 23.9 us; the launch traced here: 23.8 us
  starting transfers between devices  11.6 us (49%)
  Pallas kernels  6.42 us (27%)
  waiting for transfers between devices  4.82 us (20%)
  between operations  0.72 us (3%)
    ppermute x3, starting transfers between devices, interval(): lax.ppermute(heat, 'lev', [(i, peer(i, s, lev_count)) for i in range(lev_...  4.51 us
    pallas_call x1, Pallas kernels, interval(): pl.pallas_call(functools.partial(tracer_kernel, levels, group, tiles, til...  3.24 us
    ppermute x2, starting transfers between devices, across(): return lax.ppermute(surface, ('comp', 'tile', 'lev'), pairs)  2.68 us
    ppermute x1, starting transfers between devices, interval(): got_b = lax.ppermute(send_b, 'tile', swap_b)  2.59 us
    pallas_call x1, Pallas kernels, interval(): pl.pallas_call(functools.partial(pack_kernel, levels, tiles, tracers, gro...  1.71 us
    ppermute x2, waiting for transfers between devices, across(): return lax.ppermute(surface, ('comp', 'tile', 'lev'), pairs)  1.69 us
    ppermute x1, waiting for transfers between devices, interval(): got_b = lax.ppermute(send_b, 'tile', swap_b)  1.39 us
    ppermute x2, starting transfers between devices, interval(): got[s ^ 1] = lax.ppermute(got[s], 'tile', swap_a)  1.28 us
  transfers between devices with their start and end apart: 9, of which 5 were waited for; matrix products, arithmetic and copies ran while one was open for 1% of the time, Pallas kernels for 14%

profile of v4, /device:TPU:0, one launch (start us, length us, event | category | flops | bytes accessed | tf_op | source)
XLA Modules:
  0.0 23.8 jit_solution(17253013746442371755)
XLA Ops:
  0.6 0.0 copy-start
  0.6 0.0 copy-start.4
  0.7 0.0 copy-start.1
  0.7 1.7 %pack.1 = (f32[40,128]{1,0:T(8,128)S(1)}, f32[40,128]{1,0:T(8,128)S(1)}, f32[80,128]{1,0:T(8,128)S(1)}, f32[80,128]{1,0:T(8,128)S(1)}, f32[80,128]{1,0:T(8,128)S(1)}) custom-call(f32[80,128]{1,0:T(8,128)} %bitcast.27, f32[80,128]{1,0:T(8,128)} %bitcast.28, f32[80,128]{1,0:T(8,128)} %bitcast.29, f32[20,40,512]{2,1,0:T(8,128)} %bitcast.21), custom_call_target="tpu_custom_call" | custom-call | tf_op jit(solution)/shard_map/pack/pallas_call | solution.py:288
  2.4 0.0 copy-start.2
  2.4 0.0 copy-start.3
  2.4 0.6 %collective-permute-start = (f32[40,128]{1,0:T(8,128)S(1)}, f32[40,128]{1,0:T(8,128)S(1)}, u32[]{:S(2)}, u32[]{:S(2)}) collective-permute-start(f32[40,128]{1,0:T(8,128)S(1)} %get-tuple-element.21), channel_id=1, source_target_pairs={{0,4},{4,0},{8,12},{12,8},{1,5},{5,1},{9,13},{13,9},{2,6},{6,2},{1... | collective-permute-start | bytes 61448 | tf_op jit(solution)/shard_map/ppermute | solution.py:300
  3.0 2.6 %collective-permute-start.1 = (f32[40,128]{1,0:T(8,128)S(1)}, f32[40,128]{1,0:T(8,128)S(1)}, u32[]{:S(2)}, u32[]{:S(2)}) collective-permute-start(f32[40,128]{1,0:T(8,128)S(1)} %get-tuple-element.22), channel_id=1, source_target_pairs={{0,12},{4,8},{8,4},{12,0},{1,13},{5,9},{9,5},{13,1},{2,14},{6,10},... | collective-permute-start | bytes 61448 | tf_op jit(solution)/shard_map/ppermute | solution.py:301
  5.6 0.0 copy-done.4
  5.6 0.1 dynamic-slice_bitcast_fusion.3
  5.6 0.0 collective-permute-done.a_ref
  5.6 1.4 %collective-permute-done.1.b_ref = f32[40,128]{1,0:T(8,128)S(1)} collective-permute-done((f32[40,128]{1,0:T(8,128)S(1)}, f32[40,128]{1,0:T(8,128)S(1)}, u32[]{:S(2)}, u32[]{:S(2)}) %collective-permute-start.1) | collective-permute-done | bytes 20512 | tf_op jit(solution)/shard_map/ppermute | solution.py:301
  7.0 0.2 heat.1
  7.3 3.9 %collective-permute-start.4 = (f32[80,128]{1,0:T(8,128)S(1)}, f32[80,128]{1,0:T(8,128)S(1)}, u32[]{:S(2)}, u32[]{:S(2)}) collective-permute-start(f32[80,128]{1,0:T(8,128)S(1)} %get-tuple-element.27.own_ref), channel_id=1, source_target_pairs={{0,3},{1,2},{2,1},{3,0},{4,7},{5,6},{6,5},{7,4},{8,11},{9,10},{10,... | collective-permute-start | bytes 122888 | tf_op jit(solution)/shard_map/ppermute | solution.py:313
  11.1 0.0 collective-permute-start.3
  11.1 0.6 %collective-permute-start.2 = (f32[80,128]{1,0:T(8,128)S(1)}, f32[80,128]{1,0:T(8,128)S(1)}, u32[]{:S(2)}, u32[]{:S(2)}) collective-permute-start(f32[80,128]{1,0:T(8,128)S(1)} %get-tuple-element.27.own_ref), channel_id=1, source_target_pairs={{0,1},{1,0},{2,3},{3,2},{4,5},{5,4},{6,7},{7,6},{8,9},{9,8},{10,11... | collective-permute-start | bytes 122888 | tf_op jit(solution)/shard_map/ppermute | solution.py:313
  11.8 0.1 pad_maximum_fusion.m_ref
  11.9 0.0 copy-done.1
  11.9 3.2 %tracers.1 = (f32[20,40,512]{2,1,0:T(8,128)}, f32[8,512]{1,0:T(8,128)S(1)}, s32[1,128]{1,0:T(1,128)S(1)}, s32[4,512]{1,0:T(4,128)S(1)}, s32[4,512]{1,0:T(4,128)S(1)}) custom-call(f32[20,40,512]{2,1,0:T(8,128)S(1)} %bitcast.22, f32[5,20,512]{2,1,0:T(8,128)S(1)} %get-tuple-element.23.coef_ref, f32[40,128]{1,0:T(8,128)S(1)} %collective-permute-done.a_ref, ...), custom_call_target="tpu_custom_call" | custom-call | flops 3686400 | bytes 3276800 | tf_op jit(solution)/shard_map/tracers/pallas_call | solution.py:322
  15.1 0.0 collective-permute-done.4.refs_2_
  15.1 0.9 %collective-permute-done.3.refs_1_ = f32[80,128]{1,0:T(8,128)S(1)} collective-permute-done((f32[80,128]{1,0:T(8,128)S(1)}, f32[80,128]{1,0:T(8,128)S(1)}, u32[]{:S(2)}, u32[]{:S(2)}) %collective-permute-start.3) | collective-permute-done | bytes 40992 | tf_op jit(solution)/shard_map/ppermute | solution.py:313
  16.0 0.0 collective-permute-done.2.refs_0_
  16.0 0.2 surface.1
  16.3 1.4 %collective-permute-start.7 = (f32[16,128]{1,0:T(8,128)S(1)}, f32[16,128]{1,0:T(8,128)S(1)}, u32[]{:S(2)}, u32[]{:S(2)}) collective-permute-start(f32[16,128]{1,0:T(8,128)S(1)} %get-tuple-element.30), channel_id=1, source_target_pairs={{0,28},{1,29},{2,30},{3,31},{4,24},{5,25},{6,26},{7,27},{8,20},{9,... | collective-permute-start | bytes 24584 | tf_op jit(solution)/shard_map/ppermute | solution.py:365
  17.7 1.3 %collective-permute-start.5 = (f32[16,128]{1,0:T(8,128)S(1)}, f32[16,128]{1,0:T(8,128)S(1)}, u32[]{:S(2)}, u32[]{:S(2)}) collective-permute-start(f32[16,128]{1,0:T(8,128)S(1)} %get-tuple-element.30), channel_id=1, source_target_pairs={{0,20},{1,21},{2,22},{3,23},{4,16},{5,17},{6,18},{7,19},{8,28},{9,... | collective-permute-start | bytes 24584 | tf_op jit(solution)/shard_map/ppermute | solution.py:365
  18.9 1.3 %collective-permute-done.7.refs_3_ = f32[16,128]{1,0:T(8,128)S(1)} collective-permute-done((f32[16,128]{1,0:T(8,128)S(1)}, f32[16,128]{1,0:T(8,128)S(1)}, u32[]{:S(2)}, u32[]{:S(2)}) %collective-permute-start.7) | collective-permute-done | bytes 8224 | tf_op jit(solution)/shard_map/ppermute | solution.py:365
  20.2 0.1 collective-permute-start.8
  20.4 0.4 %collective-permute-done.5.refs_1_ = f32[16,128]{1,0:T(8,128)S(1)} collective-permute-done((f32[16,128]{1,0:T(8,128)S(1)}, f32[16,128]{1,0:T(8,128)S(1)}, u32[]{:S(2)}, u32[]{:S(2)}) %collective-permute-start.5) | collective-permute-done | bytes 8224 | tf_op jit(solution)/shard_map/ppermute | solution.py:365
  20.7 1.2 %collective-permute-start.6 = (f32[16,128]{1,0:T(8,128)S(1)}, f32[16,128]{1,0:T(8,128)S(1)}, u32[]{:S(2)}, u32[]{:S(2)}) collective-permute-start(f32[16,128]{1,0:T(8,128)S(1)} %collective-permute-done.5.refs_1_), channel_id=1, source_target_pairs={{0,4},{4,0},{8,12},{12,8},{1,5},{5,1},{9,13},{13,9},{2,6},{6,2},{1... | collective-permute-start | bytes 24584 | tf_op jit(solution)/shard_map/ppermute | solution.py:371
  21.9 0.0 collective-permute-done.8.refs_2_
  21.9 0.8 %collective-permute-done.6.refs_0_ = f32[16,128]{1,0:T(8,128)S(1)} collective-permute-done((f32[16,128]{1,0:T(8,128)S(1)}, f32[16,128]{1,0:T(8,128)S(1)}, u32[]{:S(2)}, u32[]{:S(2)}) %collective-permute-start.6) | collective-permute-done | bytes 8224 | tf_op jit(solution)/shard_map/ppermute | solution.py:371
  22.7 1.0 %remap.1 = (f32[80,128]{1,0:T(8,128)}, f32[20,40,512]{2,1,0:T(8,128)}) custom-call(s32[1,128]{1,0:T(1,128)S(1)} %get-tuple-element.24.first_ref, s32[4,512]{1,0:T(4,128)S(1)} %get-tuple-element.25.inner_ref, s32[4,512]{1,0:T(4,128)S(1)} %get-tuple-element.26.outer_ref, f32[20,512]{1,0:T(8,128)S(1)} %get-tuple-element.29.mixed_ref, ...), custom_call_target="tpu_custom_call", output_to_operand_aliasing={{1}: (11, {})} | custom-call | tf_op jit(solution)/shard_map/remap/pallas_call | solution.py:373
  (3 shorter events, 0.0 us)
Async XLA Ops:
  0.6 11.2 %copy-start = (f32[1,40,20,512]{3,1,2,0:T(8,128)S(1)}, f32[1,40,20,512]{3,1,2,0:T(8,128)}, u32[]{:S(2)}) copy-start(f32[1,40,20,512]{3,1,2,0:T(8,128)} %param.10) | copy-start | bytes 4915204
  0.6 4.9 %copy-start.4 = (f32[1,80,80]{2,1,0:T(8,128)S(1)}, f32[1,80,80]{2,1,0:T(8,128)}, u32[]{:S(2)}) copy-start(f32[1,80,80]{2,1,0:T(8,128)} %param.12) | copy-start | bytes 76804
  0.7 11.2 %copy-start.1 = (s32[512,4]{0,1:T(4,128)S(1)}, s32[512,4]{0,1:T(4,128)}, u32[]{:S(2)}) copy-start(s32[512,4]{0,1:T(4,128)} %param.14) | copy-start | bytes 24580
  2.4 20.4 %copy-start.2 = (f32[512,4]{0,1:T(4,128)S(1)}, f32[512,4]{0,1:T(4,128)}, u32[]{:S(2)}) copy-start(f32[512,4]{0,1:T(4,128)} %param.13) | copy-start | bytes 24580
  2.4 20.3 %copy-start.3 = (s32[512]{0:T(512)S(1)}, s32[512]{0:T(512)}, u32[]{:S(2)}) copy-start(s32[512]{0:T(512)} %param.15) | copy-start | bytes 6148
  2.4 3.2 %collective-permute-start = (f32[40,128]{1,0:T(8,128)S(1)}, f32[40,128]{1,0:T(8,128)S(1)}, u32[]{:S(2)}, u32[]{:S(2)}) collective-permute-start(f32[40,128]{1,0:T(8,128)S(1)} %get-tuple-element.21), channel_id=1, source_target_pairs={{0,4},{4,0},{8,12},{12,8},{1,5},{5,1},{9,13},{13,9},{2,6},{6,2},{1... | collective-permute-start | bytes 61448 | tf_op jit(solution)/shard_map/ppermute | solution.py:300
  3.0 4.1 %collective-permute-start.1 = (f32[40,128]{1,0:T(8,128)S(1)}, f32[40,128]{1,0:T(8,128)S(1)}, u32[]{:S(2)}, u32[]{:S(2)}) collective-permute-start(f32[40,128]{1,0:T(8,128)S(1)} %get-tuple-element.22), channel_id=1, source_target_pairs={{0,12},{4,8},{8,4},{12,0},{1,13},{5,9},{9,5},{13,1},{2,14},{6,10},... | collective-permute-start | bytes 61448 | tf_op jit(solution)/shard_map/ppermute | solution.py:301
  7.3 7.8 %collective-permute-start.4 = (f32[80,128]{1,0:T(8,128)S(1)}, f32[80,128]{1,0:T(8,128)S(1)}, u32[]{:S(2)}, u32[]{:S(2)}) collective-permute-start(f32[80,128]{1,0:T(8,128)S(1)} %get-tuple-element.27.own_ref), channel_id=1, source_target_pairs={{0,3},{1,2},{2,1},{3,0},{4,7},{5,6},{6,5},{7,4},{8,11},{9,10},{10,... | collective-permute-start | bytes 122888 | tf_op jit(solution)/shard_map/ppermute | solution.py:313
  11.1 4.9 %collective-permute-start.3 = (f32[80,128]{1,0:T(8,128)S(1)}, f32[80,128]{1,0:T(8,128)S(1)}, u32[]{:S(2)}, u32[]{:S(2)}) collective-permute-start(f32[80,128]{1,0:T(8,128)S(1)} %get-tuple-element.27.own_ref), channel_id=1, source_target_pairs={{0,2},{1,3},{2,0},{3,1},{4,6},{5,7},{6,4},{7,5},{8,10},{9,11},{10,... | collective-permute-start | bytes 122888 | tf_op jit(solution)/shard_map/ppermute | solution.py:313
  11.1 4.9 %collective-permute-start.2 = (f32[80,128]{1,0:T(8,128)S(1)}, f32[80,128]{1,0:T(8,128)S(1)}, u32[]{:S(2)}, u32[]{:S(2)}) collective-permute-start(f32[80,128]{1,0:T(8,128)S(1)} %get-tuple-element.27.own_ref), channel_id=1, source_target_pairs={{0,1},{1,0},{2,3},{3,2},{4,5},{5,4},{6,7},{7,6},{8,9},{9,8},{10,11... | collective-permute-start | bytes 122888 | tf_op jit(solution)/shard_map/ppermute | solution.py:313
  16.3 4.0 %collective-permute-start.7 = (f32[16,128]{1,0:T(8,128)S(1)}, f32[16,128]{1,0:T(8,128)S(1)}, u32[]{:S(2)}, u32[]{:S(2)}) collective-permute-start(f32[16,128]{1,0:T(8,128)S(1)} %get-tuple-element.30), channel_id=1, source_target_pairs={{0,28},{1,29},{2,30},{3,31},{4,24},{5,25},{6,26},{7,27},{8,20},{9,... | collective-permute-start | bytes 24584 | tf_op jit(solution)/shard_map/ppermute | solution.py:365
  17.7 3.1 %collective-permute-start.5 = (f32[16,128]{1,0:T(8,128)S(1)}, f32[16,128]{1,0:T(8,128)S(1)}, u32[]{:S(2)}, u32[]{:S(2)}) collective-permute-start(f32[16,128]{1,0:T(8,128)S(1)} %get-tuple-element.30), channel_id=1, source_target_pairs={{0,20},{1,21},{2,22},{3,23},{4,16},{5,17},{6,18},{7,19},{8,28},{9,... | collective-permute-start | bytes 24584 | tf_op jit(solution)/shard_map/ppermute | solution.py:365
  20.2 1.7 %collective-permute-start.8 = (f32[16,128]{1,0:T(8,128)S(1)}, f32[16,128]{1,0:T(8,128)S(1)}, u32[]{:S(2)}, u32[]{:S(2)}) collective-permute-start(f32[16,128]{1,0:T(8,128)S(1)} %collective-permute-done.7.refs_3_), channel_id=1, source_target_pairs={{0,4},{4,0},{8,12},{12,8},{1,5},{5,1},{9,13},{13,9},{2,6},{6,2},{1... | collective-permute-start | bytes 24584 | tf_op jit(solution)/shard_map/ppermute | solution.py:371
  20.7 2.0 %collective-permute-start.6 = (f32[16,128]{1,0:T(8,128)S(1)}, f32[16,128]{1,0:T(8,128)S(1)}, u32[]{:S(2)}, u32[]{:S(2)}) collective-permute-start(f32[16,128]{1,0:T(8,128)S(1)} %collective-permute-done.5.refs_1_), channel_id=1, source_target_pairs={{0,4},{4,0},{8,12},{12,8},{1,5},{5,1},{9,13},{13,9},{2,6},{6,2},{1... | collective-permute-start | bytes 24584 | tf_op jit(solution)/shard_map/ppermute | solution.py:371

commit v5 on v4

--- a/solution.py
+++ b/solution.py
@@ -50,44 +50,54 @@
     return jnp.concatenate([moved[:, : width - LANES], tail], axis=1)
 
 
-def pack_kernel(
-    levels, tiles, tracers, group, t_hbm, u_hbm, n_hbm, q_hbm, a_ref, b_ref, t_ref, u_ref, n_ref, left, right, sems
+def edge_kernel(
+    levels, tiles, t_hbm, u_hbm, n_hbm, q_hbm, a_ref, b_ref, t_ref, u_ref, n_ref, top_ref, sems
 ):
+    copies = [
+        pltpu.make_async_copy(source, target, sems.at[i])
+        for i, (source, target) in enumerate(
+            ((t_hbm, t_ref), (u_hbm, u_ref), (n_hbm, n_ref), (q_hbm.at[0, pl.ds(0, SUB), :], top_ref))
+        )
+    ]
+    for copy in copies:
+        copy.start()
+    even = lax.rem(lax.axis_index("tile"), 2) == 0
+    lane = lane_iota((levels, LANES))
+
+    def small(tile, edge):
+        t, u, n = [
+            pltpu.roll(r[pl.ds(tile, levels, stride=tiles), :], (at - edge) % LANES, 1)
+            for r, at in ((t_ref, T_AT), (u_ref, U_AT), (n_ref, N_AT))
+        ]
+        top = pltpu.roll(top_ref[:, tile * LANES : (tile + 1) * LANES], -edge % LANES, 1)
+        top = jnp.concatenate([top, jnp.zeros((levels - SUB, LANES), jnp.float32)], axis=0)
+        return jnp.where(lane < 2, top, jnp.where(lane < U_AT, t, jnp.where(lane < N_AT, u, n)))
+
+    for copy in copies:
+        copy.wait()
+    left = small(0, 0)
+    right = small(tiles - 1, LANES - 2)
+    a_ref[...] = jnp.where(even, right, left)
+    b_ref[...] = jnp.where(even, left, right)
+
+
+def pack_kernel(levels, tiles, group, q_hbm, a_ref, b_ref, left, right, sems):
     width = tiles * LANES
-    flats = [
-        pltpu.make_async_copy(source, target, sems.at[0, i])
-        for i, (source, target) in enumerate(((t_hbm, t_ref), (u_hbm, u_ref), (n_hbm, n_ref)))
-    ]
     chunks = []
     for g in range(levels // group):
         cut = pl.ds(g * group, group)
         chunks.append(
             [
-                pltpu.make_async_copy(q_hbm.at[cut, :, pl.ds(0, LANES)], left.at[cut], sems.at[1, g]),
-                pltpu.make_async_copy(q_hbm.at[cut, :, pl.ds(width - LANES, LANES)], right.at[cut], sems.at[2, g]),
+                pltpu.make_async_copy(q_hbm.at[cut, :, pl.ds(0, LANES)], left.at[cut], sems.at[0, g]),
+                pltpu.make_async_copy(q_hbm.at[cut, :, pl.ds(width - LANES, LANES)], right.at[cut], sems.at[1, g]),
             ]
         )
-    for copy in flats:
-        copy.start()
-    for chunk in chunks:
-        for copy in chunk:
+        for copy in chunks[-1]:
             copy.start()
     even = lax.rem(lax.axis_index("tile"), 2) == 0
-    lane = lane_iota((levels, LANES))
-
-    def small(row, edge):
-        t, u, n = [
-            pltpu.roll(r[pl.ds(row, levels, stride=tiles), :], (at - edge) % LANES, 1)
-            for r, at in ((t_ref, T_AT), (u_ref, U_AT), (n_ref, N_AT))
-        ]
-        return jnp.where(lane < U_AT, t, jnp.where(lane < N_AT, u, n))
-
-    for copy in flats:
-        copy.wait()
-    fill = jnp.zeros((tracers - levels, LANES), jnp.float32)
-    packed_left = jnp.concatenate([small(0, 0), fill], axis=0)
-    packed_right = jnp.concatenate([small(tiles - 1, LANES - 2), fill], axis=0)
+    tracers = a_ref.shape[0]
     pair = lane_iota((tracers, LANES)) // 2
+    packed_left = packed_right = jnp.zeros((tracers, LANES), jnp.float32)
     for g, chunk in enumerate(chunks):
         for copy in chunk:
             copy.wait()
@@ -99,14 +109,12 @@
     b_ref[...] = jnp.where(even, packed_left, packed_right)
 
 
-def heat_kernel(levels, tiles, sections, t_ref, u_ref, n_ref, a_ref, b_ref, heat_ref, coef_ref):
+def heat_kernel(levels, tiles, sections, t_ref, u_ref, n_ref, near_ref, a_ref, b_ref, heat_ref, coef_ref, top_ref):
     even = lax.rem(lax.axis_index("tile"), 2) == 0
     ocean = lax.axis_index("comp") >= sections // 2
     t, u, n = [wide(r, levels, tiles) for r in (t_ref, u_ref, n_ref)]
-    got_a = a_ref[pl.ds(0, levels), :]
-    got_b = b_ref[pl.ds(0, levels), :]
-    low = jnp.where(even, got_b, got_a)
-    high = jnp.where(even, got_a, got_b)
+    low = jnp.where(even, b_ref[...], a_ref[...])
+    high = jnp.where(even, a_ref[...], b_ref[...])
     ul1, ul2 = [from_left(u, k, low, U_AT) for k in (1, 2)]
     ur1 = from_right(u, 1, high, U_AT)
     plus = lambda v: jnp.maximum(v, 0.0)
@@ -124,8 +132,19 @@
             jnp.where(ocean, 0.0, c0 * cp),
         )
 
-    for k, value in enumerate(composed(a0, b0, c0, am, bm, cm, ap, bp, cp)):
+    shared = composed(a0, b0, c0, am, bm, cm, ap, bp, cp)
+    for k, value in enumerate(shared):
         coef_ref[k] = value
+    q = near_ref[...]
+    f0, f1, f2, f3, f4 = [value[0:1] for value in shared]
+    top_low, top_high = low[:SUB], high[:SUB]
+    top_ref[...] = (
+        f0 * q
+        + f1 * from_left(q, 1, top_low, 0)
+        + f2 * from_right(q, 1, top_high, 0)
+        + f3 * from_left(q, 2, top_low, 0)
+        + f4 * from_right(q, 2, top_high, 0)
+    )
     nl = from_left(n, 1, low, N_AT)
     nr = from_right(n, 1, high, N_AT)
     e0, e1, e2, e3, e4 = composed(
@@ -153,40 +172,49 @@
     outer_ref[...] = jnp.right_shift(at, 7)
 
 
-def advance(levels, group, q_ref, coef_ref, a_ref, b_ref, out_hbm, new_ref, sems, top_ref):
+def inner_kernel(
+    levels, tiles, count, q_ref, coef_ref, index_ref, new_ref, first_ref, inner_ref, outer_ref
+):
+    plan(tiles, count, index_ref, first_ref, inner_ref, outer_ref)
+    none = jnp.zeros((q_ref.shape[1], LANES), jnp.float32)
+    for level in range(levels):
+        q = q_ref[level]
+        e0, e1, e2, e3, e4 = [coef_ref[k, level : level + 1, :] for k in range(5)]
+        new_ref[level] = (
+            e0 * q
+            + e1 * from_left(q, 1, none, 0)
+            + e2 * from_right(q, 1, none, 0)
+            + e3 * from_left(q, 2, none, 0)
+            + e4 * from_right(q, 2, none, 0)
+        )
+
+
+def outer_kernel(levels, tiles, group, part_ref, coef_ref, a_ref, b_ref, after_ref, out_hbm, new_ref, sems):
+    del after_ref
     even = lax.rem(lax.axis_index("tile"), 2) == 0
     low = jnp.where(even, b_ref[...], a_ref[...])
     high = jnp.where(even, a_ref[...], b_ref[...])
+    lane = lane_iota(low.shape)
+    head, last = slice(0, LANES), slice((tiles - 1) * LANES, tiles * LANES)
     copies = []
     for level in range(levels):
-        q = q_ref[level]
-        place = 2 * level
-        e0, e1, e2, e3, e4 = [coef_ref[k, level : level + 1, :] for k in range(5)]
-        new = (
-            e0 * q
-            + e1 * from_left(q, 1, low, place)
-            + e2 * from_right(q, 1, high, place)
-            + e3 * from_left(q, 2, low, place)
-            + e4 * from_right(q, 2, high, place)
-        )
-        new_ref[level] = new
-        if level == 0:
-            top_ref[...] = new[:SUB]
+        new_ref[level] = part_ref[level]
+        added = jnp.zeros(low.shape, jnp.float32)
+        for k, e in ((1, 1), (2, 3)):
+            halo = pltpu.roll(low, (k - 2 * level - 2) % LANES, 1)
+            added = added + coef_ref[e, level : level + 1, head] * jnp.where(lane < k, halo, 0.0)
+        new_ref[level, :, head] = part_ref[level, :, head] + added
+        added = jnp.zeros(low.shape, jnp.float32)
+        for k, e in ((1, 2), (2, 4)):
+            halo = pltpu.roll(high, (-k - 2 * level) % LANES, 1)
+            added = added + coef_ref[e, level : level + 1, last] * jnp.where(lane >= LANES - k, halo, 0.0)
+        new_ref[level, :, last] = (new_ref if tiles == 1 else part_ref)[level, :, last] + added
         if level % group == group - 1:
             cut = pl.ds(level - group + 1, group)
             copies.append(pltpu.make_async_copy(new_ref.at[cut], out_hbm.at[cut], sems.at[level // group]))
             copies[-1].start()
     for copy in copies:
         copy.wait()
-
-
-def tracer_kernel(
-    levels, group, tiles, count,
-    q_ref, coef_ref, a_ref, b_ref, index_ref,
-    out_hbm, top_ref, first_ref, inner_ref, outer_ref, new_ref, sems,
-):
-    plan(tiles, count, index_ref, first_ref, inner_ref, outer_ref)
-    advance(levels, group, q_ref, coef_ref, a_ref, b_ref, out_hbm, new_ref, sems, top_ref)
 
 
 def surface_kernel(levels, tiles, count, m_ref, own_ref, *refs):
@@ -283,31 +311,43 @@
     q = jnp.transpose(species_ratios, (0, 2, 1, 3)).reshape(levels, tracers, width)
     lev = lax.axis_index("lev")
 
-    pack_rows = tracers
     group = 5 if levels % 5 == 0 else 1
-    send_a, send_b, t_near, u_near, n_near = pl.pallas_call(
-        functools.partial(pack_kernel, levels, tiles, tracers, group),
-        out_shape=[shape((pack_rows, LANES), f32)] * 2 + [shape((rows, LANES), f32)] * 3,
+    send_a, send_b, t_near, u_near, n_near, q_near = pl.pallas_call(
+        functools.partial(edge_kernel, levels, tiles),
+        out_shape=[shape((levels, LANES), f32)] * 2 + [shape((rows, LANES), f32)] * 3 + [shape((SUB, width), f32)],
         in_specs=[HBM] * 4,
-        out_specs=[VMEM] * 5,
-        scratch_shapes=[pltpu.VMEM((levels, tracers, LANES), f32)] * 2
-        + [pltpu.SemaphoreType.DMA((3, max(3, levels // group)))],
-        compiler_params=PARAMS,
-        name="pack",
+        out_specs=[VMEM] * 6,
+        scratch_shapes=[pltpu.SemaphoreType.DMA((4,))],
+        compiler_params=PARAMS,
+        name="edges",
     )(*(pltpu.with_memory_space_constraint(x, pltpu.HBM) for x in (t, u, n, q)))
     swap_a = [(i, i ^ 1) for i in range(tile_count)]
     swap_b = [(i, (i + 1) % tile_count if i % 2 else (i - 1) % tile_count) for i in range(tile_count)]
     got_a = lax.ppermute(send_a, "tile", swap_a)
     got_b = lax.ppermute(send_b, "tile", swap_b)
-
-    heat, coef = pl.pallas_call(
+    pack = pl.pallas_call(
+        functools.partial(pack_kernel, levels, tiles, group),
+        out_shape=[shape((tracers, LANES), f32)] * 2,
+        in_specs=[HBM],
+        out_specs=[VMEM, VMEM],
+        scratch_shapes=[pltpu.VMEM((levels, tracers, LANES), f32)] * 2
+        + [pltpu.SemaphoreType.DMA((2, levels // group))],
+        compiler_params=PARAMS,
+        name="pack",
+    )
+    side_a, side_b = pack(pltpu.with_memory_space_constraint(q, pltpu.HBM))
+    got_side_a = lax.ppermute(side_a, "tile", swap_a)
+    got_side_b = lax.ppermute(side_b, "tile", swap_b)
+
+    heating = pl.pallas_call(
         functools.partial(heat_kernel, levels, tiles, sections),
-        out_shape=[shape((rows, LANES), f32), shape((5, levels, width), f32)],
-        in_specs=[VMEM] * 5,
-        out_specs=[VMEM, VMEM],
+        out_shape=[shape((rows, LANES), f32), shape((5, levels, width), f32), shape((SUB, width), f32)],
+        in_specs=[VMEM] * 6,
+        out_specs=[VMEM] * 3,
         compiler_params=PARAMS,
         name="heat",
-    )(t_near, u_near, n_near, got_a, got_b)
+    )
+    heat, coef, top = heating(t_near, u_near, n_near, q_near, got_a, got_b)
 
     others = [
         lax.ppermute(heat, "lev", [(i, peer(i, s, lev_count)) for i in range(lev_count)])
@@ -316,25 +356,23 @@
 
     index = sky_point_of_entry.T
     estimate = pl.CostEstimate(
-        flops=9 * levels * tracers * width, bytes_accessed=8 * levels * tracers * width, transcendentals=0
-    )
-    buffers = [pltpu.VMEM((levels, tracers, width), f32), pltpu.SemaphoreType.DMA((levels,))]
-    moved, top, first, inner, outer = pl.pallas_call(
-        functools.partial(tracer_kernel, levels, group, tiles, tile_count),
+        flops=9 * levels * tracers * width, bytes_accessed=4 * levels * tracers * width, transcendentals=0
+    )
+    inside = pl.pallas_call(
+        functools.partial(inner_kernel, levels, tiles, tile_count),
         out_shape=[
             shape((levels, tracers, width), f32),
-            shape((SUB, width), f32),
             shape((1, LANES), jnp.int32),
             shape(index.shape, jnp.int32),
             shape(index.shape, jnp.int32),
         ],
-        in_specs=[VMEM] * 5,
-        out_specs=[HBM] + [VMEM] * 4,
-        scratch_shapes=buffers,
+        in_specs=[VMEM] * 3,
+        out_specs=[VMEM] * 4,
         cost_estimate=estimate,
         compiler_params=PARAMS,
-        name="tracers",
-    )(q, coef, got_a, got_b, index)
+        name="inside",
+    )
+    part, first, inner, outer = inside(q, coef, index)
 
     mine = lax.dynamic_slice_in_dim(depth_physics_operator[0], lev * levels, levels, 0)
     columns = [
@@ -370,6 +408,18 @@
     for s in range(1, tile_count, 2):
         got[s ^ 1] = lax.ppermute(got[s], "tile", swap_a)
 
+    finish = pl.pallas_call(
+        functools.partial(outer_kernel, levels, tiles, group),
+        out_shape=shape((levels, tracers, width), f32),
+        in_specs=[VMEM] * 5,
+        out_specs=HBM,
+        scratch_shapes=[pltpu.VMEM((levels, tracers, width), f32), pltpu.SemaphoreType.DMA((levels // group,))],
+        cost_estimate=estimate,
+        compiler_params=PARAMS,
+        name="finish",
+    )
+    moved = finish(part, coef, got_side_a, got_side_b, mixed)
+
     heat_out, q_out = pl.pallas_call(
         functools.partial(final_kernel, levels, tiles, tile_count, sections),
         out_shape=[shape((rows, LANES), f32), shape((levels, tracers, width), f32)],

time: 23.9 us -> 28 us (1.17)
  waiting for transfers between devices: 4.82 us -> 6.98 us
  Pallas kernels: 6.42 us -> 7.33 us
  starting transfers between devices: 11.6 us -> 12.5 us
    ppermute x3, waiting for transfers between devices: 0.92 us -> 5.71 us  [interval(): lax.ppermute(heat, 'lev', [(i, peer(i, s, lev_count)) for i in range(lev_...]
    ppermute x1, waiting for transfers between devices: 1.39 us -> 0.01 us  [interval(): got_b = lax.ppermute(send_b, 'tile', swap_b)]
    pallas_call x3 -> x5, Pallas kernels: 5.18 us -> 6.08 us  [the longest x1 1.9 us: interval(): part, first, inner, outer = inside(q, coef, index)]
    ppermute x2, waiting for transfers between devices: 0.83 us -> 0.01 us  [interval(): got[s ^ 1] = lax.ppermute(got[s], 'tile', swap_a)]
    ppermute x2, waiting for transfers between devices: 1.69 us -> 1.25 us  [across(): return lax.ppermute(surface, ('comp', 'tile', 'lev'), pairs)]
    ppermute x2, starting transfers between devices: 1.28 us -> 1.68 us  [interval(): got[s ^ 1] = lax.ppermute(got[s], 'tile', swap_a)]
  transfers between devices with their start and end apart: 9 -> 11, of which waited for: 5 -> 4; matrix products, arithmetic and copies ran while one was open for 1% -> 1% of each run, Pallas kernels for 14% -> 19%
where the time goes in v5:
time: 28 us; the launch traced here: 27.7 us
  starting transfers between devices  12.5 us (45%)
  Pallas kernels  7.33 us (26%)
  waiting for transfers between devices  6.98 us (25%)
  between operations  0.79 us (3%)
    ppermute x3, waiting for transfers between devices, interval(): lax.ppermute(heat, 'lev', [(i, peer(i, s, lev_count)) for i in range(lev_...  5.71 us
    ppermute x3, starting transfers between devices, interval(): lax.ppermute(heat, 'lev', [(i, peer(i, s, lev_count)) for i in range(lev_...  4.73 us
    ppermute x2, starting transfers between devices, across(): return lax.ppermute(surface, ('comp', 'tile', 'lev'), pairs)  2.68 us
    ppermute x1, starting transfers between devices, interval(): got_b = lax.ppermute(send_b, 'tile', swap_b)  2.59 us
    pallas_call x1, Pallas kernels, interval(): part, first, inner, outer = inside(q, coef, index)  1.9 us
    ppermute x2, starting transfers between devices, interval(): got[s ^ 1] = lax.ppermute(got[s], 'tile', swap_a)  1.68 us
    pallas_call x1, Pallas kernels, interval(): side_a, side_b = pack(pltpu.with_memory_space_constraint(q, pltpu.HBM))  1.5 us
    pallas_call x1, Pallas kernels, interval(): moved = finish(part, coef, got_side_a, got_side_b, mixed)  1.38 us
  transfers between devices with their start and end apart: 11, of which 4 were waited for; matrix products, arithmetic and copies ran while one was open for 1% of the time, Pallas kernels for 19%

profile of v5, /device:TPU:0, one launch (start us, length us, event | category | flops | bytes accessed | tf_op | source)
XLA Modules:
  0.0 27.7 jit_solution(8963947325021066849)
XLA Ops:
  0.6 0.0 copy-start
  0.7 1.1 %edges.1 = (f32[20,128]{1,0:T(8,128)S(1)}, f32[20,128]{1,0:T(8,128)S(1)}, f32[80,128]{1,0:T(8,128)S(1)}, f32[80,128]{1,0:T(8,128)S(1)}, f32[80,128]{1,0:T(8,128)S(1)}, /*index=5*/f32[8,512]{1,0:T(8,128)S(1)}) custom-call(f32[80,128]{1,0:T(8,128)} %bitcast.28, f32[80,128]{1,0:T(8,128)} %bitcast.29, f32[80,128]{1,0:T(8,128)} %bitcast.30, f32[20,40,512]{2,1,0:T(8,128)} %bitcast.21), custom_call_target="tpu_custom_call" | custom-call | tf_op jit(solution)/shard_map/edges/pallas_call | solution.py:315
  1.7 0.6 %collective-permute-start = (f32[20,128]{1,0:T(8,128)S(1)}, f32[20,128]{1,0:T(8,128)S(1)}, u32[]{:S(2)}, u32[]{:S(2)}) collective-permute-start(f32[20,128]{1,0:T(8,128)S(1)} %get-tuple-element.25), channel_id=1, source_target_pairs={{0,4},{4,0},{8,12},{12,8},{1,5},{5,1},{9,13},{13,9},{2,6},{6,2},{1... | collective-permute-start | bytes 30728 | tf_op jit(solution)/shard_map/ppermute | solution.py:326
  2.3 2.6 %collective-permute-start.1 = (f32[20,128]{1,0:T(8,128)S(1)}, f32[20,128]{1,0:T(8,128)S(1)}, u32[]{:S(2)}, u32[]{:S(2)}) collective-permute-start(f32[20,128]{1,0:T(8,128)S(1)} %get-tuple-element.26), channel_id=1, source_target_pairs={{0,12},{4,8},{8,4},{12,0},{1,13},{5,9},{9,5},{13,1},{2,14},{6,10},... | collective-permute-start | bytes 30728 | tf_op jit(solution)/shard_map/ppermute | solution.py:327
  4.9 1.5 %pack.1 = (f32[40,128]{1,0:T(8,128)S(1)}, f32[40,128]{1,0:T(8,128)S(1)}) custom-call(f32[20,40,512]{2,1,0:T(8,128)} %bitcast.22), custom_call_target="tpu_custom_call" | custom-call | tf_op jit(solution)/shard_map/pack/pallas_call | solution.py:338
  6.4 0.1 collective-permute-start.10
  6.5 0.1 collective-permute-start.9
  6.6 0.1 dynamic-slice_bitcast_fusion.3
  6.7 0.0 collective-permute-done.a_ref
  6.7 0.0 collective-permute-done.1.b_ref
  6.7 0.2 heat.1
  7.0 2.1 %collective-permute-start.2 = (f32[80,128]{1,0:T(8,128)S(1)}, f32[80,128]{1,0:T(8,128)S(1)}, u32[]{:S(2)}, u32[]{:S(2)}) collective-permute-start(f32[80,128]{1,0:T(8,128)S(1)} %get-tuple-element.31.own_ref), channel_id=1, source_target_pairs={{0,1},{1,0},{2,3},{3,2},{4,5},{5,4},{6,7},{7,6},{8,9},{9,8},{10,11... | collective-permute-start | bytes 122888 | tf_op jit(solution)/shard_map/ppermute | solution.py:353
  9.1 2.6 %collective-permute-start.3 = (f32[80,128]{1,0:T(8,128)S(1)}, f32[80,128]{1,0:T(8,128)S(1)}, u32[]{:S(2)}, u32[]{:S(2)}) collective-permute-start(f32[80,128]{1,0:T(8,128)S(1)} %get-tuple-element.31.own_ref), channel_id=1, source_target_pairs={{0,2},{1,3},{2,0},{3,1},{4,6},{5,7},{6,4},{7,5},{8,10},{9,11},{10,... | collective-permute-start | bytes 122888 | tf_op jit(solution)/shard_map/ppermute | solution.py:353
  11.7 0.0 collective-permute-start.4
  11.7 0.1 pad_maximum_fusion.m_ref
  11.8 0.0 collective-permute-done.2.refs_0_
  11.8 3.1 %collective-permute-done.3.refs_1_ = f32[80,128]{1,0:T(8,128)S(1)} collective-permute-done((f32[80,128]{1,0:T(8,128)S(1)}, f32[80,128]{1,0:T(8,128)S(1)}, u32[]{:S(2)}, u32[]{:S(2)}) %collective-permute-start.3) | collective-permute-done | bytes 40992 | tf_op jit(solution)/shard_map/ppermute | solution.py:353
  14.9 2.6 %collective-permute-done.4.refs_2_ = f32[80,128]{1,0:T(8,128)S(1)} collective-permute-done((f32[80,128]{1,0:T(8,128)S(1)}, f32[80,128]{1,0:T(8,128)S(1)}, u32[]{:S(2)}, u32[]{:S(2)}) %collective-permute-start.4) | collective-permute-done | bytes 40992 | tf_op jit(solution)/shard_map/ppermute | solution.py:353
  17.5 0.2 surface.1
  17.7 0.0 collective-permute-start.5
  17.7 2.7 %collective-permute-start.7 = (f32[16,128]{1,0:T(8,128)S(1)}, f32[16,128]{1,0:T(8,128)S(1)}, u32[]{:S(2)}, u32[]{:S(2)}) collective-permute-start(f32[16,128]{1,0:T(8,128)S(1)} %get-tuple-element.34), channel_id=1, source_target_pairs={{0,28},{1,29},{2,30},{3,31},{4,24},{5,25},{6,26},{7,27},{8,20},{9,... | collective-permute-start | bytes 24584 | tf_op jit(solution)/shard_map/ppermute | solution.py:403
  20.4 0.4 %collective-permute-done.5.refs_1_ = f32[16,128]{1,0:T(8,128)S(1)} collective-permute-done((f32[16,128]{1,0:T(8,128)S(1)}, f32[16,128]{1,0:T(8,128)S(1)}, u32[]{:S(2)}, u32[]{:S(2)}) %collective-permute-start.5) | collective-permute-done | bytes 8224 | tf_op jit(solution)/shard_map/ppermute | solution.py:403
  20.8 0.1 collective-permute-start.6
  20.9 0.8 %collective-permute-done.7.refs_3_ = f32[16,128]{1,0:T(8,128)S(1)} collective-permute-done((f32[16,128]{1,0:T(8,128)S(1)}, f32[16,128]{1,0:T(8,128)S(1)}, u32[]{:S(2)}, u32[]{:S(2)}) %collective-permute-start.7) | collective-permute-done | bytes 8224 | tf_op jit(solution)/shard_map/ppermute | solution.py:403
  21.7 1.6 %collective-permute-start.8 = (f32[16,128]{1,0:T(8,128)S(1)}, f32[16,128]{1,0:T(8,128)S(1)}, u32[]{:S(2)}, u32[]{:S(2)}) collective-permute-start(f32[16,128]{1,0:T(8,128)S(1)} %collective-permute-done.7.refs_3_), channel_id=1, source_target_pairs={{0,4},{4,0},{8,12},{12,8},{1,5},{5,1},{9,13},{13,9},{2,6},{6,2},{1... | collective-permute-start | bytes 24584 | tf_op jit(solution)/shard_map/ppermute | solution.py:409
  23.3 1.9 %inside.1 = (f32[20,40,512]{2,1,0:T(8,128)S(1)}, s32[1,128]{1,0:T(1,128)S(1)}, s32[4,512]{1,0:T(4,128)S(1)}, s32[4,512]{1,0:T(4,128)S(1)}) custom-call(f32[20,40,512]{2,1,0:T(8,128)S(1)} %bitcast.23, f32[5,20,512]{2,1,0:T(8,128)S(1)} %get-tuple-element.27.coef_ref, s32[4,512]{1,0:T(4,128)S(1)} %bitcast.25), custom_call_target="tpu_custom_call" | custom-call | flops 3686400 | bytes 1638400 | tf_op jit(solution)/shard_map/inside/pallas_call | solution.py:375
  25.2 0.0 collective-permute-done.10.b_ref
  25.2 0.0 collective-permute-done.9.a_ref
  25.2 0.0 copy-start.1
  25.3 0.0 copy-start.3
  25.3 1.4 %finish.1.refs_4_ = f32[20,40,512]{2,1,0:T(8,128)} custom-call(f32[20,40,512]{2,1,0:T(8,128)S(1)} %get-tuple-element.35.part_ref, f32[5,20,512]{2,1,0:T(8,128)S(1)} %get-tuple-element.27.coef_ref, f32[40,128]{1,0:T(8,128)S(1)} %collective-permute-done.9.a_ref, f32[40,128]{1,0:T(8,128)S(1)} %collective-permute-done.10.b_ref, ...), custom_call_target="tpu_custom_call" | custom-call | flops 3686400 | bytes 1638400 | tf_op jit(solution)/shard_map/finish/pallas_call | solution.py:421
  26.7 1.0 %remap.1 = (f32[80,128]{1,0:T(8,128)}, f32[20,40,512]{2,1,0:T(8,128)}) custom-call(s32[1,128]{1,0:T(1,128)S(1)} %get-tuple-element.28.first_ref, s32[4,512]{1,0:T(4,128)S(1)} %get-tuple-element.29.inner_ref, s32[4,512]{1,0:T(4,128)S(1)} %get-tuple-element.30.outer_ref, ...), custom_call_target="tpu_custom_call", output_to_operand_aliasing={{1}: (11, {})} | custom-call | tf_op jit(solution)/shard_map/remap/pallas_call | solution.py:423
  (9 shorter events, 0.0 us)
Async XLA Ops:
  0.6 6.0 %copy-start.4 = (f32[1,80,80]{2,1,0:T(8,128)S(1)}, f32[1,80,80]{2,1,0:T(8,128)}, u32[]{:S(2)}) copy-start(f32[1,80,80]{2,1,0:T(8,128)} %param.12) | copy-start | bytes 76804
  0.6 22.7 %copy-start = (f32[1,40,20,512]{3,1,2,0:T(8,128)S(1)}, f32[1,40,20,512]{3,1,2,0:T(8,128)}, u32[]{:S(2)}) copy-start(f32[1,40,20,512]{3,1,2,0:T(8,128)} %param.10) | copy-start | bytes 4915204
  0.7 22.7 %copy-start.2 = (s32[512,4]{0,1:T(4,128)S(1)}, s32[512,4]{0,1:T(4,128)}, u32[]{:S(2)}) copy-start(s32[512,4]{0,1:T(4,128)} %param.14) | copy-start | bytes 24580
  1.7 5.0 %collective-permute-start = (f32[20,128]{1,0:T(8,128)S(1)}, f32[20,128]{1,0:T(8,128)S(1)}, u32[]{:S(2)}, u32[]{:S(2)}) collective-permute-start(f32[20,128]{1,0:T(8,128)S(1)} %get-tuple-element.25), channel_id=1, source_target_pairs={{0,4},{4,0},{8,12},{12,8},{1,5},{5,1},{9,13},{13,9},{2,6},{6,2},{1... | collective-permute-start | bytes 30728 | tf_op jit(solution)/shard_map/ppermute | solution.py:326
  2.3 4.4 %collective-permute-start.1 = (f32[20,128]{1,0:T(8,128)S(1)}, f32[20,128]{1,0:T(8,128)S(1)}, u32[]{:S(2)}, u32[]{:S(2)}) collective-permute-start(f32[20,128]{1,0:T(8,128)S(1)} %get-tuple-element.26), channel_id=1, source_target_pairs={{0,12},{4,8},{8,4},{12,0},{1,13},{5,9},{9,5},{13,1},{2,14},{6,10},... | collective-permute-start | bytes 30728 | tf_op jit(solution)/shard_map/ppermute | solution.py:327
  6.4 18.8 %collective-permute-start.10 = (f32[40,128]{1,0:T(8,128)S(1)}, f32[40,128]{1,0:T(8,128)S(1)}, u32[]{:S(2)}, u32[]{:S(2)}) collective-permute-start(f32[40,128]{1,0:T(8,128)S(1)} %get-tuple-element.37), channel_id=1, source_target_pairs={{0,12},{4,8},{8,4},{12,0},{1,13},{5,9},{9,5},{13,1},{2,14},{6,10},... | collective-permute-start | bytes 61448 | tf_op jit(solution)/shard_map/ppermute | solution.py:340
  6.5 18.8 %collective-permute-start.9 = (f32[40,128]{1,0:T(8,128)S(1)}, f32[40,128]{1,0:T(8,128)S(1)}, u32[]{:S(2)}, u32[]{:S(2)}) collective-permute-start(f32[40,128]{1,0:T(8,128)S(1)} %get-tuple-element.36), channel_id=1, source_target_pairs={{0,4},{4,0},{8,12},{12,8},{1,5},{5,1},{9,13},{13,9},{2,6},{6,2},{1... | collective-permute-start | bytes 61448 | tf_op jit(solution)/shard_map/ppermute | solution.py:339
  7.0 4.8 %collective-permute-start.2 = (f32[80,128]{1,0:T(8,128)S(1)}, f32[80,128]{1,0:T(8,128)S(1)}, u32[]{:S(2)}, u32[]{:S(2)}) collective-permute-start(f32[80,128]{1,0:T(8,128)S(1)} %get-tuple-element.31.own_ref), channel_id=1, source_target_pairs={{0,1},{1,0},{2,3},{3,2},{4,5},{5,4},{6,7},{7,6},{8,9},{9,8},{10,11... | collective-permute-start | bytes 122888 | tf_op jit(solution)/shard_map/ppermute | solution.py:353
  9.1 5.8 %collective-permute-start.3 = (f32[80,128]{1,0:T(8,128)S(1)}, f32[80,128]{1,0:T(8,128)S(1)}, u32[]{:S(2)}, u32[]{:S(2)}) collective-permute-start(f32[80,128]{1,0:T(8,128)S(1)} %get-tuple-element.31.own_ref), channel_id=1, source_target_pairs={{0,2},{1,3},{2,0},{3,1},{4,6},{5,7},{6,4},{7,5},{8,10},{9,11},{10,... | collective-permute-start | bytes 122888 | tf_op jit(solution)/shard_map/ppermute | solution.py:353
  11.7 5.8 %collective-permute-start.4 = (f32[80,128]{1,0:T(8,128)S(1)}, f32[80,128]{1,0:T(8,128)S(1)}, u32[]{:S(2)}, u32[]{:S(2)}) collective-permute-start(f32[80,128]{1,0:T(8,128)S(1)} %get-tuple-element.31.own_ref), channel_id=1, source_target_pairs={{0,3},{1,2},{2,1},{3,0},{4,7},{5,6},{6,5},{7,4},{8,11},{9,10},{10,... | collective-permute-start | bytes 122888 | tf_op jit(solution)/shard_map/ppermute | solution.py:353
  17.7 3.1 %collective-permute-start.5 = (f32[16,128]{1,0:T(8,128)S(1)}, f32[16,128]{1,0:T(8,128)S(1)}, u32[]{:S(2)}, u32[]{:S(2)}) collective-permute-start(f32[16,128]{1,0:T(8,128)S(1)} %get-tuple-element.34), channel_id=1, source_target_pairs={{0,20},{1,21},{2,22},{3,23},{4,16},{5,17},{6,18},{7,19},{8,28},{9,... | collective-permute-start | bytes 24584 | tf_op jit(solution)/shard_map/ppermute | solution.py:403
  17.7 4.0 %collective-permute-start.7 = (f32[16,128]{1,0:T(8,128)S(1)}, f32[16,128]{1,0:T(8,128)S(1)}, u32[]{:S(2)}, u32[]{:S(2)}) collective-permute-start(f32[16,128]{1,0:T(8,128)S(1)} %get-tuple-element.34), channel_id=1, source_target_pairs={{0,28},{1,29},{2,30},{3,31},{4,24},{5,25},{6,26},{7,27},{8,20},{9,... | collective-permute-start | bytes 24584 | tf_op jit(solution)/shard_map/ppermute | solution.py:403
  20.8 5.9 %collective-permute-start.6 = (f32[16,128]{1,0:T(8,128)S(1)}, f32[16,128]{1,0:T(8,128)S(1)}, u32[]{:S(2)}, u32[]{:S(2)}) collective-permute-start(f32[16,128]{1,0:T(8,128)S(1)} %collective-permute-done.5.refs_1_), channel_id=1, source_target_pairs={{0,4},{4,0},{8,12},{12,8},{1,5},{5,1},{9,13},{13,9},{2,6},{6,2},{1... | collective-permute-start | bytes 24584 | tf_op jit(solution)/shard_map/ppermute | solution.py:409
  21.7 4.9 %collective-permute-start.8 = (f32[16,128]{1,0:T(8,128)S(1)}, f32[16,128]{1,0:T(8,128)S(1)}, u32[]{:S(2)}, u32[]{:S(2)}) collective-permute-start(f32[16,128]{1,0:T(8,128)S(1)} %collective-permute-done.7.refs_3_), channel_id=1, source_target_pairs={{0,4},{4,0},{8,12},{12,8},{1,5},{5,1},{9,13},{13,9},{2,6},{6,2},{1... | collective-permute-start | bytes 24584 | tf_op jit(solution)/shard_map/ppermute | solution.py:409
  25.2 1.4 %copy-start.1 = (f32[512,4]{0,1:T(4,128)S(1)}, f32[512,4]{0,1:T(4,128)}, u32[]{:S(2)}) copy-start(f32[512,4]{0,1:T(4,128)} %param.13) | copy-start | bytes 24580
  25.3 1.4 %copy-start.3 = (s32[512]{0:T(512)S(1)}, s32[512]{0:T(512)}, u32[]{:S(2)}) copy-start(s32[512]{0:T(512)} %param.15) | copy-start | bytes 6148

commit v6 on v5

--- a/solution.py
+++ b/solution.py
@@ -15,6 +15,7 @@
 T_AT, U_AT, N_AT = LANES - 6, LANES - 4, LANES - 2
 
 VMEM = pl.BlockSpec(memory_space=pltpu.VMEM)
+SMEM = pl.BlockSpec(memory_space=pltpu.SMEM)
 HBM = pl.BlockSpec(memory_space=pltpu.HBM)
 PARAMS = pltpu.CompilerParams(vmem_limit_bytes=8 * 2**20)
 
@@ -157,15 +158,11 @@
         heat_ref[pl.ds(tile, levels, stride=tiles), :] = heat[:, tile * LANES : (tile + 1) * LANES]
 
 
-def plan(tiles, count, index_ref, first_ref, inner_ref, outer_ref):
-    width = tiles * LANES
-    cells = count * width
+def plan(tiles, count, first_ref, index_ref, inner_ref, outer_ref):
+    cells = count * tiles * LANES
     index = index_ref[...]
     lane = lane_iota(index.shape)
-    corner = jnp.max(jnp.where(lane_iota((1, LANES)) == 0, index[0:1, :LANES], 0))
-    block = lax.rem(corner + REACH, cells) // width
-    first_ref[...] = jnp.full(first_ref.shape, block * tiles, jnp.int32)
-    at = index - (block * width - REACH) - lane
+    at = index - (first_ref[0] * LANES - REACH) - lane
     at = jnp.where(at < 0, at + cells, at)
     at = jnp.where(at >= cells, at - cells, at) + jnp.bitwise_and(lane, LANES - 1)
     inner_ref[...] = jnp.bitwise_and(at, LANES - 1)
@@ -173,9 +170,9 @@
 
 
 def inner_kernel(
-    levels, tiles, count, q_ref, coef_ref, index_ref, new_ref, first_ref, inner_ref, outer_ref
+    levels, tiles, count, first_ref, q_ref, coef_ref, index_ref, new_ref, inner_ref, outer_ref
 ):
-    plan(tiles, count, index_ref, first_ref, inner_ref, outer_ref)
+    plan(tiles, count, first_ref, index_ref, inner_ref, outer_ref)
     none = jnp.zeros((q_ref.shape[1], LANES), jnp.float32)
     for level in range(levels):
         q = q_ref[level]
@@ -247,7 +244,7 @@
         base = (here ^ s) * tiles * SUB
         for tile in range(tiles):
             whole[pl.ds(pl.multiple_of(base + tile * SUB, SUB), NFLUX), :] = got[s][pl.ds(tile * NFLUX, NFLUX), :]
-    first = jnp.max(first_ref[...])
+    first = first_ref[0]
     top = top_ref[...]
     mixed = mixed_ref[...]
     first_row = lax.broadcasted_iota(jnp.int32, (SUB, LANES), 0) == 0
@@ -355,6 +352,7 @@
     ]
 
     index = sky_point_of_entry.T
+    first = ((index[0, 0:1] + REACH) % (tile_count * width)) // width * tiles
     estimate = pl.CostEstimate(
         flops=9 * levels * tracers * width, bytes_accessed=4 * levels * tracers * width, transcendentals=0
     )
@@ -362,19 +360,19 @@
         functools.partial(inner_kernel, levels, tiles, tile_count),
         out_shape=[
             shape((levels, tracers, width), f32),
-            shape((1, LANES), jnp.int32),
             shape(index.shape, jnp.int32),
             shape(index.shape, jnp.int32),
         ],
-        in_specs=[VMEM] * 3,
-        out_specs=[VMEM] * 4,
+        in_specs=[SMEM] + [VMEM] * 3,
+        out_specs=[VMEM] * 3,
         cost_estimate=estimate,
         compiler_params=PARAMS,
         name="inside",
     )
-    part, first, inner, outer = inside(q, coef, index)
-
-    mine = lax.dynamic_slice_in_dim(depth_physics_operator[0], lev * levels, levels, 0)
+    part, inner, outer = inside(first, q, coef, index)
+
+    operator, _ = lax.optimization_barrier((depth_physics_operator, heat))
+    mine = lax.dynamic_slice_in_dim(operator[0], lev * levels, levels, 0)
     columns = [
         lax.dynamic_slice_in_dim(mine, source_of(lev, s, lev_count) * levels, levels, 1)
         for s in range(lev_count)
@@ -423,7 +421,7 @@
     heat_out, q_out = pl.pallas_call(
         functools.partial(final_kernel, levels, tiles, tile_count, sections),
         out_shape=[shape((rows, LANES), f32), shape((levels, tracers, width), f32)],
-        in_specs=[VMEM] * (7 + tile_count) + [HBM],
+        in_specs=[SMEM] + [VMEM] * (6 + tile_count) + [HBM],
         out_specs=[HBM, HBM],
         scratch_shapes=[
             pltpu.VMEM((tile_count * tiles * SUB, LANES), f32),

time: 28 us -> 28.8 us (1.029)
  between operations: 0.79 us -> 1.48 us
  local copies, waits for them, and re-layouts: 0.11 us -> 0.62 us
    slice x0 -> x1, local copies, waits for them, and re-layouts: none -> 0.51 us  [interval(): first = (index[0, 0:1] + REACH) % (tile_count * width) // width * tiles]
  transfers between devices with their start and end apart: 11 -> 11, of which waited for: 4 -> 4; matrix products, arithmetic and copies ran while one was open for 1% -> 2% of each run, Pallas kernels for 19% -> 18%
where the time goes in v6:
time: 28.8 us; the launch traced here: 28.6 us
  starting transfers between devices  12.5 us (43%)
  Pallas kernels  7.05 us (24%)
  waiting for transfers between devices  6.89 us (24%)
  between operations  1.48 us (5%)
  local copies, waits for them, and re-layouts  0.62 us (2%)
    ppermute x3, waiting for transfers between devices, interval(): lax.ppermute(heat, 'lev', [(i, peer(i, s, lev_count)) for i in range(lev_...  5.62 us
    ppermute x3, starting transfers between devices, interval(): lax.ppermute(heat, 'lev', [(i, peer(i, s, lev_count)) for i in range(lev_...  4.73 us
    ppermute x2, starting transfers between devices, across(): return lax.ppermute(surface, ('comp', 'tile', 'lev'), pairs)  2.68 us
    ppermute x1, starting transfers between devices, interval(): got_b = lax.ppermute(send_b, 'tile', swap_b)  2.59 us
    pallas_call x1, Pallas kernels, interval(): part, inner, outer = inside(first, q, coef, index)  1.8 us
    ppermute x2, starting transfers between devices, interval(): got[s ^ 1] = lax.ppermute(got[s], 'tile', swap_a)  1.68 us
    pallas_call x1, Pallas kernels, interval(): side_a, side_b = pack(pltpu.with_memory_space_constraint(q, pltpu.HBM))  1.5 us
    pallas_call x1, Pallas kernels, interval(): moved = finish(part, coef, got_side_a, got_side_b, mixed)  1.38 us
  transfers between devices with their start and end apart: 11, of which 4 were waited for; matrix products, arithmetic and copies ran while one was open for 2% of the time, Pallas kernels for 18%

profile of v6, /device:TPU:0, one launch (start us, length us, event | category | flops | bytes accessed | tf_op | source)
XLA Modules:
  0.0 28.6 jit_solution(12960918950293860202)
XLA Ops:
  0.7 0.0 copy-start
  0.7 1.1 %edges.1 = (f32[20,128]{1,0:T(8,128)S(1)}, f32[20,128]{1,0:T(8,128)S(1)}, f32[80,128]{1,0:T(8,128)S(1)}, f32[80,128]{1,0:T(8,128)S(1)}, f32[80,128]{1,0:T(8,128)S(1)}, /*index=5*/f32[8,512]{1,0:T(8,128)S(1)}) custom-call(f32[80,128]{1,0:T(8,128)} %bitcast.30, f32[80,128]{1,0:T(8,128)} %bitcast.31, f32[80,128]{1,0:T(8,128)} %bitcast.32, f32[20,40,512]{2,1,0:T(8,128)} %bitcast.22), custom_call_target="tpu_custom_call" | custom-call | tf_op jit(solution)/shard_map/edges/pallas_call | solution.py:312
  1.7 0.6 %collective-permute-start = (f32[20,128]{1,0:T(8,128)S(1)}, f32[20,128]{1,0:T(8,128)S(1)}, u32[]{:S(2)}, u32[]{:S(2)}) collective-permute-start(f32[20,128]{1,0:T(8,128)S(1)} %get-tuple-element.25), channel_id=1, source_target_pairs={{0,4},{4,0},{8,12},{12,8},{1,5},{5,1},{9,13},{13,9},{2,6},{6,2},{1... | collective-permute-start | bytes 30728 | tf_op jit(solution)/shard_map/ppermute | solution.py:323
  2.3 2.6 %collective-permute-start.1 = (f32[20,128]{1,0:T(8,128)S(1)}, f32[20,128]{1,0:T(8,128)S(1)}, u32[]{:S(2)}, u32[]{:S(2)}) collective-permute-start(f32[20,128]{1,0:T(8,128)S(1)} %get-tuple-element.26), channel_id=1, source_target_pairs={{0,12},{4,8},{8,4},{12,0},{1,13},{5,9},{9,5},{13,1},{2,14},{6,10},... | collective-permute-start | bytes 30728 | tf_op jit(solution)/shard_map/ppermute | solution.py:324
  4.9 1.5 %pack.1 = (f32[40,128]{1,0:T(8,128)S(1)}, f32[40,128]{1,0:T(8,128)S(1)}) custom-call(f32[20,40,512]{2,1,0:T(8,128)} %bitcast.23), custom_call_target="tpu_custom_call" | custom-call | tf_op jit(solution)/shard_map/pack/pallas_call | solution.py:335
  6.4 0.1 collective-permute-start.10
  6.5 0.1 collective-permute-start.9
  6.6 0.0 collective-permute-done.a_ref
  6.6 0.0 collective-permute-done.1.b_ref
  6.6 0.2 heat.1
  6.9 2.1 %collective-permute-start.2 = (f32[80,128]{1,0:T(8,128)S(1)}, f32[80,128]{1,0:T(8,128)S(1)}, u32[]{:S(2)}, u32[]{:S(2)}) collective-permute-start(f32[80,128]{1,0:T(8,128)S(1)} %get-tuple-element.30.own_ref), channel_id=1, source_target_pairs={{0,1},{1,0},{2,3},{3,2},{4,5},{5,4},{6,7},{7,6},{8,9},{9,8},{10,11... | collective-permute-start | bytes 122888 | tf_op jit(solution)/shard_map/ppermute | solution.py:350
  9.0 2.6 %collective-permute-start.3 = (f32[80,128]{1,0:T(8,128)S(1)}, f32[80,128]{1,0:T(8,128)S(1)}, u32[]{:S(2)}, u32[]{:S(2)}) collective-permute-start(f32[80,128]{1,0:T(8,128)S(1)} %get-tuple-element.30.own_ref), channel_id=1, source_target_pairs={{0,2},{1,3},{2,0},{3,1},{4,6},{5,7},{6,4},{7,5},{8,10},{9,11},{10,... | collective-permute-start | bytes 122888 | tf_op jit(solution)/shard_map/ppermute | solution.py:350
  11.6 0.1 dynamic-slice_bitcast_fusion.3
  11.7 0.1 pad_maximum_fusion.m_ref
  11.8 0.0 collective-permute-done.2.refs_0_
  11.8 3.0 %collective-permute-done.3.refs_1_ = f32[80,128]{1,0:T(8,128)S(1)} collective-permute-done((f32[80,128]{1,0:T(8,128)S(1)}, f32[80,128]{1,0:T(8,128)S(1)}, u32[]{:S(2)}, u32[]{:S(2)}) %collective-permute-start.3) | collective-permute-done | bytes 40992 | tf_op jit(solution)/shard_map/ppermute | solution.py:350
  14.8 2.6 %collective-permute-done.4.refs_2_ = f32[80,128]{1,0:T(8,128)S(1)} collective-permute-done((f32[80,128]{1,0:T(8,128)S(1)}, f32[80,128]{1,0:T(8,128)S(1)}, u32[]{:S(2)}, u32[]{:S(2)}) %collective-permute-start.4) | collective-permute-done | bytes 40992 | tf_op jit(solution)/shard_map/ppermute | solution.py:350
  17.4 0.2 surface.1
  17.6 0.0 collective-permute-start.5
  17.6 2.7 %collective-permute-start.7 = (f32[16,128]{1,0:T(8,128)S(1)}, f32[16,128]{1,0:T(8,128)S(1)}, u32[]{:S(2)}, u32[]{:S(2)}) collective-permute-start(f32[16,128]{1,0:T(8,128)S(1)} %get-tuple-element.34), channel_id=1, source_target_pairs={{0,28},{1,29},{2,30},{3,31},{4,24},{5,25},{6,26},{7,27},{8,20},{9,... | collective-permute-start | bytes 24584 | tf_op jit(solution)/shard_map/ppermute | solution.py:401
  20.3 0.4 %collective-permute-done.5.refs_1_ = f32[16,128]{1,0:T(8,128)S(1)} collective-permute-done((f32[16,128]{1,0:T(8,128)S(1)}, f32[16,128]{1,0:T(8,128)S(1)}, u32[]{:S(2)}, u32[]{:S(2)}) %collective-permute-start.5) | collective-permute-done | bytes 8224 | tf_op jit(solution)/shard_map/ppermute | solution.py:401
  20.7 0.1 collective-permute-start.6
  20.8 0.8 %collective-permute-done.7.refs_3_ = f32[16,128]{1,0:T(8,128)S(1)} collective-permute-done((f32[16,128]{1,0:T(8,128)S(1)}, f32[16,128]{1,0:T(8,128)S(1)}, u32[]{:S(2)}, u32[]{:S(2)}) %collective-permute-start.7) | collective-permute-done | bytes 8224 | tf_op jit(solution)/shard_map/ppermute | solution.py:401
  21.7 1.6 %collective-permute-start.8 = (f32[16,128]{1,0:T(8,128)S(1)}, f32[16,128]{1,0:T(8,128)S(1)}, u32[]{:S(2)}, u32[]{:S(2)}) collective-permute-start(f32[16,128]{1,0:T(8,128)S(1)} %collective-permute-done.7.refs_3_), channel_id=1, source_target_pairs={{0,4},{4,0},{8,12},{12,8},{1,5},{5,1},{9,13},{13,9},{2,6},{6,2},{1... | collective-permute-start | bytes 24584 | tf_op jit(solution)/shard_map/ppermute | solution.py:407
  23.2 0.5 %slice.4 = s32[1,1]{1,0:T(1,128)} slice(s32[4,512]{1,0:T(4,128)S(1)} %bitcast.25), slice={[0:1], [0:1]} | slice | bytes 8 | tf_op jit(solution)/shard_map/slice | solution.py:355
  24.4 1.8 %inside.1 = (f32[20,40,512]{2,1,0:T(8,128)S(1)}, s32[4,512]{1,0:T(4,128)S(1)}, s32[4,512]{1,0:T(4,128)S(1)}) custom-call(s32[1]{0:T(128)S(6)} %mul.16.first_ref, f32[20,40,512]{2,1,0:T(8,128)S(1)} %bitcast.24, f32[5,20,512]{2,1,0:T(8,128)S(1)} %get-tuple-element.27.coef_ref, s32[4,512]{1,0:T(4,128)S(1)} %bitcast.26), custom_call_target="tpu_custom_call" | custom-call | flops 3686400 | bytes 1638400 | tf_op jit(solution)/shard_map/inside/pallas_call | solution.py:372
  26.2 0.0 collective-permute-done.10.b_ref
  26.3 0.0 copy-start.2
  26.3 0.0 copy-start.3
  26.3 1.4 %finish.1.refs_4_ = f32[20,40,512]{2,1,0:T(8,128)} custom-call(f32[20,40,512]{2,1,0:T(8,128)S(1)} %get-tuple-element.35.part_ref, f32[5,20,512]{2,1,0:T(8,128)S(1)} %get-tuple-element.27.coef_ref, f32[40,128]{1,0:T(8,128)S(1)} %collective-permute-done.9.a_ref, f32[40,128]{1,0:T(8,128)S(1)} %collective-permute-done.10.b_ref, ...), custom_call_target="tpu_custom_call" | custom-call | flops 3686400 | bytes 1638400 | tf_op jit(solution)/shard_map/finish/pallas_call | solution.py:419
  27.7 0.0 collective-permute-done.6.refs_0_
  27.7 0.8 %remap.1 = (f32[80,128]{1,0:T(8,128)}, f32[20,40,512]{2,1,0:T(8,128)}) custom-call(s32[1]{0:T(128)S(6)} %mul.16.first_ref, s32[4,512]{1,0:T(4,128)S(1)} %get-tuple-element.28.inner_ref, s32[4,512]{1,0:T(4,128)S(1)} %get-tuple-element.29.outer_ref, f32[20,512]{1,0:T(8,128)S(1)} %get-tuple-element.33.after_ref.mixed_ref, ...), custom_call_target="tpu_custom_call", output_to_operand_aliasing={{1}: (11, {})} | custom-call | tf_op jit(solution)/shard_map/remap/pallas_call | solution.py:421
  (10 shorter events, 0.0 us)
Async XLA Ops:
  0.6 11.0 %copy-start.4 = (f32[1,80,80]{2,1,0:T(8,128)S(1)}, f32[1,80,80]{2,1,0:T(8,128)}, u32[]{:S(2)}) copy-start(f32[1,80,80]{2,1,0:T(8,128)} %param.12) | copy-start | bytes 76804
  0.6 22.6 %copy-start.1 = (s32[512,4]{0,1:T(4,128)S(1)}, s32[512,4]{0,1:T(4,128)}, u32[]{:S(2)}) copy-start(s32[512,4]{0,1:T(4,128)} %param.14) | copy-start | bytes 24580
  0.7 23.8 %copy-start = (f32[1,40,20,512]{3,1,2,0:T(8,128)S(1)}, f32[1,40,20,512]{3,1,2,0:T(8,128)}, u32[]{:S(2)}) copy-start(f32[1,40,20,512]{3,1,2,0:T(8,128)} %param.10) | copy-start | bytes 4915204
  1.7 4.9 %collective-permute-start = (f32[20,128]{1,0:T(8,128)S(1)}, f32[20,128]{1,0:T(8,128)S(1)}, u32[]{:S(2)}, u32[]{:S(2)}) collective-permute-start(f32[20,128]{1,0:T(8,128)S(1)} %get-tuple-element.25), channel_id=1, source_target_pairs={{0,4},{4,0},{8,12},{12,8},{1,5},{5,1},{9,13},{13,9},{2,6},{6,2},{1... | collective-permute-start | bytes 30728 | tf_op jit(solution)/shard_map/ppermute | solution.py:323
  2.3 4.3 %collective-permute-start.1 = (f32[20,128]{1,0:T(8,128)S(1)}, f32[20,128]{1,0:T(8,128)S(1)}, u32[]{:S(2)}, u32[]{:S(2)}) collective-permute-start(f32[20,128]{1,0:T(8,128)S(1)} %get-tuple-element.26), channel_id=1, source_target_pairs={{0,12},{4,8},{8,4},{12,0},{1,13},{5,9},{9,5},{13,1},{2,14},{6,10},... | collective-permute-start | bytes 30728 | tf_op jit(solution)/shard_map/ppermute | solution.py:324
  6.4 19.9 %collective-permute-start.10 = (f32[40,128]{1,0:T(8,128)S(1)}, f32[40,128]{1,0:T(8,128)S(1)}, u32[]{:S(2)}, u32[]{:S(2)}) collective-permute-start(f32[40,128]{1,0:T(8,128)S(1)} %get-tuple-element.37), channel_id=1, source_target_pairs={{0,12},{4,8},{8,4},{12,0},{1,13},{5,9},{9,5},{13,1},{2,14},{6,10},... | collective-permute-start | bytes 61448 | tf_op jit(solution)/shard_map/ppermute | solution.py:337
  6.5 19.8 %collective-permute-start.9 = (f32[40,128]{1,0:T(8,128)S(1)}, f32[40,128]{1,0:T(8,128)S(1)}, u32[]{:S(2)}, u32[]{:S(2)}) collective-permute-start(f32[40,128]{1,0:T(8,128)S(1)} %get-tuple-element.36), channel_id=1, source_target_pairs={{0,4},{4,0},{8,12},{12,8},{1,5},{5,1},{9,13},{13,9},{2,6},{6,2},{1... | collective-permute-start | bytes 61448 | tf_op jit(solution)/shard_map/ppermute | solution.py:336
  6.9 4.9 %collective-permute-start.2 = (f32[80,128]{1,0:T(8,128)S(1)}, f32[80,128]{1,0:T(8,128)S(1)}, u32[]{:S(2)}, u32[]{:S(2)}) collective-permute-start(f32[80,128]{1,0:T(8,128)S(1)} %get-tuple-element.30.own_ref), channel_id=1, source_target_pairs={{0,1},{1,0},{2,3},{3,2},{4,5},{5,4},{6,7},{7,6},{8,9},{9,8},{10,11... | collective-permute-start | bytes 122888 | tf_op jit(solution)/shard_map/ppermute | solution.py:350
  9.0 5.8 %collective-permute-start.3 = (f32[80,128]{1,0:T(8,128)S(1)}, f32[80,128]{1,0:T(8,128)S(1)}, u32[]{:S(2)}, u32[]{:S(2)}) collective-permute-start(f32[80,128]{1,0:T(8,128)S(1)} %get-tuple-element.30.own_ref), channel_id=1, source_target_pairs={{0,2},{1,3},{2,0},{3,1},{4,6},{5,7},{6,4},{7,5},{8,10},{9,11},{10,... | collective-permute-start | bytes 122888 | tf_op jit(solution)/shard_map/ppermute | solution.py:350
  11.6 5.8 %collective-permute-start.4 = (f32[80,128]{1,0:T(8,128)S(1)}, f32[80,128]{1,0:T(8,128)S(1)}, u32[]{:S(2)}, u32[]{:S(2)}) collective-permute-start(f32[80,128]{1,0:T(8,128)S(1)} %get-tuple-element.30.own_ref), channel_id=1, source_target_pairs={{0,3},{1,2},{2,1},{3,0},{4,7},{5,6},{6,5},{7,4},{8,11},{9,10},{10,... | collective-permute-start | bytes 122888 | tf_op jit(solution)/shard_map/ppermute | solution.py:350
  17.6 3.1 %collective-permute-start.5 = (f32[16,128]{1,0:T(8,128)S(1)}, f32[16,128]{1,0:T(8,128)S(1)}, u32[]{:S(2)}, u32[]{:S(2)}) collective-permute-start(f32[16,128]{1,0:T(8,128)S(1)} %get-tuple-element.34), channel_id=1, source_target_pairs={{0,20},{1,21},{2,22},{3,23},{4,16},{5,17},{6,18},{7,19},{8,28},{9,... | collective-permute-start | bytes 24584 | tf_op jit(solution)/shard_map/ppermute | solution.py:401
  17.6 4.0 %collective-permute-start.7 = (f32[16,128]{1,0:T(8,128)S(1)}, f32[16,128]{1,0:T(8,128)S(1)}, u32[]{:S(2)}, u32[]{:S(2)}) collective-permute-start(f32[16,128]{1,0:T(8,128)S(1)} %get-tuple-element.34), channel_id=1, source_target_pairs={{0,28},{1,29},{2,30},{3,31},{4,24},{5,25},{6,26},{7,27},{8,20},{9,... | collective-permute-start | bytes 24584 | tf_op jit(solution)/shard_map/ppermute | solution.py:401
  20.7 7.0 %collective-permute-start.6 = (f32[16,128]{1,0:T(8,128)S(1)}, f32[16,128]{1,0:T(8,128)S(1)}, u32[]{:S(2)}, u32[]{:S(2)}) collective-permute-start(f32[16,128]{1,0:T(8,128)S(1)} %collective-permute-done.5.refs_1_), channel_id=1, source_target_pairs={{0,4},{4,0},{8,12},{12,8},{1,5},{5,1},{9,13},{13,9},{2,6},{6,2},{1... | collective-permute-start | bytes 24584 | tf_op jit(solution)/shard_map/ppermute | solution.py:407
  21.7 6.0 %collective-permute-start.8 = (f32[16,128]{1,0:T(8,128)S(1)}, f32[16,128]{1,0:T(8,128)S(1)}, u32[]{:S(2)}, u32[]{:S(2)}) collective-permute-start(f32[16,128]{1,0:T(8,128)S(1)} %collective-permute-done.7.refs_3_), channel_id=1, source_target_pairs={{0,4},{4,0},{8,12},{12,8},{1,5},{5,1},{9,13},{13,9},{2,6},{6,2},{1... | collective-permute-start | bytes 24584 | tf_op jit(solution)/shard_map/ppermute | solution.py:407
  26.3 1.4 %copy-start.2 = (f32[512,4]{0,1:T(4,128)S(1)}, f32[512,4]{0,1:T(4,128)}, u32[]{:S(2)}) copy-start(f32[512,4]{0,1:T(4,128)} %param.13) | copy-start | bytes 24580
  26.3 1.4 %copy-start.3 = (s32[512]{0:T(512)S(1)}, s32[512]{0:T(512)}, u32[]{:S(2)}) copy-start(s32[512]{0:T(512)} %param.15) | copy-start | bytes 6148

commit v7 on v6

--- a/solution.py
+++ b/solution.py
@@ -234,7 +234,7 @@
 def final_kernel(
     levels, tiles, count, sections, first_ref, inner_ref, outer_ref, mixed_ref, top_ref, weight_ref, water_ref, *refs
 ):
-    got, (q_ref, heat_hbm, out_ref, whole, patch, heat_ref, sems) = refs[:count], refs[count:]
+    joined_ref, shared_ref, q_ref, heat_hbm, out_ref, whole, patch, heat_ref, sems = refs
     del q_ref
     here = lax.axis_index("tile")
     sea = jnp.logical_and(
@@ -243,7 +243,9 @@
     for s in range(count):
         base = (here ^ s) * tiles * SUB
         for tile in range(tiles):
-            whole[pl.ds(pl.multiple_of(base + tile * SUB, SUB), NFLUX), :] = got[s][pl.ds(tile * NFLUX, NFLUX), :]
+            row = (s // 2 * tiles + tile) * NFLUX
+            got = joined_ref if s % 2 else shared_ref
+            whole[pl.ds(pl.multiple_of(base + tile * SUB, SUB), NFLUX), :] = got[pl.ds(row, NFLUX), :]
     first = first_ref[0]
     top = top_ref[...]
     mixed = mixed_ref[...]
@@ -371,8 +373,7 @@
     )
     part, inner, outer = inside(first, q, coef, index)
 
-    operator, _ = lax.optimization_barrier((depth_physics_operator, heat))
-    mine = lax.dynamic_slice_in_dim(operator[0], lev * levels, levels, 0)
+    mine = lax.dynamic_slice_in_dim(depth_physics_operator[0], lev * levels, levels, 0)
     columns = [
         lax.dynamic_slice_in_dim(mine, source_of(lev, s, lev_count) * levels, levels, 1)
         for s in range(lev_count)
@@ -400,11 +401,9 @@
         ]
         return lax.ppermute(surface, ("comp", "tile", "lev"), pairs)
 
-    got = [None] * tile_count
-    for s in range(1, tile_count, 2):
-        got[s] = across(s)
-    for s in range(1, tile_count, 2):
-        got[s ^ 1] = lax.ppermute(got[s], "tile", swap_a)
+    direct = [across(s) for s in range(1, tile_count, 2)]
+    joined = jnp.concatenate(direct, axis=0)
+    shared = lax.ppermute(joined, "tile", swap_a)
 
     finish = pl.pallas_call(
         functools.partial(outer_kernel, levels, tiles, group),
@@ -421,7 +420,7 @@
     heat_out, q_out = pl.pallas_call(
         functools.partial(final_kernel, levels, tiles, tile_count, sections),
         out_shape=[shape((rows, LANES), f32), shape((levels, tracers, width), f32)],
-        in_specs=[SMEM] + [VMEM] * (6 + tile_count) + [HBM],
+        in_specs=[SMEM] + [VMEM] * 8 + [HBM],
         out_specs=[HBM, HBM],
         scratch_shapes=[
             pltpu.VMEM((tile_count * tiles * SUB, LANES), f32),
@@ -429,11 +428,11 @@
             pltpu.VMEM((rows, LANES), f32),
             pltpu.SemaphoreType.DMA((2,)),
         ],
-        input_output_aliases={7 + tile_count: 1},
+        input_output_aliases={9: 1},
         compiler_params=PARAMS,
         name="remap",
     )(
-        first, inner, outer, mixed, top, exchange_weight_table.T, water_indicator.reshape(1, width), *got, moved
+        first, inner, outer, mixed, top, exchange_weight_table.T, water_indicator.reshape(1, width), joined, shared, moved
     )
     thermal_anomaly_ending = heat_out.reshape(1, levels, width)
     species_ratios_ending = jnp.transpose(q_out.reshape(1, levels, tracers, width), (0, 2, 1, 3))

time: 28.8 us -> 31.3 us (1.087)
  waiting for transfers between devices: 6.89 us -> 10.5 us
  starting transfers between devices: 12.5 us -> 11.4 us
    ppermute x2, waiting for transfers between devices: 1.25 us -> 3.46 us  [across(): return lax.ppermute(surface, ('comp', 'tile', 'lev'), pairs)]
    ppermute x2, starting transfers between devices: 2.68 us -> 0.52 us  [across(): return lax.ppermute(surface, ('comp', 'tile', 'lev'), pairs)]
    ppermute x1, starting transfers between devices: 0.14 us -> 1.7 us  [interval(): got_side_a = lax.ppermute(side_a, 'tile', swap_a)]
    ppermute x1, waiting for transfers between devices: 0.01 us -> 1.31 us  [interval(): got_b = lax.ppermute(send_b, 'tile', swap_b)]
    ppermute x2 -> x1, starting transfers between devices: 1.68 us -> 0.43 us  [interval(): shared = lax.ppermute(joined, 'tile', swap_a)]
    ppermute x1, starting transfers between devices: 0.07 us -> 1.17 us  [interval(): got_side_b = lax.ppermute(side_b, 'tile', swap_b)]
  transfers between devices with their start and end apart: 11 -> 10, of which waited for: 4 -> 4; matrix products, arithmetic and copies ran while one was open for 2% -> 2% of each run, Pallas kernels for 18% -> 15%
where the time goes in v7:
time: 31.3 us; the launch traced here: 31.1 us
  starting transfers between devices  11.4 us (36%)
  waiting for transfers between devices  10.5 us (34%)
  Pallas kernels  7.05 us (23%)
  between operations  1.47 us (5%)
  local copies, waits for them, and re-layouts  0.63 us (2%)
    ppermute x3, waiting for transfers between devices, interval(): lax.ppermute(heat, 'lev', [(i, peer(i, s, lev_count)) for i in range(lev_...  5.68 us
    ppermute x3, starting transfers between devices, interval(): lax.ppermute(heat, 'lev', [(i, peer(i, s, lev_count)) for i in range(lev_...  4.45 us
    ppermute x2, waiting for transfers between devices, across(): return lax.ppermute(surface, ('comp', 'tile', 'lev'), pairs)  3.46 us
    ppermute x1, starting transfers between devices, interval(): got_b = lax.ppermute(send_b, 'tile', swap_b)  2.59 us
    pallas_call x1, Pallas kernels, interval(): part, inner, outer = inside(first, q, coef, index)  1.8 us
    ppermute x1, starting transfers between devices, interval(): got_side_a = lax.ppermute(side_a, 'tile', swap_a)  1.7 us
    pallas_call x1, Pallas kernels, interval(): side_a, side_b = pack(pltpu.with_memory_space_constraint(q, pltpu.HBM))  1.5 us
    pallas_call x1, Pallas kernels, interval(): moved = finish(part, coef, got_side_a, got_side_b, mixed)  1.38 us
  transfers between devices with their start and end apart: 10, of which 4 were waited for; matrix products, arithmetic and copies ran while one was open for 2% of the time, Pallas kernels for 15%

profile of v7, /device:TPU:0, one launch (start us, length us, event | category | flops | bytes accessed | tf_op | source)
XLA Modules:
  0.0 31.1 jit_solution(9513575622453495561)
XLA Ops:
  0.7 0.0 copy-start
  0.7 1.1 %edges.1 = (f32[20,128]{1,0:T(8,128)S(1)}, f32[20,128]{1,0:T(8,128)S(1)}, f32[80,128]{1,0:T(8,128)S(1)}, f32[80,128]{1,0:T(8,128)S(1)}, f32[80,128]{1,0:T(8,128)S(1)}, /*index=5*/f32[8,512]{1,0:T(8,128)S(1)}) custom-call(f32[80,128]{1,0:T(8,128)} %bitcast.30, f32[80,128]{1,0:T(8,128)} %bitcast.31, f32[80,128]{1,0:T(8,128)} %bitcast.32, f32[20,40,512]{2,1,0:T(8,128)} %bitcast.22), custom_call_target="tpu_custom_call" | custom-call | tf_op jit(solution)/shard_map/edges/pallas_call | solution.py:314
  1.7 0.6 %collective-permute-start = (f32[20,128]{1,0:T(8,128)S(1)}, f32[20,128]{1,0:T(8,128)S(1)}, u32[]{:S(2)}, u32[]{:S(2)}) collective-permute-start(f32[20,128]{1,0:T(8,128)S(1)} %get-tuple-element.24), channel_id=1, source_target_pairs={{0,4},{4,0},{8,12},{12,8},{1,5},{5,1},{9,13},{13,9},{2,6},{6,2},{1... | collective-permute-start | bytes 30728 | tf_op jit(solution)/shard_map/ppermute | solution.py:325
  2.3 2.6 %collective-permute-start.1 = (f32[20,128]{1,0:T(8,128)S(1)}, f32[20,128]{1,0:T(8,128)S(1)}, u32[]{:S(2)}, u32[]{:S(2)}) collective-permute-start(f32[20,128]{1,0:T(8,128)S(1)} %get-tuple-element.25), channel_id=1, source_target_pairs={{0,12},{4,8},{8,4},{12,0},{1,13},{5,9},{9,5},{13,1},{2,14},{6,10},... | collective-permute-start | bytes 30728 | tf_op jit(solution)/shard_map/ppermute | solution.py:326
  4.9 0.1 dynamic-slice_bitcast_fusion.3
  5.0 0.0 collective-permute-done.a_ref
  5.0 1.3 %collective-permute-done.1.b_ref = f32[20,128]{1,0:T(8,128)S(1)} collective-permute-done((f32[20,128]{1,0:T(8,128)S(1)}, f32[20,128]{1,0:T(8,128)S(1)}, u32[]{:S(2)}, u32[]{:S(2)}) %collective-permute-start.1) | collective-permute-done | bytes 10272 | tf_op jit(solution)/shard_map/ppermute | solution.py:326
  6.3 0.2 heat.1
  6.5 1.8 %collective-permute-start.2 = (f32[80,128]{1,0:T(8,128)S(1)}, f32[80,128]{1,0:T(8,128)S(1)}, u32[]{:S(2)}, u32[]{:S(2)}) collective-permute-start(f32[80,128]{1,0:T(8,128)S(1)} %get-tuple-element.29.own_ref), channel_id=1, source_target_pairs={{0,1},{1,0},{2,3},{3,2},{4,5},{5,4},{6,7},{7,6},{8,9},{9,8},{10,11... | collective-permute-start | bytes 122888 | tf_op jit(solution)/shard_map/ppermute | solution.py:352
  8.4 2.6 %collective-permute-start.3 = (f32[80,128]{1,0:T(8,128)S(1)}, f32[80,128]{1,0:T(8,128)S(1)}, u32[]{:S(2)}, u32[]{:S(2)}) collective-permute-start(f32[80,128]{1,0:T(8,128)S(1)} %get-tuple-element.29.own_ref), channel_id=1, source_target_pairs={{0,2},{1,3},{2,0},{3,1},{4,6},{5,7},{6,4},{7,5},{8,10},{9,11},{10,... | collective-permute-start | bytes 122888 | tf_op jit(solution)/shard_map/ppermute | solution.py:352
  11.0 0.0 collective-permute-start.4
  11.0 0.1 pad_maximum_fusion.m_ref
  11.1 0.0 collective-permute-done.2.refs_0_
  11.1 3.0 %collective-permute-done.3.refs_1_ = f32[80,128]{1,0:T(8,128)S(1)} collective-permute-done((f32[80,128]{1,0:T(8,128)S(1)}, f32[80,128]{1,0:T(8,128)S(1)}, u32[]{:S(2)}, u32[]{:S(2)}) %collective-permute-start.3) | collective-permute-done | bytes 40992 | tf_op jit(solution)/shard_map/ppermute | solution.py:352
  14.0 2.7 %collective-permute-done.4.refs_2_ = f32[80,128]{1,0:T(8,128)S(1)} collective-permute-done((f32[80,128]{1,0:T(8,128)S(1)}, f32[80,128]{1,0:T(8,128)S(1)}, u32[]{:S(2)}, u32[]{:S(2)}) %collective-permute-start.4) | collective-permute-done | bytes 40992 | tf_op jit(solution)/shard_map/ppermute | solution.py:352
  16.8 0.2 surface.1
  17.0 0.0 collective-permute-start.5
  17.0 1.5 %pack.1 = (f32[40,128]{1,0:T(8,128)S(1)}, f32[40,128]{1,0:T(8,128)S(1)}) custom-call(f32[20,40,512]{2,1,0:T(8,128)} %bitcast.23), custom_call_target="tpu_custom_call" | custom-call | tf_op jit(solution)/shard_map/pack/pallas_call | solution.py:337
  18.5 1.7 %collective-permute-start.8 = (f32[40,128]{1,0:T(8,128)S(1)}, f32[40,128]{1,0:T(8,128)S(1)}, u32[]{:S(2)}, u32[]{:S(2)}) collective-permute-start(f32[40,128]{1,0:T(8,128)S(1)} %get-tuple-element.34), channel_id=1, source_target_pairs={{0,4},{4,0},{8,12},{12,8},{1,5},{5,1},{9,13},{13,9},{2,6},{6,2},{1... | collective-permute-start | bytes 61448 | tf_op jit(solution)/shard_map/ppermute | solution.py:338
  20.2 1.2 %collective-permute-start.9 = (f32[40,128]{1,0:T(8,128)S(1)}, f32[40,128]{1,0:T(8,128)S(1)}, u32[]{:S(2)}, u32[]{:S(2)}) collective-permute-start(f32[40,128]{1,0:T(8,128)S(1)} %get-tuple-element.35), channel_id=1, source_target_pairs={{0,12},{4,8},{8,4},{12,0},{1,13},{5,9},{9,5},{13,1},{2,14},{6,10},... | collective-permute-start | bytes 61448 | tf_op jit(solution)/shard_map/ppermute | solution.py:339
  21.4 0.5 %collective-permute-start.6 = (f32[16,128]{1,0:T(8,128)S(1)}, f32[16,128]{1,0:T(8,128)S(1)}, u32[]{:S(2)}, u32[]{:S(2)}) collective-permute-start(f32[16,128]{1,0:T(8,128)S(1)} %get-tuple-element.32), channel_id=1, source_target_pairs={{0,28},{1,29},{2,30},{3,31},{4,24},{5,25},{6,26},{7,27},{8,20},{9,... | collective-permute-start | bytes 24584 | tf_op jit(solution)/shard_map/ppermute | solution.py:402
  21.9 0.0 collective-permute-done.5
  21.9 3.5 %collective-permute-done.6 = f32[16,128]{1,0:T(8,128)S(1)} collective-permute-done((f32[16,128]{1,0:T(8,128)S(1)}, f32[16,128]{1,0:T(8,128)S(1)}, u32[]{:S(2)}, u32[]{:S(2)}) %collective-permute-start.6) | collective-permute-done | bytes 8224 | tf_op jit(solution)/shard_map/ppermute | solution.py:402
  25.3 0.4 %collective-permute-start.7 = (f32[32,128]{1,0:T(8,128)S(1)}, f32[32,128]{1,0:T(8,128)S(1)}, u32[]{:S(2)}, u32[]{:S(2)}) collective-permute-start(f32[32,128]{1,0:T(8,128)S(1)} %constant_dynamic-update-slice_fusion.refs_0_), channel_id=1, source_target_pairs={{0,4},{4,0},{8,12},{12,8},{1,5},{5,1},{9,13},{13,9},{2,6},{6,2},{1... | collective-permute-start | bytes 49160 | tf_op jit(solution)/shard_map/ppermute | solution.py:406
  25.8 0.5 %slice.4 = s32[1,1]{1,0:T(1,128)} slice(s32[4,512]{1,0:T(4,128)S(1)} %bitcast.25), slice={[0:1], [0:1]} | slice | bytes 8 | tf_op jit(solution)/shard_map/slice | solution.py:357
  27.0 1.8 %inside.1 = (f32[20,40,512]{2,1,0:T(8,128)S(1)}, s32[4,512]{1,0:T(4,128)S(1)}, s32[4,512]{1,0:T(4,128)S(1)}) custom-call(s32[1]{0:T(128)S(6)} %mul.16.first_ref, f32[20,40,512]{2,1,0:T(8,128)S(1)} %bitcast.24, f32[5,20,512]{2,1,0:T(8,128)S(1)} %get-tuple-element.26.coef_ref, s32[4,512]{1,0:T(4,128)S(1)} %bitcast.26), custom_call_target="tpu_custom_call" | custom-call | flops 3686400 | bytes 1638400 | tf_op jit(solution)/shard_map/inside/pallas_call | solution.py:374
  28.8 0.0 collective-permute-done.9.b_ref
  28.8 0.0 copy-start.2
  28.8 0.0 copy-start.3
  28.8 1.4 %finish.1.refs_2_ = f32[20,40,512]{2,1,0:T(8,128)} custom-call(f32[20,40,512]{2,1,0:T(8,128)S(1)} %get-tuple-element.33.part_ref, f32[5,20,512]{2,1,0:T(8,128)S(1)} %get-tuple-element.26.coef_ref, f32[40,128]{1,0:T(8,128)S(1)} %collective-permute-done.8.a_ref, f32[40,128]{1,0:T(8,128)S(1)} %collective-permute-done.9.b_ref, ...), custom_call_target="tpu_custom_call" | custom-call | flops 3686400 | bytes 1638400 | tf_op jit(solution)/shard_map/finish/pallas_call | solution.py:418
  30.2 0.0 collective-permute-done.7.refs_1_
  30.3 0.8 %remap.1 = (f32[80,128]{1,0:T(8,128)}, f32[20,40,512]{2,1,0:T(8,128)}) custom-call(s32[1]{0:T(128)S(6)} %mul.16.first_ref, s32[4,512]{1,0:T(4,128)S(1)} %get-tuple-element.27.inner_ref, s32[4,512]{1,0:T(4,128)S(1)} %get-tuple-element.28.outer_ref, f32[20,512]{1,0:T(8,128)S(1)} %get-tuple-element.31.after_ref.mixed_ref, ...), custom_call_target="tpu_custom_call", output_to_operand_aliasing={{1}: (9, {})} | custom-call | tf_op jit(solution)/shard_map/remap/pallas_call | solution.py:420
  (10 shorter events, 0.0 us)
Async XLA Ops:
  0.6 4.3 %copy-start.4 = (f32[1,80,80]{2,1,0:T(8,128)S(1)}, f32[1,80,80]{2,1,0:T(8,128)}, u32[]{:S(2)}) copy-start(f32[1,80,80]{2,1,0:T(8,128)} %param.12) | copy-start | bytes 76804
  0.6 25.1 %copy-start.1 = (s32[512,4]{0,1:T(4,128)S(1)}, s32[512,4]{0,1:T(4,128)}, u32[]{:S(2)}) copy-start(s32[512,4]{0,1:T(4,128)} %param.14) | copy-start | bytes 24580
  0.7 26.3 %copy-start = (f32[1,40,20,512]{3,1,2,0:T(8,128)S(1)}, f32[1,40,20,512]{3,1,2,0:T(8,128)}, u32[]{:S(2)}) copy-start(f32[1,40,20,512]{3,1,2,0:T(8,128)} %param.10) | copy-start | bytes 4915204
  1.7 3.2 %collective-permute-start = (f32[20,128]{1,0:T(8,128)S(1)}, f32[20,128]{1,0:T(8,128)S(1)}, u32[]{:S(2)}, u32[]{:S(2)}) collective-permute-start(f32[20,128]{1,0:T(8,128)S(1)} %get-tuple-element.24), channel_id=1, source_target_pairs={{0,4},{4,0},{8,12},{12,8},{1,5},{5,1},{9,13},{13,9},{2,6},{6,2},{1... | collective-permute-start | bytes 30728 | tf_op jit(solution)/shard_map/ppermute | solution.py:325
  2.3 4.0 %collective-permute-start.1 = (f32[20,128]{1,0:T(8,128)S(1)}, f32[20,128]{1,0:T(8,128)S(1)}, u32[]{:S(2)}, u32[]{:S(2)}) collective-permute-start(f32[20,128]{1,0:T(8,128)S(1)} %get-tuple-element.25), channel_id=1, source_target_pairs={{0,12},{4,8},{8,4},{12,0},{1,13},{5,9},{9,5},{13,1},{2,14},{6,10},... | collective-permute-start | bytes 30728 | tf_op jit(solution)/shard_map/ppermute | solution.py:326
  6.5 4.5 %collective-permute-start.2 = (f32[80,128]{1,0:T(8,128)S(1)}, f32[80,128]{1,0:T(8,128)S(1)}, u32[]{:S(2)}, u32[]{:S(2)}) collective-permute-start(f32[80,128]{1,0:T(8,128)S(1)} %get-tuple-element.29.own_ref), channel_id=1, source_target_pairs={{0,1},{1,0},{2,3},{3,2},{4,5},{5,4},{6,7},{7,6},{8,9},{9,8},{10,11... | collective-permute-start | bytes 122888 | tf_op jit(solution)/shard_map/ppermute | solution.py:352
  8.4 5.7 %collective-permute-start.3 = (f32[80,128]{1,0:T(8,128)S(1)}, f32[80,128]{1,0:T(8,128)S(1)}, u32[]{:S(2)}, u32[]{:S(2)}) collective-permute-start(f32[80,128]{1,0:T(8,128)S(1)} %get-tuple-element.29.own_ref), channel_id=1, source_target_pairs={{0,2},{1,3},{2,0},{3,1},{4,6},{5,7},{6,4},{7,5},{8,10},{9,11},{10,... | collective-permute-start | bytes 122888 | tf_op jit(solution)/shard_map/ppermute | solution.py:352
  11.0 5.8 %collective-permute-start.4 = (f32[80,128]{1,0:T(8,128)S(1)}, f32[80,128]{1,0:T(8,128)S(1)}, u32[]{:S(2)}, u32[]{:S(2)}) collective-permute-start(f32[80,128]{1,0:T(8,128)S(1)} %get-tuple-element.29.own_ref), channel_id=1, source_target_pairs={{0,3},{1,2},{2,1},{3,0},{4,7},{5,6},{6,5},{7,4},{8,11},{9,10},{10,... | collective-permute-start | bytes 122888 | tf_op jit(solution)/shard_map/ppermute | solution.py:352
  17.0 4.9 %collective-permute-start.5 = (f32[16,128]{1,0:T(8,128)S(1)}, f32[16,128]{1,0:T(8,128)S(1)}, u32[]{:S(2)}, u32[]{:S(2)}) collective-permute-start(f32[16,128]{1,0:T(8,128)S(1)} %get-tuple-element.32), channel_id=1, source_target_pairs={{0,20},{1,21},{2,22},{3,23},{4,16},{5,17},{6,18},{7,19},{8,28},{9,... | collective-permute-start | bytes 24584 | tf_op jit(solution)/shard_map/ppermute | solution.py:402
  18.5 10.3 %collective-permute-start.8 = (f32[40,128]{1,0:T(8,128)S(1)}, f32[40,128]{1,0:T(8,128)S(1)}, u32[]{:S(2)}, u32[]{:S(2)}) collective-permute-start(f32[40,128]{1,0:T(8,128)S(1)} %get-tuple-element.34), channel_id=1, source_target_pairs={{0,4},{4,0},{8,12},{12,8},{1,5},{5,1},{9,13},{13,9},{2,6},{6,2},{1... | collective-permute-start | bytes 61448 | tf_op jit(solution)/shard_map/ppermute | solution.py:338
  20.2 8.6 %collective-permute-start.9 = (f32[40,128]{1,0:T(8,128)S(1)}, f32[40,128]{1,0:T(8,128)S(1)}, u32[]{:S(2)}, u32[]{:S(2)}) collective-permute-start(f32[40,128]{1,0:T(8,128)S(1)} %get-tuple-element.35), channel_id=1, source_target_pairs={{0,12},{4,8},{8,4},{12,0},{1,13},{5,9},{9,5},{13,1},{2,14},{6,10},... | collective-permute-start | bytes 61448 | tf_op jit(solution)/shard_map/ppermute | solution.py:339
  21.4 4.0 %collective-permute-start.6 = (f32[16,128]{1,0:T(8,128)S(1)}, f32[16,128]{1,0:T(8,128)S(1)}, u32[]{:S(2)}, u32[]{:S(2)}) collective-permute-start(f32[16,128]{1,0:T(8,128)S(1)} %get-tuple-element.32), channel_id=1, source_target_pairs={{0,28},{1,29},{2,30},{3,31},{4,24},{5,25},{6,26},{7,27},{8,20},{9,... | collective-permute-start | bytes 24584 | tf_op jit(solution)/shard_map/ppermute | solution.py:402
  25.3 4.9 %collective-permute-start.7 = (f32[32,128]{1,0:T(8,128)S(1)}, f32[32,128]{1,0:T(8,128)S(1)}, u32[]{:S(2)}, u32[]{:S(2)}) collective-permute-start(f32[32,128]{1,0:T(8,128)S(1)} %constant_dynamic-update-slice_fusion.refs_0_), channel_id=1, source_target_pairs={{0,4},{4,0},{8,12},{12,8},{1,5},{5,1},{9,13},{13,9},{2,6},{6,2},{1... | collective-permute-start | bytes 49160 | tf_op jit(solution)/shard_map/ppermute | solution.py:406
  28.8 1.4 %copy-start.2 = (f32[512,4]{0,1:T(4,128)S(1)}, f32[512,4]{0,1:T(4,128)}, u32[]{:S(2)}) copy-start(f32[512,4]{0,1:T(4,128)} %param.13) | copy-start | bytes 24580
  28.8 1.4 %copy-start.3 = (s32[512]{0:T(512)S(1)}, s32[512]{0:T(512)}, u32[]{:S(2)}) copy-start(s32[512]{0:T(512)} %param.15) | copy-start | bytes 6148
